TPU v7x, 128 devices: a whole 4x4x4 slice. The times are simulated.
128 devices in a mesh: grp: 4 (over y), row: 32 (over x, z, core).
Axes of the slice: x: 4, y: 4, z: 4, core: 2. Of those that a mesh axis runs over, the one named last changes fastest.
Arguments:
- b_tensor: bfloat16 [9984, 8, 768], P(None, 'grp', 'row'), may hold values from -0.21875 to 0.21875
- aux_counts: int32 [4], replicated, may hold values from 1 to 2, as said below
Outputs:
- exchange_matrix: float32 [9984, 9984], P('row', 'grp')
Inputs may be any that keep to these rules, and one draw needn't show every extreme that they name: `aux_counts`: some group has all 2 slots live.
All inputs are finite; a program needn't handle non-finite values.
Results may differ from a plain program's by a relative error of at most 0.0003.
Values may be sent and summed in bfloat16 or wider, within the bound.
No kernel may reach another device: no remote copies, remote signals or barrier semaphores. Data moves between devices by JAX's collectives and lax.ppermute only.
A program may use at most 128 MiB of HBM per device.

v0:
```python
import jax
import jax.numpy as jnp
from jax import lax
from jax.experimental import pallas as pl
from jax.experimental.pallas import tpu as pltpu
from jax.sharding import Mesh, PartitionSpec as P


SIDE = 4
CORES = 2
PLANE = SIDE * SIDE
WIDE = 1280
VMEM = pl.BlockSpec(memory_space=pltpu.VMEM)
SMEM = pl.BlockSpec(memory_space=pltpu.SMEM)


def along_y(block, step):
    return lax.ppermute(block, "y", [(i, (i + step) % SIDE) for i in range(SIDE)])


def swap_cores(block):
    return lax.ppermute(block, "core", [(0, 1), (1, 0)])


def along_plane(block, order, step):
    route = []
    for x in range(SIDE):
        for z in range(SIDE):
            for core in range(CORES):
                to = ((x + step) % SIDE, z) if core == order else (x, (z + step) % SIDE)
                route.append(((x * SIDE + z) * CORES + core, (to[0] * SIDE + to[1]) * CORES + core))
    return lax.ppermute(block, ("x", "z", "core"), route)


def join(blocks):
    def kernel(*refs):
        at = 0
        for ref in refs[:-1]:
            refs[-1][at : at + ref.shape[0]] = ref[...]
            at += ref.shape[0]

    total = sum(block.shape[0] for block in blocks)
    joined = jax.ShapeDtypeStruct((total, *blocks[0].shape[1:]), blocks[0].dtype)
    size = joined.size * joined.dtype.itemsize
    return pl.pallas_call(
        kernel,
        out_shape=joined,
        in_specs=[VMEM] * len(blocks),
        out_specs=VMEM,
        compiler_params=pltpu.CompilerParams(vmem_limit_bytes=2 * size + (1 << 18)),
        cost_estimate=pl.CostEstimate(flops=0, bytes_accessed=2 * size, transcendentals=0),
        name="join",
    )(*blocks)


def pack_kernel(count_ref, terms_ref, *refs):
    mine_refs, theirs_ref, rows_refs, (windows, rows) = refs[:SIDE], refs[SIDE], refs[SIDE + 1 : -2], refs[-2:]
    slots, orbitals, basis = terms_ref.shape
    columns = basis // SIDE
    chip_rows = rows.shape[2]
    x, y, z, core = (lax.axis_index(name) for name in ("x", "y", "z", "core"))
    for s in range(slots):
        live = s < count_ref[y]
        at = pl.ds(s * orbitals, orbitals)
        for p in range(SIDE):
            for q in range(CORES):
                start = p * columns + q * WIDE
                width = min(WIDE, basis - start)
                block = terms_ref[s, :, start : start + width]
                windows[p * CORES + q, at, :width] = jnp.where(live, block, jnp.zeros_like(block))
                if width < WIDE:
                    windows[p * CORES + q, at, width:] = jnp.zeros((orbitals, WIDE - width), block.dtype)
        for i in range(PLANE):
            block = terms_ref[s, :, i * chip_rows : (i + 1) * chip_rows]
            rows[i, at, :] = jnp.where(live, block, jnp.zeros_like(block))
    for dy in range(SIDE):
        plane = lax.rem(y + dy, SIDE) * CORES
        mine_refs[dy][...] = windows[plane + core]
        theirs_ref[dy] = windows[plane + 1 - core]
    for u, rows_ref in zip(OFFSETS, rows_refs):
        for i, v in enumerate(OFFSETS):
            dx, dz = jnp.where(core == 0, u, v), jnp.where(core == 0, v, u)
            rows_ref[i] = rows[lax.rem(x + dx + SIDE, SIDE) * SIDE + lax.rem(z + dz + SIDE, SIDE)]


def pack(counts, terms):
    slots, orbitals, basis = terms.shape
    depth = slots * orbitals
    window = jax.ShapeDtypeStruct((depth, WIDE), terms.dtype)
    other_windows = jax.ShapeDtypeStruct((SIDE, depth, WIDE), terms.dtype)
    line_rows = jax.ShapeDtypeStruct((SIDE, depth, basis // PLANE), terms.dtype)
    *mine, theirs, rows_0, rows_1, rows_2, rows_3 = pl.pallas_call(
        pack_kernel,
        out_shape=(window,) * SIDE + (other_windows,) + (line_rows,) * SIDE,
        in_specs=[SMEM, VMEM],
        out_specs=(VMEM,) * (2 * SIDE + 1),
        scratch_shapes=[
            pltpu.VMEM((CORES * SIDE, depth, WIDE), terms.dtype),
            pltpu.VMEM((PLANE, depth, basis // PLANE), terms.dtype),
        ],
        compiler_params=pltpu.CompilerParams(vmem_limit_bytes=12 << 20),
        name="pack",
    )(counts, terms)
    return mine, theirs, (rows_0, rows_1, rows_2, rows_3)


def regroup_kernel(*refs):
    for i, in_ref in enumerate(refs[:SIDE]):
        for j, out_ref in enumerate(refs[SIDE:]):
            out_ref[i] = in_ref[j]


def regroup(blocks):
    return pl.pallas_call(
        regroup_kernel,
        out_shape=tuple(jax.ShapeDtypeStruct(block.shape, block.dtype) for block in blocks),
        in_specs=[VMEM] * SIDE,
        out_specs=(VMEM,) * SIDE,
        compiler_params=pltpu.CompilerParams(vmem_limit_bytes=6 << 20),
        name="regroup",
    )(*blocks)


def along_line(blocks, order):
    got = {0: blocks[0]}
    for offset, block in zip(OFFSETS[1:], blocks[1:]):
        got[-offset if offset < 2 else 2] = along_plane(block, order, offset)
    return [got[offset] for offset in OFFSETS]


def pair_kernel(*refs):
    mine_refs, got_ref, out_refs = refs[:SIDE], refs[SIDE], refs[SIDE + 1 :]
    depth = got_ref.shape[1]
    for dy in range(SIDE):
        out_refs[dy][:depth, :] = mine_refs[dy][...]
        out_refs[dy][depth:, :] = got_ref[dy]


def pair(mine, got):
    window = jax.ShapeDtypeStruct((CORES * got.shape[1], WIDE), got.dtype)
    return pl.pallas_call(
        pair_kernel,
        out_shape=(window,) * SIDE,
        in_specs=[VMEM] * (SIDE + 1),
        out_specs=(VMEM,) * SIDE,
        compiler_params=pltpu.CompilerParams(vmem_limit_bytes=6 << 20),
        name="pair",
    )(*mine, got)


OFFSETS = (0, -1, 1, 2)
OWN = tuple((dcore, 0) for dcore in range(CORES))
OTHERS = tuple((dcore, dy) for dy in range(1, SIDE) for dcore in range(CORES))


def at(v, *us):
    return tuple((u, v) for u in us)


def gathered_briefly(own):
    before, after, far = (along_plane(own, 0, step) for step in (1, -1, 2))
    line = join([own, before, after, far])
    left, right = along_plane(line, 1, 1), along_plane(line, 1, -1)
    cut = line.shape[0] // 2
    opposite = along_plane(left[:cut], 1, 1), along_plane(right[cut:], 1, -1)
    first = sum((at(v, 0, -1, 1, 2) for v in (0, -1, 1)), ())
    last = join(opposite)
    return (first, join([line, left, right])), (at(2, 0, -1, 1, 2), last)


def gathered(own):
    cut = own.shape[0] // 2
    before, after = along_plane(own, 0, 1), along_plane(own, 0, -1)
    near = join([before, after])
    far = along_plane(before, 0, 1)
    near_sides = along_plane(near, 1, 1), along_plane(near, 1, -1)
    own_sides = along_plane(own, 1, 1), along_plane(own, 1, -1)
    far_sides = along_plane(far, 1, 1), along_plane(far, 1, -1)
    own_opposite = along_plane(own_sides[0], 1, 1)
    near_opposite = along_plane(near_sides[0][:cut], 1, 1), along_plane(near_sides[1][cut:], 1, -1)
    far_opposite = along_plane(far_sides[1], 1, -1)

    first = at(0, 0, -1, 1, 2) + at(-1, 0) + at(1, 0) + at(2, 0)
    parts = [(first, 0, join([own, near, far, *own_sides, own_opposite]))]
    parts += [(at(v, -1, 1), 0, block) for v, block in zip((-1, 1), near_sides)]
    parts += [(at(v, 2), 0, block) for v, block in zip((-1, 1), far_sides)]
    parts += [(at(2, -1, 1), 0, near_opposite[0]), (at(2, -1, 1), len(OTHERS) // 2, near_opposite[1])]
    parts += [(at(2, 2), 0, far_opposite)]
    return parts


def arrange_kernel(layout, *refs):
    in_refs, out_refs = refs[: -len(layout)], refs[-len(layout) :]
    depth = in_refs[0].shape[1]
    for blocks, out_ref in zip(layout, out_refs):
        for i, (u, v, dcore, place) in enumerate(blocks):
            first, second = (u, v) if dcore == 0 else (v, u)
            chip = OFFSETS.index(second) * SIDE + OFFSETS.index(first)
            out_ref[i * depth : (i + 1) * depth, :] = in_refs[dcore][place * PLANE + chip]


def arrange(layout, *rows):
    depth, chip_rows = rows[0].shape[1:]
    size = sum(map(len, layout)) * depth * chip_rows * rows[0].dtype.itemsize
    return pl.pallas_call(
        lambda *refs: arrange_kernel(layout, *refs),
        out_shape=tuple(jax.ShapeDtypeStruct((len(blocks) * depth, chip_rows), rows[0].dtype) for blocks in layout),
        in_specs=[VMEM] * CORES,
        out_specs=(VMEM,) * len(layout),
        compiler_params=pltpu.CompilerParams(vmem_limit_bytes=2 * size + (1 << 20)),
        cost_estimate=pl.CostEstimate(flops=0, bytes_accessed=2 * size, transcendentals=0),
        name="arrange",
    )(*rows)


def halve_kernel(tile_ref, kept_ref, sent_ref):
    rows = kept_ref.shape[0]
    for core in range(CORES):

        @pl.when(lax.axis_index("core") == core)
        def _():
            kept_ref[...] = tile_ref[core * rows : (core + 1) * rows, :]
            sent_ref[...] = tile_ref[(1 - core) * rows : (2 - core) * rows, :]


def halve(tile):
    half = jax.ShapeDtypeStruct((tile.shape[0] // CORES, tile.shape[1]), tile.dtype)
    return pl.pallas_call(
        halve_kernel,
        out_shape=(half, half),
        in_specs=[VMEM],
        out_specs=(VMEM, VMEM),
        compiler_params=pltpu.CompilerParams(vmem_limit_bytes=8 << 20),
        name="halve",
    )(tile)


def assemble_kernel(kept_ref, got_ref, out_ref):
    rest = out_ref.shape[1] - WIDE
    for core in range(CORES):

        @pl.when(lax.axis_index("core") == core)
        def _():
            first, last = (kept_ref, got_ref) if core == 0 else (got_ref, kept_ref)
            out_ref[:, :WIDE] = first[...]
            out_ref[:, WIDE:] = last[:, :rest]


def assemble(kept, got, columns):
    return pl.pallas_call(
        assemble_kernel,
        out_shape=jax.ShapeDtypeStruct((got.shape[0], columns), got.dtype),
        in_specs=[VMEM, VMEM],
        out_specs=VMEM,
        compiler_params=pltpu.CompilerParams(vmem_limit_bytes=8 << 20),
        name="assemble",
    )(kept, got)


def body(b_tensor, aux_counts):
    basis = b_tensor.shape[0]
    mine, theirs, rows = pack(aux_counts, b_tensor.transpose(1, 2, 0))

    got = swap_cores(theirs)
    windows = pair(mine, got)
    others = join([along_y(windows[-dy % SIDE], -dy % SIDE) for dy in range(1, SIDE)])
    rows = along_line(rows, 0)
    rows = regroup(rows)
    rows = along_line(rows, 1)
    rows = join(rows)
    early = gathered_briefly(windows[0])
    parts = gathered(others)

    left, right = along_y(rows, 1), along_y(rows, -1)
    half = PLANE // 2
    far = along_y(left[:half], 1), along_y(right[half:], -1)
    rest = join([right, *far, left])
    other_rows = swap_cores(rows)
    other_rest = swap_cores(rest)

    def product(weight, block):
        return lax.dot_general(weight, block, (((0,), (0,)), ((), ())), preferred_element_type=jnp.float32)

    layout = [[(u, v, dcore, dy) for u, v in offsets for dcore, dy in OWN] for offsets, _ in early]
    weights = arrange(layout, rows, other_rows)
    tile = product(weights[0], early[0][1])
    layout = []
    for offsets, skipped, block in parts:
        blocks = [(u, v, dcore, dy - 1) for u, v in offsets for dcore, dy in OTHERS]
        layout.append(blocks[skipped : skipped + block.shape[0] // rows.shape[1]])
    weights = (*arrange(layout, rest, other_rest), weights[1])
    blocks = [block for *_, block in parts] + [early[1][1]]
    for i in (0, 1, 2, len(parts), *range(3, len(parts))):
        tile = lax.optimization_barrier(tile + product(weights[i], blocks[i]))

    kept, sent = halve(tile)
    return assemble(kept, swap_cores(sent), basis // SIDE)


def solution(mesh):
    fine = Mesh(mesh.devices.reshape(SIDE, SIDE, SIDE, CORES), ("y", "x", "z", "core"))
    return jax.shard_map(
        body,
        mesh=fine,
        in_specs=(P(None, "y", ("x", "z", "core")), P()),
        out_specs=P(("x", "z", "core"), "y"),
        check_vma=False,
    )
```

profile of v0, /device:TPU:15, one launch (start us, length us, event | category | flops | bytes accessed | tf_op | source)
XLA Modules:
  0.0 190.1 jit_solution(13107446798931811060)
XLA Ops:
  3.0 1.7 collective-permute-start
  4.8 2.2 %collective-permute-start.1 = (bf16[4,48,624]{2,1,0:T(8,128)(2,1)S(1)}, bf16[4,48,624]{2,1,0:T(8,128)(2,1)S(1)}, u32[]{:S(2)}, u32[]{:S(2)}) collective-permute-start(bf16[4,48,624]{2,1,0:T(8,128)(2,1)S(1)} %get-tuple-element.36), channel_id=1, source_target_pairs={{0,24},{1,7},{2,26},{3,1},{4,28},{5,3},{6,30},{7,5},{8,0},{9,15},{... | collective-permute-start | bytes 718856 | tf_op jit(solution)/shard_map/ppermute | solution.py:32
  8.2 2.6 %collective-permute-done.refs_1_ = bf16[4,48,624]{2,1,0:T(8,128)(2,1)S(1)} collective-permute-done((bf16[4,48,624]{2,1,0:T(8,128)(2,1)S(1)}, bf16[4,48,624]{2,1,0:T(8,128)(2,1)S(1)}, u32[]{:S(2)}, u32[]{:S(2)}) %collective-permute-start) | collective-permute-done | bytes 239648 | tf_op jit(solution)/shard_map/ppermute | solution.py:32
  10.8 2.0 %collective-permute-done.1.refs_2_ = bf16[4,48,624]{2,1,0:T(8,128)(2,1)S(1)} collective-permute-done((bf16[4,48,624]{2,1,0:T(8,128)(2,1)S(1)}, bf16[4,48,624]{2,1,0:T(8,128)(2,1)S(1)}, u32[]{:S(2)}, u32[]{:S(2)}) %collective-permute-start.1) | collective-permute-done | bytes 239648 | tf_op jit(solution)/shard_map/ppermute | solution.py:32
  17.0 2.8 %collective-permute-done.3.refs_1_ = bf16[4,48,624]{2,1,0:T(8,128)(2,1)S(1)} collective-permute-done((bf16[4,48,624]{2,1,0:T(8,128)(2,1)S(1)}, bf16[4,48,624]{2,1,0:T(8,128)(2,1)S(1)}, u32[]{:S(2)}, u32[]{:S(2)}) %collective-permute-start.3) | collective-permute-done | bytes 239648 | tf_op jit(solution)/shard_map/ppermute | solution.py:32
  19.8 4.2 %collective-permute-done.4.refs_2_ = bf16[4,48,624]{2,1,0:T(8,128)(2,1)S(1)} collective-permute-done((bf16[4,48,624]{2,1,0:T(8,128)(2,1)S(1)}, bf16[4,48,624]{2,1,0:T(8,128)(2,1)S(1)}, u32[]{:S(2)}, u32[]{:S(2)}) %collective-permute-start.4) | collective-permute-done | bytes 239648 | tf_op jit(solution)/shard_map/ppermute | solution.py:32
  25.6 3.4 %collective-permute-start.7 = (bf16[4,48,1280]{2,1,0:T(8,128)(2,1)S(1)}, bf16[4,48,1280]{2,1,0:T(8,128)(2,1)S(1)}, u32[]{:S(2)}, u32[]{:S(2)}) collective-permute-start(bf16[4,48,1280]{2,1,0:T(8,128)(2,1)S(1)} %get-tuple-element.47), channel_id=1, source_target_pairs={{0,1},{1,0},{2,3},{3,2},{4,5},{5,4},{6,7},{7,6},{8,9},{9,8},{10,11... | collective-permute-start | bytes 1474568 | tf_op jit(solution)/shard_map/ppermute | solution.py:22
  33.0 11.6 %collective-permute-done.14.refs_3_ = bf16[16,48,624]{2,1,0:T(8,128)(2,1)S(1)} collective-permute-done((bf16[16,48,624]{2,1,0:T(8,128)(2,1)S(1)}, bf16[16,48,624]{2,1,0:T(8,128)(2,1)S(1)}, u32[]{:S(2)}, u32[]{:S(2)}) %collective-permute-start.14) | collective-permute-done | bytes 958496 | tf_op jit(solution)/shard_map/ppermute | solution.py:18
  47.7 3.2 %collective-permute-done.18.refs_0_ = bf16[96,1280]{1,0:T(8,128)(2,1)S(1)} collective-permute-done((bf16[96,1280]{1,0:T(8,128)(2,1)S(1)}, bf16[96,1280]{1,0:T(8,128)(2,1)S(1)}, u32[]{:S(2)}, u32[]{:S(2)}) %collective-permute-start.18) | collective-permute-done | bytes 245792 | tf_op jit(solution)/shard_map/ppermute | solution.py:18
  50.9 12.0 %collective-permute-start.6 = (bf16[16,48,624]{2,1,0:T(8,128)(2,1)S(1)}, bf16[16,48,624]{2,1,0:T(8,128)(2,1)S(1)}, u32[]{:S(2)}, u32[]{:S(2)}) collective-permute-start(bf16[16,48,624]{2,1,0:T(8,128)(2,1)S(1)} %join.8.refs_0_), channel_id=1, source_target_pairs={{0,1},{1,0},{2,3},{3,2},{4,5},{5,4},{6,7},{7,6},{8,9},{9,8},{10,11... | collective-permute-start | bytes 2875400 | tf_op jit(solution)/shard_map/ppermute | solution.py:22
  64.1 1.6 collective-permute-done.20.refs_2_
  66.1 3.1 %collective-permute-done.8.refs_1_ = bf16[96,1280]{1,0:T(8,128)(2,1)S(1)} collective-permute-done((bf16[96,1280]{1,0:T(8,128)(2,1)S(1)}, bf16[96,1280]{1,0:T(8,128)(2,1)S(1)}, u32[]{:S(2)}, u32[]{:S(2)}) %collective-permute-start.8) | collective-permute-done | bytes 245792 | tf_op jit(solution)/shard_map/ppermute | solution.py:32
  70.0 2.4 %collective-permute-start.10 = (bf16[96,1280]{1,0:T(8,128)(2,1)S(1)}, bf16[96,1280]{1,0:T(8,128)(2,1)S(1)}, u32[]{:S(2)}, u32[]{:S(2)}) collective-permute-start(bf16[96,1280]{1,0:T(8,128)(2,1)S(1)} %get-tuple-element.48.refs_0_), channel_id=1, source_target_pairs={{0,16},{1,5},{2,18},{3,7},{4,20},{5,1},{6,22},{7,3},{8,24},{9,13},... | collective-permute-start | bytes 737288 | tf_op jit(solution)/shard_map/ppermute | solution.py:32
  72.7 1.8 collective-permute-done.9.refs_2_
  74.5 3.5 %collective-permute-start.17 = (bf16[48,48,624]{2,1,0:T(8,128)(2,1)S(1)}, bf16[48,48,624]{2,1,0:T(8,128)(2,1)S(1)}, u32[]{:S(2)}, u32[]{:S(2)}) collective-permute-start(bf16[48,48,624]{2,1,0:T(8,128)(2,1)S(1)} %join.11.refs_0_), channel_id=1, source_target_pairs={{0,1},{1,0},{2,3},{3,2},{4,5},{5,4},{6,7},{7,6},{8,9},{9,8},{10,11... | collective-permute-start | bytes 8626184 | tf_op jit(solution)/shard_map/ppermute | solution.py:22
  78.0 2.3 %collective-permute-done.10.refs_3_ = bf16[96,1280]{1,0:T(8,128)(2,1)S(1)} collective-permute-done((bf16[96,1280]{1,0:T(8,128)(2,1)S(1)}, bf16[96,1280]{1,0:T(8,128)(2,1)S(1)}, u32[]{:S(2)}, u32[]{:S(2)}) %collective-permute-start.10) | collective-permute-done | bytes 245792 | tf_op jit(solution)/shard_map/ppermute | solution.py:32
  83.4 7.6 %collective-permute-done.24.refs_3_ = bf16[288,1280]{1,0:T(8,128)(2,1)S(1)} collective-permute-done((bf16[288,1280]{1,0:T(8,128)(2,1)S(1)}, bf16[288,1280]{1,0:T(8,128)(2,1)S(1)}, u32[]{:S(2)}, u32[]{:S(2)}) %collective-permute-start.24) | collective-permute-done | bytes 737312 | tf_op jit(solution)/shard_map/ppermute | solution.py:32
  91.1 4.6 %collective-permute-start.23 = (bf16[288,1280]{1,0:T(8,128)(2,1)S(1)}, bf16[288,1280]{1,0:T(8,128)(2,1)S(1)}, u32[]{:S(2)}, u32[]{:S(2)}) collective-permute-start(bf16[288,1280]{1,0:T(8,128)(2,1)S(1)} %collective-permute-done.21.refs_0_), channel_id=1, source_target_pairs={{0,8},{1,3},{2,10},{3,5},{4,12},{5,7},{6,14},{7,1},{8,16},{9,11},{... | collective-permute-start | bytes 2211848 | tf_op jit(solution)/shard_map/ppermute | solution.py:32
  95.7 11.6 %collective-permute-done.25.refs_4_ = bf16[288,1280]{1,0:T(8,128)(2,1)S(1)} collective-permute-done((bf16[288,1280]{1,0:T(8,128)(2,1)S(1)}, bf16[288,1280]{1,0:T(8,128)(2,1)S(1)}, u32[]{:S(2)}, u32[]{:S(2)}) %collective-permute-start.25) | collective-permute-done | bytes 737312 | tf_op jit(solution)/shard_map/ppermute | solution.py:32
  109.1 5.7 %collective-permute-done.23.refs_2_ = bf16[288,1280]{1,0:T(8,128)(2,1)S(1)} collective-permute-done((bf16[288,1280]{1,0:T(8,128)(2,1)S(1)}, bf16[288,1280]{1,0:T(8,128)(2,1)S(1)}, u32[]{:S(2)}, u32[]{:S(2)}) %collective-permute-start.23) | collective-permute-done | bytes 737312 | tf_op jit(solution)/shard_map/ppermute | solution.py:32
  114.8 2.2 %collective-permute-start.29 = (bf16[192,1280]{1,0:T(8,128)(2,1)S(1)}, bf16[192,1280]{1,0:T(8,128)(2,1)S(1)}, u32[]{:S(2)}, u32[]{:S(2)}) collective-permute-start(bf16[192,1280]{1,0:T(8,128)(2,1)S(1)} %slice.26), channel_id=1, source_target_pairs={{0,2},{1,9},{2,4},{3,11},{4,6},{5,13},{6,0},{7,15},{8,10},{9,17},{... | collective-permute-start | bytes 1474568 | tf_op jit(solution)/shard_map/ppermute | solution.py:32
  117.4 4.3 %collective-permute-done.26.refs_5_ = bf16[288,1280]{1,0:T(8,128)(2,1)S(1)} collective-permute-done((bf16[288,1280]{1,0:T(8,128)(2,1)S(1)}, bf16[288,1280]{1,0:T(8,128)(2,1)S(1)}, u32[]{:S(2)}, u32[]{:S(2)}) %collective-permute-start.26) | collective-permute-done | bytes 737312 | tf_op jit(solution)/shard_map/ppermute | solution.py:32
  121.8 2.4 %collective-permute-start.30 = (bf16[192,1280]{1,0:T(8,128)(2,1)S(1)}, bf16[192,1280]{1,0:T(8,128)(2,1)S(1)}, u32[]{:S(2)}, u32[]{:S(2)}) collective-permute-start(bf16[192,1280]{1,0:T(8,128)(2,1)S(1)} %slice.27), channel_id=1, source_target_pairs={{0,6},{1,25},{2,0},{3,27},{4,2},{5,29},{6,4},{7,31},{8,14},{9,1},{... | collective-permute-start | bytes 1474568 | tf_op jit(solution)/shard_map/ppermute | solution.py:32
  124.2 22.7 %collective-permute-done.29.refs_0_ = bf16[192,1280]{1,0:T(8,128)(2,1)S(1)} collective-permute-done((bf16[192,1280]{1,0:T(8,128)(2,1)S(1)}, bf16[192,1280]{1,0:T(8,128)(2,1)S(1)}, u32[]{:S(2)}, u32[]{:S(2)}) %collective-permute-start.29) | collective-permute-done | bytes 491552 | tf_op jit(solution)/shard_map/ppermute | solution.py:32
  146.9 2.3 %fusion = f32[624,1280]{1,0:T(8,128)S(1)} fusion(bf16[1152,624]{1,0:T(8,128)(2,1)S(1)} %get-tuple-element.42, bf16[1152,1280]{1,0:T(8,128)(2,1)S(1)} %join.10), kind=kOutput, calls=%fused_computation.3 | convolution fusion | flops 1840250880 | bytes 7581696 | tf_op jit(solution)/shard_map/dot_general | solution.py:282
  149.6 2.7 %collective-permute-start.31 = (bf16[288,1280]{1,0:T(8,128)(2,1)S(1)}, bf16[288,1280]{1,0:T(8,128)(2,1)S(1)}, u32[]{:S(2)}, u32[]{:S(2)}) collective-permute-start(bf16[288,1280]{1,0:T(8,128)(2,1)S(1)} %collective-permute-done.23.refs_2_), channel_id=1, source_target_pairs={{0,2},{1,9},{2,4},{3,11},{4,6},{5,13},{6,0},{7,15},{8,10},{9,17},{... | collective-permute-start | bytes 2211848 | tf_op jit(solution)/shard_map/ppermute | solution.py:32
  155.1 3.3 %collective-permute-done.32 = bf16[288,1280]{1,0:T(8,128)(2,1)S(1)} collective-permute-done((bf16[288,1280]{1,0:T(8,128)(2,1)S(1)}, bf16[288,1280]{1,0:T(8,128)(2,1)S(1)}, u32[]{:S(2)}, u32[]{:S(2)}) %collective-permute-start.32) | collective-permute-done | bytes 737312 | tf_op jit(solution)/shard_map/ppermute | solution.py:32
  158.9 3.8 %convolution_add_fusion.2 = f32[624,1280]{1,0:T(8,128)S(1)} fusion(f32[624,1280]{1,0:T(8,128)S(1)} %fusion, bf16[2016,624]{1,0:T(8,128)(2,1)S(1)} %get-tuple-element.49, bf16[2016,1280]{1,0:T(8,128)(2,1)S(1)} %join.14), kind=kOutput, calls=%fused_computation.2 | convolution fusion | flops 3221237760 | bytes 14066688 | tf_op jit(solution)/shard_map/dot_general | solution.py:282
  172.0 6.1 %collective-permute-done.35 = bf16[288,1280]{1,0:T(8,128)(2,1)S(1)} collective-permute-done((bf16[288,1280]{1,0:T(8,128)(2,1)S(1)}, bf16[288,1280]{1,0:T(8,128)(2,1)S(1)}, u32[]{:S(2)}, u32[]{:S(2)}) %collective-permute-start.35) | collective-permute-done | bytes 737312 | tf_op jit(solution)/shard_map/ppermute | solution.py:32
  179.4 5.7 %collective-permute-start.36 = (f32[312,1280]{1,0:T(8,128)S(1)}, f32[312,1280]{1,0:T(8,128)S(1)}, u32[]{:S(2)}, u32[]{:S(2)}) collective-permute-start(f32[312,1280]{1,0:T(8,128)S(1)} %get-tuple-element.62), channel_id=1, source_target_pairs={{0,1},{1,0},{2,3},{3,2},{4,5},{5,4},{6,7},{7,6},{8,9},{9,8},{10,11... | collective-permute-start | bytes 4792328 | tf_op jit(solution)/shard_map/ppermute | solution.py:22
  185.1 3.1 %collective-permute-done.36.got_ref = f32[312,1280]{1,0:T(8,128)S(1)} collective-permute-done((f32[312,1280]{1,0:T(8,128)S(1)}, f32[312,1280]{1,0:T(8,128)S(1)}, u32[]{:S(2)}, u32[]{:S(2)}) %collective-permute-start.36) | collective-permute-done | bytes 1597472 | tf_op jit(solution)/shard_map/ppermute | solution.py:22
  188.2 1.9 assemble.1
  (83 shorter events, 39.3 us)
Async XLA Ops:
  3.0 7.7 %collective-permute-start = (bf16[4,48,624]{2,1,0:T(8,128)(2,1)S(1)}, bf16[4,48,624]{2,1,0:T(8,128)(2,1)S(1)}, u32[]{:S(2)}, u32[]{:S(2)}) collective-permute-start(bf16[4,48,624]{2,1,0:T(8,128)(2,1)S(1)} %get-tuple-element.35), channel_id=1, source_target_pairs={{0,8},{1,3},{2,10},{3,5},{4,12},{5,7},{6,14},{7,1},{8,16},{9,11},{... | collective-permute-start | bytes 718856 | tf_op jit(solution)/shard_map/ppermute | solution.py:32
  4.8 8.0 %collective-permute-start.1 = (bf16[4,48,624]{2,1,0:T(8,128)(2,1)S(1)}, bf16[4,48,624]{2,1,0:T(8,128)(2,1)S(1)}, u32[]{:S(2)}, u32[]{:S(2)}) collective-permute-start(bf16[4,48,624]{2,1,0:T(8,128)(2,1)S(1)} %get-tuple-element.36), channel_id=1, source_target_pairs={{0,24},{1,7},{2,26},{3,1},{4,28},{5,3},{6,30},{7,5},{8,0},{9,15},{... | collective-permute-start | bytes 718856 | tf_op jit(solution)/shard_map/ppermute | solution.py:32
  14.8 9.2 %collective-permute-start.4 = (bf16[4,48,624]{2,1,0:T(8,128)(2,1)S(1)}, bf16[4,48,624]{2,1,0:T(8,128)(2,1)S(1)}, u32[]{:S(2)}, u32[]{:S(2)}) collective-permute-start(bf16[4,48,624]{2,1,0:T(8,128)(2,1)S(1)} %get-tuple-element.40), channel_id=1, source_target_pairs={{0,6},{1,25},{2,0},{3,27},{4,2},{5,29},{6,4},{7,31},{8,14},{9,1},{... | collective-permute-start | bytes 718856 | tf_op jit(solution)/shard_map/ppermute | solution.py:32
  15.9 8.1 %collective-permute-start.5 = (bf16[4,48,624]{2,1,0:T(8,128)(2,1)S(1)}, bf16[4,48,624]{2,1,0:T(8,128)(2,1)S(1)}, u32[]{:S(2)}, u32[]{:S(2)}) collective-permute-start(bf16[4,48,624]{2,1,0:T(8,128)(2,1)S(1)} %get-tuple-element.41), channel_id=1, source_target_pairs={{0,4},{1,17},{2,6},{3,19},{4,0},{5,21},{6,2},{7,23},{8,12},{9,25},... | collective-permute-start | bytes 718856 | tf_op jit(solution)/shard_map/ppermute | solution.py:32
  24.0 20.6 %collective-permute-start.14 = (bf16[16,48,624]{2,1,0:T(8,128)(2,1)S(1)}, bf16[16,48,624]{2,1,0:T(8,128)(2,1)S(1)}, u32[]{:S(2)}, u32[]{:S(2)}) collective-permute-start(bf16[16,48,624]{2,1,0:T(8,128)(2,1)S(1)} %join.8.refs_0_), channel_id=1, source_target_pairs={{0,32},{32,64},{64,96},{96,0},{1,33},{33,65},{65,97},{97,1},{2,34}... | collective-permute-start | bytes 2875400 | tf_op jit(solution)/shard_map/ppermute | solution.py:18
  25.4 20.7 %collective-permute-start.13 = (bf16[16,48,624]{2,1,0:T(8,128)(2,1)S(1)}, bf16[16,48,624]{2,1,0:T(8,128)(2,1)S(1)}, u32[]{:S(2)}, u32[]{:S(2)}) collective-permute-start(bf16[16,48,624]{2,1,0:T(8,128)(2,1)S(1)} %join.8.refs_0_), channel_id=1, source_target_pairs={{0,96},{32,0},{64,32},{96,64},{1,97},{33,1},{65,33},{97,65},{2,98}... | collective-permute-start | bytes 2875400 | tf_op jit(solution)/shard_map/ppermute | solution.py:18
  30.5 20.4 %collective-permute-start.18 = (bf16[96,1280]{1,0:T(8,128)(2,1)S(1)}, bf16[96,1280]{1,0:T(8,128)(2,1)S(1)}, u32[]{:S(2)}, u32[]{:S(2)}) collective-permute-start(bf16[96,1280]{1,0:T(8,128)(2,1)S(1)} %get-tuple-element.50), channel_id=1, source_target_pairs={{0,96},{32,0},{64,32},{96,64},{1,97},{33,1},{65,33},{97,65},{2,98}... | collective-permute-start | bytes 737288 | tf_op jit(solution)/shard_map/ppermute | solution.py:18
  31.9 31.0 %collective-permute-start.19 = (bf16[96,1280]{1,0:T(8,128)(2,1)S(1)}, bf16[96,1280]{1,0:T(8,128)(2,1)S(1)}, u32[]{:S(2)}, u32[]{:S(2)}) collective-permute-start(bf16[96,1280]{1,0:T(8,128)(2,1)S(1)} %get-tuple-element.51), channel_id=1, source_target_pairs={{0,64},{32,96},{64,0},{96,32},{1,65},{33,97},{65,1},{97,33},{2,66}... | collective-permute-start | bytes 737288 | tf_op jit(solution)/shard_map/ppermute | solution.py:18
  44.7 25.2 %collective-permute-start.15 = (bf16[8,48,624]{2,1,0:T(8,128)(2,1)S(1)}, bf16[8,48,624]{2,1,0:T(8,128)(2,1)S(1)}, u32[]{:S(2)}, u32[]{:S(2)}) collective-permute-start(bf16[8,48,624]{2,1,0:T(8,128)(2,1)S(1)} %slice.24), channel_id=1, source_target_pairs={{0,32},{32,64},{64,96},{96,0},{1,33},{33,65},{65,97},{97,1},{2,34}... | collective-permute-start | bytes 1437704 | tf_op jit(solution)/shard_map/ppermute | solution.py:18
  46.2 23.9 %collective-permute-start.16 = (bf16[8,48,624]{2,1,0:T(8,128)(2,1)S(1)}, bf16[8,48,624]{2,1,0:T(8,128)(2,1)S(1)}, u32[]{:S(2)}, u32[]{:S(2)}) collective-permute-start(bf16[8,48,624]{2,1,0:T(8,128)(2,1)S(1)} %slice.25), channel_id=1, source_target_pairs={{0,96},{32,0},{64,32},{96,64},{1,97},{33,1},{65,33},{97,65},{2,98}... | collective-permute-start | bytes 1437704 | tf_op jit(solution)/shard_map/ppermute | solution.py:18
  46.4 19.3 %collective-permute-start.20 = (bf16[96,1280]{1,0:T(8,128)(2,1)S(1)}, bf16[96,1280]{1,0:T(8,128)(2,1)S(1)}, u32[]{:S(2)}, u32[]{:S(2)}) collective-permute-start(bf16[96,1280]{1,0:T(8,128)(2,1)S(1)} %get-tuple-element.52), channel_id=1, source_target_pairs={{0,32},{32,64},{64,96},{96,0},{1,33},{33,65},{65,97},{97,1},{2,34}... | collective-permute-start | bytes 737288 | tf_op jit(solution)/shard_map/ppermute | solution.py:18
  50.9 30.8 %collective-permute-start.6 = (bf16[16,48,624]{2,1,0:T(8,128)(2,1)S(1)}, bf16[16,48,624]{2,1,0:T(8,128)(2,1)S(1)}, u32[]{:S(2)}, u32[]{:S(2)}) collective-permute-start(bf16[16,48,624]{2,1,0:T(8,128)(2,1)S(1)} %join.8.refs_0_), channel_id=1, source_target_pairs={{0,1},{1,0},{2,3},{3,2},{4,5},{5,4},{6,7},{7,6},{8,9},{9,8},{10,11... | collective-permute-start | bytes 2875400 | tf_op jit(solution)/shard_map/ppermute | solution.py:22
  65.7 16.6 %collective-permute-start.21 = (bf16[288,1280]{1,0:T(8,128)(2,1)S(1)}, bf16[288,1280]{1,0:T(8,128)(2,1)S(1)}, u32[]{:S(2)}, u32[]{:S(2)}) collective-permute-start(bf16[288,1280]{1,0:T(8,128)(2,1)S(1)} %join.12.refs_0_), channel_id=1, source_target_pairs={{0,8},{1,3},{2,10},{3,5},{4,12},{5,7},{6,14},{7,1},{8,16},{9,11},{... | collective-permute-start | bytes 2211848 | tf_op jit(solution)/shard_map/ppermute | solution.py:32
  69.9 13.4 %collective-permute-start.22 = (bf16[288,1280]{1,0:T(8,128)(2,1)S(1)}, bf16[288,1280]{1,0:T(8,128)(2,1)S(1)}, u32[]{:S(2)}, u32[]{:S(2)}) collective-permute-start(bf16[288,1280]{1,0:T(8,128)(2,1)S(1)} %join.12.refs_0_), channel_id=1, source_target_pairs={{0,24},{1,7},{2,26},{3,1},{4,28},{5,3},{6,30},{7,5},{8,0},{9,15},{... | collective-permute-start | bytes 2211848 | tf_op jit(solution)/shard_map/ppermute | solution.py:32
  70.0 10.3 %collective-permute-start.10 = (bf16[96,1280]{1,0:T(8,128)(2,1)S(1)}, bf16[96,1280]{1,0:T(8,128)(2,1)S(1)}, u32[]{:S(2)}, u32[]{:S(2)}) collective-permute-start(bf16[96,1280]{1,0:T(8,128)(2,1)S(1)} %get-tuple-element.48.refs_0_), channel_id=1, source_target_pairs={{0,16},{1,5},{2,18},{3,7},{4,20},{5,1},{6,22},{7,3},{8,24},{9,13},... | collective-permute-start | bytes 737288 | tf_op jit(solution)/shard_map/ppermute | solution.py:32
  74.5 83.9 %collective-permute-start.17 = (bf16[48,48,624]{2,1,0:T(8,128)(2,1)S(1)}, bf16[48,48,624]{2,1,0:T(8,128)(2,1)S(1)}, u32[]{:S(2)}, u32[]{:S(2)}) collective-permute-start(bf16[48,48,624]{2,1,0:T(8,128)(2,1)S(1)} %join.11.refs_0_), channel_id=1, source_target_pairs={{0,1},{1,0},{2,3},{3,2},{4,5},{5,4},{6,7},{7,6},{8,9},{9,8},{10,11... | collective-permute-start | bytes 8626184 | tf_op jit(solution)/shard_map/ppermute | solution.py:22
  80.3 10.7 %collective-permute-start.24 = (bf16[288,1280]{1,0:T(8,128)(2,1)S(1)}, bf16[288,1280]{1,0:T(8,128)(2,1)S(1)}, u32[]{:S(2)}, u32[]{:S(2)}) collective-permute-start(bf16[288,1280]{1,0:T(8,128)(2,1)S(1)} %join.12.refs_0_), channel_id=1, source_target_pairs={{0,2},{1,9},{2,4},{3,11},{4,6},{5,13},{6,0},{7,15},{8,10},{9,17},{... | collective-permute-start | bytes 2211848 | tf_op jit(solution)/shard_map/ppermute | solution.py:32
  81.7 25.7 %collective-permute-start.11 = (bf16[384,1280]{1,0:T(8,128)(2,1)S(1)}, bf16[384,1280]{1,0:T(8,128)(2,1)S(1)}, u32[]{:S(2)}, u32[]{:S(2)}) collective-permute-start(bf16[384,1280]{1,0:T(8,128)(2,1)S(1)} %join.9.refs_0_), channel_id=1, source_target_pairs={{0,2},{1,9},{2,4},{3,11},{4,6},{5,13},{6,0},{7,15},{8,10},{9,17},{... | collective-permute-start | bytes 2949128 | tf_op jit(solution)/shard_map/ppermute | solution.py:32
  82.3 25.6 %collective-permute-start.12 = (bf16[384,1280]{1,0:T(8,128)(2,1)S(1)}, bf16[384,1280]{1,0:T(8,128)(2,1)S(1)}, u32[]{:S(2)}, u32[]{:S(2)}) collective-permute-start(bf16[384,1280]{1,0:T(8,128)(2,1)S(1)} %join.9.refs_0_), channel_id=1, source_target_pairs={{0,6},{1,25},{2,0},{3,27},{4,2},{5,29},{6,4},{7,31},{8,14},{9,1},{... | collective-permute-start | bytes 2949128 | tf_op jit(solution)/shard_map/ppermute | solution.py:32
  83.2 24.1 %collective-permute-start.25 = (bf16[288,1280]{1,0:T(8,128)(2,1)S(1)}, bf16[288,1280]{1,0:T(8,128)(2,1)S(1)}, u32[]{:S(2)}, u32[]{:S(2)}) collective-permute-start(bf16[288,1280]{1,0:T(8,128)(2,1)S(1)} %join.12.refs_0_), channel_id=1, source_target_pairs={{0,6},{1,25},{2,0},{3,27},{4,2},{5,29},{6,4},{7,31},{8,14},{9,1},{... | collective-permute-start | bytes 2211848 | tf_op jit(solution)/shard_map/ppermute | solution.py:32
  91.1 23.8 %collective-permute-start.23 = (bf16[288,1280]{1,0:T(8,128)(2,1)S(1)}, bf16[288,1280]{1,0:T(8,128)(2,1)S(1)}, u32[]{:S(2)}, u32[]{:S(2)}) collective-permute-start(bf16[288,1280]{1,0:T(8,128)(2,1)S(1)} %collective-permute-done.21.refs_0_), channel_id=1, source_target_pairs={{0,8},{1,3},{2,10},{3,5},{4,12},{5,7},{6,14},{7,1},{8,16},{9,11},{... | collective-permute-start | bytes 2211848 | tf_op jit(solution)/shard_map/ppermute | solution.py:32
  107.3 14.5 %collective-permute-start.26 = (bf16[288,1280]{1,0:T(8,128)(2,1)S(1)}, bf16[288,1280]{1,0:T(8,128)(2,1)S(1)}, u32[]{:S(2)}, u32[]{:S(2)}) collective-permute-start(bf16[288,1280]{1,0:T(8,128)(2,1)S(1)} %collective-permute-done.24.refs_3_), channel_id=1, source_target_pairs={{0,2},{1,9},{2,4},{3,11},{4,6},{5,13},{6,0},{7,15},{8,10},{9,17},{... | collective-permute-start | bytes 2211848 | tf_op jit(solution)/shard_map/ppermute | solution.py:32
  107.4 46.0 %collective-permute-start.27 = (bf16[576,1280]{1,0:T(8,128)(2,1)S(1)}, bf16[576,1280]{1,0:T(8,128)(2,1)S(1)}, u32[]{:S(2)}, u32[]{:S(2)}) collective-permute-start(bf16[576,1280]{1,0:T(8,128)(2,1)S(1)} %join.13.refs_1_), channel_id=1, source_target_pairs={{0,2},{1,9},{2,4},{3,11},{4,6},{5,13},{6,0},{7,15},{8,10},{9,17},{... | collective-permute-start | bytes 4423688 | tf_op jit(solution)/shard_map/ppermute | solution.py:32
  108.0 45.6 %collective-permute-start.28 = (bf16[576,1280]{1,0:T(8,128)(2,1)S(1)}, bf16[576,1280]{1,0:T(8,128)(2,1)S(1)}, u32[]{:S(2)}, u32[]{:S(2)}) collective-permute-start(bf16[576,1280]{1,0:T(8,128)(2,1)S(1)} %join.13.refs_1_), channel_id=1, source_target_pairs={{0,6},{1,25},{2,0},{3,27},{4,2},{5,29},{6,4},{7,31},{8,14},{9,1},{... | collective-permute-start | bytes 4423688 | tf_op jit(solution)/shard_map/ppermute | solution.py:32
  114.8 32.1 %collective-permute-start.29 = (bf16[192,1280]{1,0:T(8,128)(2,1)S(1)}, bf16[192,1280]{1,0:T(8,128)(2,1)S(1)}, u32[]{:S(2)}, u32[]{:S(2)}) collective-permute-start(bf16[192,1280]{1,0:T(8,128)(2,1)S(1)} %slice.26), channel_id=1, source_target_pairs={{0,2},{1,9},{2,4},{3,11},{4,6},{5,13},{6,0},{7,15},{8,10},{9,17},{... | collective-permute-start | bytes 1474568 | tf_op jit(solution)/shard_map/ppermute | solution.py:32
  121.8 27.8 %collective-permute-start.30 = (bf16[192,1280]{1,0:T(8,128)(2,1)S(1)}, bf16[192,1280]{1,0:T(8,128)(2,1)S(1)}, u32[]{:S(2)}, u32[]{:S(2)}) collective-permute-start(bf16[192,1280]{1,0:T(8,128)(2,1)S(1)} %slice.27), channel_id=1, source_target_pairs={{0,6},{1,25},{2,0},{3,27},{4,2},{5,29},{6,4},{7,31},{8,14},{9,1},{... | collective-permute-start | bytes 1474568 | tf_op jit(solution)/shard_map/ppermute | solution.py:32
  146.9 11.5 %collective-permute-start.32 = (bf16[288,1280]{1,0:T(8,128)(2,1)S(1)}, bf16[288,1280]{1,0:T(8,128)(2,1)S(1)}, u32[]{:S(2)}, u32[]{:S(2)}) collective-permute-start(bf16[288,1280]{1,0:T(8,128)(2,1)S(1)} %collective-permute-done.23.refs_2_), channel_id=1, source_target_pairs={{0,6},{1,25},{2,0},{3,27},{4,2},{5,29},{6,4},{7,31},{8,14},{9,1},{... | collective-permute-start | bytes 2211848 | tf_op jit(solution)/shard_map/ppermute | solution.py:32
  149.6 17.2 %collective-permute-start.31 = (bf16[288,1280]{1,0:T(8,128)(2,1)S(1)}, bf16[288,1280]{1,0:T(8,128)(2,1)S(1)}, u32[]{:S(2)}, u32[]{:S(2)}) collective-permute-start(bf16[288,1280]{1,0:T(8,128)(2,1)S(1)} %collective-permute-done.23.refs_2_), channel_id=1, source_target_pairs={{0,2},{1,9},{2,4},{3,11},{4,6},{5,13},{6,0},{7,15},{8,10},{9,17},{... | collective-permute-start | bytes 2211848 | tf_op jit(solution)/shard_map/ppermute | solution.py:32
  153.5 15.9 %collective-permute-start.33 = (bf16[144,1280]{1,0:T(8,128)(2,1)S(1)}, bf16[144,1280]{1,0:T(8,128)(2,1)S(1)}, u32[]{:S(2)}, u32[]{:S(2)}) collective-permute-start(bf16[144,1280]{1,0:T(8,128)(2,1)S(1)} %slice.28), channel_id=1, source_target_pairs={{0,2},{1,9},{2,4},{3,11},{4,6},{5,13},{6,0},{7,15},{8,10},{9,17},{... | collective-permute-start | bytes 1105928 | tf_op jit(solution)/shard_map/ppermute | solution.py:32
  153.6 16.9 %collective-permute-start.34 = (bf16[432,1280]{1,0:T(8,128)(2,1)S(1)}, bf16[432,1280]{1,0:T(8,128)(2,1)S(1)}, u32[]{:S(2)}, u32[]{:S(2)}) collective-permute-start(bf16[432,1280]{1,0:T(8,128)(2,1)S(1)} %slice.29), channel_id=1, source_target_pairs={{0,6},{1,25},{2,0},{3,27},{4,2},{5,29},{6,4},{7,31},{8,14},{9,1},{... | collective-permute-start | bytes 3317768 | tf_op jit(solution)/shard_map/ppermute | solution.py:32
  158.4 19.7 %collective-permute-start.35 = (bf16[288,1280]{1,0:T(8,128)(2,1)S(1)}, bf16[288,1280]{1,0:T(8,128)(2,1)S(1)}, u32[]{:S(2)}, u32[]{:S(2)}) collective-permute-start(bf16[288,1280]{1,0:T(8,128)(2,1)S(1)} %collective-permute-done.32), channel_id=1, source_target_pairs={{0,6},{1,25},{2,0},{3,27},{4,2},{5,29},{6,4},{7,31},{8,14},{9,1},{... | collective-permute-start | bytes 2211848 | tf_op jit(solution)/shard_map/ppermute | solution.py:32
  179.4 8.8 %collective-permute-start.36 = (f32[312,1280]{1,0:T(8,128)S(1)}, f32[312,1280]{1,0:T(8,128)S(1)}, u32[]{:S(2)}, u32[]{:S(2)}) collective-permute-start(f32[312,1280]{1,0:T(8,128)S(1)} %get-tuple-element.62), channel_id=1, source_target_pairs={{0,1},{1,0},{2,3},{3,2},{4,5},{5,4},{6,7},{7,6},{8,9},{9,8},{10,11... | collective-permute-start | bytes 4792328 | tf_op jit(solution)/shard_map/ppermute | solution.py:22
  (7 other events, 31.0 us)
where the time goes:
time: 190 us
  waiting for transfers between devices  103 us (54%)
  starting transfers between devices  62.4 us (33%)
  matrix products  14.8 us (8%)
  Pallas kernels  5.16 us (3%)
  other arithmetic  2.46 us (1%)
  local copies, waits for them, and re-layouts  2.1 us (1%)
    ppermute x26, waiting for transfers between devices, along_plane(): return lax.ppermute(block, ('x', 'z', 'core'), route)  82 us
    ppermute x26, starting transfers between devices, along_plane(): return lax.ppermute(block, ('x', 'z', 'core'), route)  30.8 us
    ppermute x4, starting transfers between devices, swap_cores(): return lax.ppermute(block, 'core', [(0, 1), (1, 0)])  24.5 us
    ppermute x7, waiting for transfers between devices, along_y(): lax.ppermute(block, 'y', [(i, (i + step) % SIDE) for i in range(SIDE)])  16.4 us
    dot_general x10, matrix products, product(): lax.dot_general(weight, block, (((0,), (0,)), ((), ())), preferred_elemen...  14.8 us
    ppermute x7, starting transfers between devices, along_y(): lax.ppermute(block, 'y', [(i, (i + step) % SIDE) for i in range(SIDE)])  7.09 us
    ppermute x4, waiting for transfers between devices, swap_cores(): return lax.ppermute(block, 'core', [(0, 1), (1, 0)])  4.57 us
  transfers between devices with their start and end apart: 37, of which 21 were waited for; matrix products, arithmetic and copies ran while one was open for 9% of the time, Pallas kernels for 1%

commit v1 on v0

--- a/solution.py
+++ b/solution.py
@@ -180,10 +180,10 @@
     near_opposite = along_plane(near_sides[0][:cut], 1, 1), along_plane(near_sides[1][cut:], 1, -1)
     far_opposite = along_plane(far_sides[1], 1, -1)
 
-    first = at(0, 0, -1, 1, 2) + at(-1, 0) + at(1, 0) + at(2, 0)
-    parts = [(first, 0, join([own, near, far, *own_sides, own_opposite]))]
+    first = at(0, 0, -1, 1, 2) + at(-1, 0) + at(1, 0)
+    parts = [(first, 0, join([own, near, far, *own_sides]))]
     parts += [(at(v, -1, 1), 0, block) for v, block in zip((-1, 1), near_sides)]
-    parts += [(at(v, 2), 0, block) for v, block in zip((-1, 1), far_sides)]
+    parts += [(at(-1, 2) + at(1, 2) + at(2, 0), 0, join([*far_sides, own_opposite]))]
     parts += [(at(2, -1, 1), 0, near_opposite[0]), (at(2, -1, 1), len(OTHERS) // 2, near_opposite[1])]
     parts += [(at(2, 2), 0, far_opposite)]
     return parts
@@ -290,7 +290,7 @@
         layout.append(blocks[skipped : skipped + block.shape[0] // rows.shape[1]])
     weights = (*arrange(layout, rest, other_rest), weights[1])
     blocks = [block for *_, block in parts] + [early[1][1]]
-    for i in (0, 1, 2, len(parts), *range(3, len(parts))):
+    for i in (1, 2, len(parts), 0, 4, 5, 3, *range(6, len(parts))):
         tile = lax.optimization_barrier(tile + product(weights[i], blocks[i]))
 
     kept, sent = halve(tile)

time: 190 us -> 174 us (0.916)
  the two profiles are of different devices: /device:TPU:15 before, /device:TPU:1 now
where the time goes in v1:
time: 174 us
  waiting for transfers between devices  101 us (58%)
  starting transfers between devices  49.8 us (29%)
  matrix products  14.3 us (8%)
  Pallas kernels  5.28 us (3%)
  local copies, waits for them, and re-layouts  2.1 us (1%)
    ppermute x26, waiting for transfers between devices, along_plane(): return lax.ppermute(block, ('x', 'z', 'core'), route)  78.5 us
    ppermute x26, starting transfers between devices, along_plane(): return lax.ppermute(block, ('x', 'z', 'core'), route)  23.8 us
    ppermute x7, waiting for transfers between devices, along_y(): lax.ppermute(block, 'y', [(i, (i + step) % SIDE) for i in range(SIDE)])  17.5 us
    ppermute x4, starting transfers between devices, swap_cores(): return lax.ppermute(block, 'core', [(0, 1), (1, 0)])  14.6 us
    dot_general x9, matrix products, product(): lax.dot_general(weight, block, (((0,), (0,)), ((), ())), preferred_elemen...  14.3 us
    ppermute x7, starting transfers between devices, along_y(): lax.ppermute(block, 'y', [(i, (i + step) % SIDE) for i in range(SIDE)])  11.4 us
    ppermute x4, waiting for transfers between devices, swap_cores(): return lax.ppermute(block, 'core', [(0, 1), (1, 0)])  4.57 us
  transfers between devices with their start and end apart: 37, of which 20 were waited for; matrix products, arithmetic and copies ran while one was open for 9% of the time, Pallas kernels for 1%

profile of v1, /device:TPU:1, one launch (start us, length us, event | category | flops | bytes accessed | tf_op | source)
XLA Modules:
  0.0 173.9 jit_solution(10741605625621140894)
XLA Ops:
  3.0 2.5 %collective-permute-start = (bf16[4,48,624]{2,1,0:T(8,128)(2,1)S(1)}, bf16[4,48,624]{2,1,0:T(8,128)(2,1)S(1)}, u32[]{:S(2)}, u32[]{:S(2)}) collective-permute-start(bf16[4,48,624]{2,1,0:T(8,128)(2,1)S(1)} %get-tuple-element.34), channel_id=1, source_target_pairs={{0,8},{1,3},{2,10},{3,5},{4,12},{5,7},{6,14},{7,1},{8,16},{9,11},{... | collective-permute-start | bytes 718856 | tf_op jit(solution)/shard_map/ppermute | solution.py:32
  5.6 2.2 %collective-permute-start.1 = (bf16[4,48,624]{2,1,0:T(8,128)(2,1)S(1)}, bf16[4,48,624]{2,1,0:T(8,128)(2,1)S(1)}, u32[]{:S(2)}, u32[]{:S(2)}) collective-permute-start(bf16[4,48,624]{2,1,0:T(8,128)(2,1)S(1)} %get-tuple-element.35), channel_id=1, source_target_pairs={{0,24},{1,7},{2,26},{3,1},{4,28},{5,3},{6,30},{7,5},{8,0},{9,15},{... | collective-permute-start | bytes 718856 | tf_op jit(solution)/shard_map/ppermute | solution.py:32
  9.0 2.5 %collective-permute-done.refs_1_ = bf16[4,48,624]{2,1,0:T(8,128)(2,1)S(1)} collective-permute-done((bf16[4,48,624]{2,1,0:T(8,128)(2,1)S(1)}, bf16[4,48,624]{2,1,0:T(8,128)(2,1)S(1)}, u32[]{:S(2)}, u32[]{:S(2)}) %collective-permute-start) | collective-permute-done | bytes 239648 | tf_op jit(solution)/shard_map/ppermute | solution.py:32
  11.5 2.0 %collective-permute-done.1.refs_2_ = bf16[4,48,624]{2,1,0:T(8,128)(2,1)S(1)} collective-permute-done((bf16[4,48,624]{2,1,0:T(8,128)(2,1)S(1)}, bf16[4,48,624]{2,1,0:T(8,128)(2,1)S(1)}, u32[]{:S(2)}, u32[]{:S(2)}) %collective-permute-start.1) | collective-permute-done | bytes 239648 | tf_op jit(solution)/shard_map/ppermute | solution.py:32
  13.5 1.7 collective-permute-done.2.refs_3_
  16.4 1.6 collective-permute-start.4
  19.4 2.5 %collective-permute-done.3.refs_1_ = bf16[4,48,624]{2,1,0:T(8,128)(2,1)S(1)} collective-permute-done((bf16[4,48,624]{2,1,0:T(8,128)(2,1)S(1)}, bf16[4,48,624]{2,1,0:T(8,128)(2,1)S(1)}, u32[]{:S(2)}, u32[]{:S(2)}) %collective-permute-start.3) | collective-permute-done | bytes 239648 | tf_op jit(solution)/shard_map/ppermute | solution.py:32
  21.9 1.9 %collective-permute-done.4.refs_2_ = bf16[4,48,624]{2,1,0:T(8,128)(2,1)S(1)} collective-permute-done((bf16[4,48,624]{2,1,0:T(8,128)(2,1)S(1)}, bf16[4,48,624]{2,1,0:T(8,128)(2,1)S(1)}, u32[]{:S(2)}, u32[]{:S(2)}) %collective-permute-start.4) | collective-permute-done | bytes 239648 | tf_op jit(solution)/shard_map/ppermute | solution.py:32
  23.8 1.6 collective-permute-done.5.refs_3_
  26.9 1.5 collective-permute-start.13
  28.4 3.1 %collective-permute-start.7 = (bf16[4,48,1280]{2,1,0:T(8,128)(2,1)S(1)}, bf16[4,48,1280]{2,1,0:T(8,128)(2,1)S(1)}, u32[]{:S(2)}, u32[]{:S(2)}) collective-permute-start(bf16[4,48,1280]{2,1,0:T(8,128)(2,1)S(1)} %get-tuple-element.46), channel_id=1, source_target_pairs={{0,1},{1,0},{2,3},{3,2},{4,5},{5,4},{6,7},{7,6},{8,9},{9,8},{10,11... | collective-permute-start | bytes 1474568 | tf_op jit(solution)/shard_map/ppermute | solution.py:22
  33.0 1.6 collective-permute-start.18
  35.7 16.8 %collective-permute-done.18.refs_0_ = bf16[96,1280]{1,0:T(8,128)(2,1)S(1)} collective-permute-done((bf16[96,1280]{1,0:T(8,128)(2,1)S(1)}, bf16[96,1280]{1,0:T(8,128)(2,1)S(1)}, u32[]{:S(2)}, u32[]{:S(2)}) %collective-permute-start.18) | collective-permute-done | bytes 245792 | tf_op jit(solution)/shard_map/ppermute | solution.py:18
  53.6 2.2 %collective-permute-start.9 = (bf16[96,1280]{1,0:T(8,128)(2,1)S(1)}, bf16[96,1280]{1,0:T(8,128)(2,1)S(1)}, u32[]{:S(2)}, u32[]{:S(2)}) collective-permute-start(bf16[96,1280]{1,0:T(8,128)(2,1)S(1)} %get-tuple-element.47.refs_0_), channel_id=1, source_target_pairs={{0,24},{1,7},{2,26},{3,1},{4,28},{5,3},{6,30},{7,5},{8,0},{9,15},{... | collective-permute-start | bytes 737288 | tf_op jit(solution)/shard_map/ppermute | solution.py:32
  56.6 5.3 %collective-permute-start.15 = (bf16[8,48,624]{2,1,0:T(8,128)(2,1)S(1)}, bf16[8,48,624]{2,1,0:T(8,128)(2,1)S(1)}, u32[]{:S(2)}, u32[]{:S(2)}) collective-permute-start(bf16[8,48,624]{2,1,0:T(8,128)(2,1)S(1)} %slice.24), channel_id=1, source_target_pairs={{0,32},{32,64},{64,96},{96,0},{1,33},{33,65},{65,97},{97,1},{2,34}... | collective-permute-start | bytes 1437704 | tf_op jit(solution)/shard_map/ppermute | solution.py:18
  65.2 6.3 %collective-permute-done.10.refs_3_ = bf16[96,1280]{1,0:T(8,128)(2,1)S(1)} collective-permute-done((bf16[96,1280]{1,0:T(8,128)(2,1)S(1)}, bf16[96,1280]{1,0:T(8,128)(2,1)S(1)}, u32[]{:S(2)}, u32[]{:S(2)}) %collective-permute-start.10) | collective-permute-done | bytes 245792 | tf_op jit(solution)/shard_map/ppermute | solution.py:32
  71.5 7.8 %collective-permute-start.6 = (bf16[16,48,624]{2,1,0:T(8,128)(2,1)S(1)}, bf16[16,48,624]{2,1,0:T(8,128)(2,1)S(1)}, u32[]{:S(2)}, u32[]{:S(2)}) collective-permute-start(bf16[16,48,624]{2,1,0:T(8,128)(2,1)S(1)} %join.9.refs_0_), channel_id=1, source_target_pairs={{0,1},{1,0},{2,3},{3,2},{4,5},{5,4},{6,7},{7,6},{8,9},{9,8},{10,11... | collective-permute-start | bytes 2875400 | tf_op jit(solution)/shard_map/ppermute | solution.py:22
  80.8 2.7 %collective-permute-start.12 = (bf16[384,1280]{1,0:T(8,128)(2,1)S(1)}, bf16[384,1280]{1,0:T(8,128)(2,1)S(1)}, u32[]{:S(2)}, u32[]{:S(2)}) collective-permute-start(bf16[384,1280]{1,0:T(8,128)(2,1)S(1)} %join.10.refs_0_), channel_id=1, source_target_pairs={{0,6},{1,25},{2,0},{3,27},{4,2},{5,29},{6,4},{7,31},{8,14},{9,1},{... | collective-permute-start | bytes 2949128 | tf_op jit(solution)/shard_map/ppermute | solution.py:32
  83.6 18.2 %collective-permute-done.28.refs_3_ = bf16[288,1280]{1,0:T(8,128)(2,1)S(1)} collective-permute-done((bf16[288,1280]{1,0:T(8,128)(2,1)S(1)}, bf16[288,1280]{1,0:T(8,128)(2,1)S(1)}, u32[]{:S(2)}, u32[]{:S(2)}) %collective-permute-start.28) | collective-permute-done | bytes 737312 | tf_op jit(solution)/shard_map/ppermute | solution.py:32
  102.8 9.6 %collective-permute-done.29.refs_4_ = bf16[288,1280]{1,0:T(8,128)(2,1)S(1)} collective-permute-done((bf16[288,1280]{1,0:T(8,128)(2,1)S(1)}, bf16[288,1280]{1,0:T(8,128)(2,1)S(1)}, u32[]{:S(2)}, u32[]{:S(2)}) %collective-permute-start.29) | collective-permute-done | bytes 737312 | tf_op jit(solution)/shard_map/ppermute | solution.py:32
  112.4 9.1 %collective-permute-done.27.refs_2_ = bf16[288,1280]{1,0:T(8,128)(2,1)S(1)} collective-permute-done((bf16[288,1280]{1,0:T(8,128)(2,1)S(1)}, bf16[288,1280]{1,0:T(8,128)(2,1)S(1)}, u32[]{:S(2)}, u32[]{:S(2)}) %collective-permute-start.27) | collective-permute-done | bytes 737312 | tf_op jit(solution)/shard_map/ppermute | solution.py:32
  121.5 9.2 %collective-permute-done.25.refs_0_ = bf16[192,1280]{1,0:T(8,128)(2,1)S(1)} collective-permute-done((bf16[192,1280]{1,0:T(8,128)(2,1)S(1)}, bf16[192,1280]{1,0:T(8,128)(2,1)S(1)}, u32[]{:S(2)}, u32[]{:S(2)}) %collective-permute-start.25) | collective-permute-done | bytes 491552 | tf_op jit(solution)/shard_map/ppermute | solution.py:32
  130.8 2.7 %collective-permute-done.26.refs_1_ = bf16[192,1280]{1,0:T(8,128)(2,1)S(1)} collective-permute-done((bf16[192,1280]{1,0:T(8,128)(2,1)S(1)}, bf16[192,1280]{1,0:T(8,128)(2,1)S(1)}, u32[]{:S(2)}, u32[]{:S(2)}) %collective-permute-start.26) | collective-permute-done | bytes 491552 | tf_op jit(solution)/shard_map/ppermute | solution.py:32
  136.9 5.7 %collective-permute-done.34.refs_2_ = bf16[288,1280]{1,0:T(8,128)(2,1)S(1)} collective-permute-done((bf16[288,1280]{1,0:T(8,128)(2,1)S(1)}, bf16[288,1280]{1,0:T(8,128)(2,1)S(1)}, u32[]{:S(2)}, u32[]{:S(2)}) %collective-permute-start.34) | collective-permute-done | bytes 737312 | tf_op jit(solution)/shard_map/ppermute | solution.py:32
  144.1 2.4 %collective-permute-start.35 = (bf16[288,1280]{1,0:T(8,128)(2,1)S(1)}, bf16[288,1280]{1,0:T(8,128)(2,1)S(1)}, u32[]{:S(2)}, u32[]{:S(2)}) collective-permute-start(bf16[288,1280]{1,0:T(8,128)(2,1)S(1)} %collective-permute-done.33.refs_1_), channel_id=1, source_target_pairs={{0,6},{1,25},{2,0},{3,27},{4,2},{5,29},{6,4},{7,31},{8,14},{9,1},{... | collective-permute-start | bytes 2211848 | tf_op jit(solution)/shard_map/ppermute | solution.py:32
  146.5 4.0 %collective-permute-done.32.refs_0_ = bf16[288,1280]{1,0:T(8,128)(2,1)S(1)} collective-permute-done((bf16[288,1280]{1,0:T(8,128)(2,1)S(1)}, bf16[288,1280]{1,0:T(8,128)(2,1)S(1)}, u32[]{:S(2)}, u32[]{:S(2)}) %collective-permute-start.32) | collective-permute-done | bytes 737312 | tf_op jit(solution)/shard_map/ppermute | solution.py:32
  152.6 2.4 %convolution_add_fusion.3 = f32[624,1280]{1,0:T(8,128)S(1)} fusion(f32[624,1280]{1,0:T(8,128)S(1)} %fusion, bf16[1152,624]{1,0:T(8,128)(2,1)S(1)} %get-tuple-element.41, bf16[1152,1280]{1,0:T(8,128)(2,1)S(1)} %join.11), kind=kOutput, calls=%fused_computation.3 | convolution fusion | flops 1841049600 | bytes 10776576 | tf_op jit(solution)/shard_map/dot_general | solution.py:282
  157.2 3.2 %convolution_add_fusion.2 = f32[624,1280]{1,0:T(8,128)S(1)} fusion(f32[624,1280]{1,0:T(8,128)S(1)} %add.26, bf16[1728,624]{1,0:T(8,128)(2,1)S(1)} %get-tuple-element.54, bf16[1728,1280]{1,0:T(8,128)(2,1)S(1)} %join.16), kind=kOutput, calls=%fused_computation.2 | convolution fusion | flops 2761175040 | bytes 12969984 | tf_op jit(solution)/shard_map/dot_general | solution.py:282
  162.9 2.2 %convolution_add_fusion.1 = f32[624,1280]{1,0:T(8,128)S(1)} fusion(f32[624,1280]{1,0:T(8,128)S(1)} %add.29, bf16[864,624]{1,0:T(8,128)(2,1)S(1)} %get-tuple-element.57, bf16[864,1280]{1,0:T(8,128)(2,1)S(1)} %join.17), kind=kOutput, calls=%fused_computation.1 | convolution fusion | flops 1380986880 | bytes 9679872 | tf_op jit(solution)/shard_map/dot_general | solution.py:282
  166.3 2.6 %collective-permute-start.36 = (f32[312,1280]{1,0:T(8,128)S(1)}, f32[312,1280]{1,0:T(8,128)S(1)}, u32[]{:S(2)}, u32[]{:S(2)}) collective-permute-start(f32[312,1280]{1,0:T(8,128)S(1)} %get-tuple-element.60), channel_id=1, source_target_pairs={{0,1},{1,0},{2,3},{3,2},{4,5},{5,4},{6,7},{7,6},{8,9},{9,8},{10,11... | collective-permute-start | bytes 4792328 | tf_op jit(solution)/shard_map/ppermute | solution.py:22
  169.0 3.1 %collective-permute-done.36.got_ref = f32[312,1280]{1,0:T(8,128)S(1)} collective-permute-done((f32[312,1280]{1,0:T(8,128)S(1)}, f32[312,1280]{1,0:T(8,128)S(1)}, u32[]{:S(2)}, u32[]{:S(2)}) %collective-permute-start.36) | collective-permute-done | bytes 1597472 | tf_op jit(solution)/shard_map/ppermute | solution.py:22
  172.0 1.9 %assemble.1 = f32[312,2496]{1,0:T(8,128)} custom-call(f32[312,1280]{1,0:T(8,128)S(1)} %get-tuple-element.59.kept_ref, f32[312,1280]{1,0:T(8,128)S(1)} %collective-permute-done.36.got_ref), custom_call_target="tpu_custom_call" | custom-call | tf_op jit(solution)/shard_map/assemble/pallas_call | solution.py:250
  (81 shorter events, 31.6 us)
Async XLA Ops:
  3.0 8.5 %collective-permute-start = (bf16[4,48,624]{2,1,0:T(8,128)(2,1)S(1)}, bf16[4,48,624]{2,1,0:T(8,128)(2,1)S(1)}, u32[]{:S(2)}, u32[]{:S(2)}) collective-permute-start(bf16[4,48,624]{2,1,0:T(8,128)(2,1)S(1)} %get-tuple-element.34), channel_id=1, source_target_pairs={{0,8},{1,3},{2,10},{3,5},{4,12},{5,7},{6,14},{7,1},{8,16},{9,11},{... | collective-permute-start | bytes 718856 | tf_op jit(solution)/shard_map/ppermute | solution.py:32
  5.6 8.0 %collective-permute-start.1 = (bf16[4,48,624]{2,1,0:T(8,128)(2,1)S(1)}, bf16[4,48,624]{2,1,0:T(8,128)(2,1)S(1)}, u32[]{:S(2)}, u32[]{:S(2)}) collective-permute-start(bf16[4,48,624]{2,1,0:T(8,128)(2,1)S(1)} %get-tuple-element.35), channel_id=1, source_target_pairs={{0,24},{1,7},{2,26},{3,1},{4,28},{5,3},{6,30},{7,5},{8,0},{9,15},{... | collective-permute-start | bytes 718856 | tf_op jit(solution)/shard_map/ppermute | solution.py:32
  7.8 7.5 %collective-permute-start.2 = (bf16[4,48,624]{2,1,0:T(8,128)(2,1)S(1)}, bf16[4,48,624]{2,1,0:T(8,128)(2,1)S(1)}, u32[]{:S(2)}, u32[]{:S(2)}) collective-permute-start(bf16[4,48,624]{2,1,0:T(8,128)(2,1)S(1)} %get-tuple-element.36), channel_id=1, source_target_pairs={{0,16},{1,5},{2,18},{3,7},{4,20},{5,1},{6,22},{7,3},{8,24},{9,13},... | collective-permute-start | bytes 718856 | tf_op jit(solution)/shard_map/ppermute | solution.py:32
  25.5 31.0 %collective-permute-start.14 = (bf16[16,48,624]{2,1,0:T(8,128)(2,1)S(1)}, bf16[16,48,624]{2,1,0:T(8,128)(2,1)S(1)}, u32[]{:S(2)}, u32[]{:S(2)}) collective-permute-start(bf16[16,48,624]{2,1,0:T(8,128)(2,1)S(1)} %join.9.refs_0_), channel_id=1, source_target_pairs={{0,32},{32,64},{64,96},{96,0},{1,33},{33,65},{65,97},{97,1},{2,34}... | collective-permute-start | bytes 2875400 | tf_op jit(solution)/shard_map/ppermute | solution.py:18
  26.9 35.0 %collective-permute-start.13 = (bf16[16,48,624]{2,1,0:T(8,128)(2,1)S(1)}, bf16[16,48,624]{2,1,0:T(8,128)(2,1)S(1)}, u32[]{:S(2)}, u32[]{:S(2)}) collective-permute-start(bf16[16,48,624]{2,1,0:T(8,128)(2,1)S(1)} %join.9.refs_0_), channel_id=1, source_target_pairs={{0,96},{32,0},{64,32},{96,64},{1,97},{33,1},{65,33},{97,65},{2,98}... | collective-permute-start | bytes 2875400 | tf_op jit(solution)/shard_map/ppermute | solution.py:18
  33.0 19.4 %collective-permute-start.18 = (bf16[96,1280]{1,0:T(8,128)(2,1)S(1)}, bf16[96,1280]{1,0:T(8,128)(2,1)S(1)}, u32[]{:S(2)}, u32[]{:S(2)}) collective-permute-start(bf16[96,1280]{1,0:T(8,128)(2,1)S(1)} %get-tuple-element.49), channel_id=1, source_target_pairs={{0,96},{32,0},{64,32},{96,64},{1,97},{33,1},{65,33},{97,65},{2,98}... | collective-permute-start | bytes 737288 | tf_op jit(solution)/shard_map/ppermute | solution.py:18
  34.6 19.0 %collective-permute-start.19 = (bf16[96,1280]{1,0:T(8,128)(2,1)S(1)}, bf16[96,1280]{1,0:T(8,128)(2,1)S(1)}, u32[]{:S(2)}, u32[]{:S(2)}) collective-permute-start(bf16[96,1280]{1,0:T(8,128)(2,1)S(1)} %get-tuple-element.50), channel_id=1, source_target_pairs={{0,64},{32,96},{64,0},{96,32},{1,65},{33,97},{65,1},{97,33},{2,66}... | collective-permute-start | bytes 737288 | tf_op jit(solution)/shard_map/ppermute | solution.py:18
  35.0 21.0 %collective-permute-start.20 = (bf16[96,1280]{1,0:T(8,128)(2,1)S(1)}, bf16[96,1280]{1,0:T(8,128)(2,1)S(1)}, u32[]{:S(2)}, u32[]{:S(2)}) collective-permute-start(bf16[96,1280]{1,0:T(8,128)(2,1)S(1)} %get-tuple-element.51), channel_id=1, source_target_pairs={{0,32},{32,64},{64,96},{96,0},{1,33},{33,65},{65,97},{97,1},{2,34}... | collective-permute-start | bytes 737288 | tf_op jit(solution)/shard_map/ppermute | solution.py:18
  52.5 10.6 %collective-permute-start.8 = (bf16[96,1280]{1,0:T(8,128)(2,1)S(1)}, bf16[96,1280]{1,0:T(8,128)(2,1)S(1)}, u32[]{:S(2)}, u32[]{:S(2)}) collective-permute-start(bf16[96,1280]{1,0:T(8,128)(2,1)S(1)} %get-tuple-element.47.refs_0_), channel_id=1, source_target_pairs={{0,8},{1,3},{2,10},{3,5},{4,12},{5,7},{6,14},{7,1},{8,16},{9,11},{... | collective-permute-start | bytes 737288 | tf_op jit(solution)/shard_map/ppermute | solution.py:32
  53.6 10.1 %collective-permute-start.9 = (bf16[96,1280]{1,0:T(8,128)(2,1)S(1)}, bf16[96,1280]{1,0:T(8,128)(2,1)S(1)}, u32[]{:S(2)}, u32[]{:S(2)}) collective-permute-start(bf16[96,1280]{1,0:T(8,128)(2,1)S(1)} %get-tuple-element.47.refs_0_), channel_id=1, source_target_pairs={{0,24},{1,7},{2,26},{3,1},{4,28},{5,3},{6,30},{7,5},{8,0},{9,15},{... | collective-permute-start | bytes 737288 | tf_op jit(solution)/shard_map/ppermute | solution.py:32
  56.0 24.8 %collective-permute-start.21 = (bf16[288,1280]{1,0:T(8,128)(2,1)S(1)}, bf16[288,1280]{1,0:T(8,128)(2,1)S(1)}, u32[]{:S(2)}, u32[]{:S(2)}) collective-permute-start(bf16[288,1280]{1,0:T(8,128)(2,1)S(1)} %join.13.refs_0_), channel_id=1, source_target_pairs={{0,8},{1,3},{2,10},{3,5},{4,12},{5,7},{6,14},{7,1},{8,16},{9,11},{... | collective-permute-start | bytes 2211848 | tf_op jit(solution)/shard_map/ppermute | solution.py:32
  56.6 22.8 %collective-permute-start.15 = (bf16[8,48,624]{2,1,0:T(8,128)(2,1)S(1)}, bf16[8,48,624]{2,1,0:T(8,128)(2,1)S(1)}, u32[]{:S(2)}, u32[]{:S(2)}) collective-permute-start(bf16[8,48,624]{2,1,0:T(8,128)(2,1)S(1)} %slice.24), channel_id=1, source_target_pairs={{0,32},{32,64},{64,96},{96,0},{1,33},{33,65},{65,97},{97,1},{2,34}... | collective-permute-start | bytes 1437704 | tf_op jit(solution)/shard_map/ppermute | solution.py:18
  61.9 9.6 %collective-permute-start.10 = (bf16[96,1280]{1,0:T(8,128)(2,1)S(1)}, bf16[96,1280]{1,0:T(8,128)(2,1)S(1)}, u32[]{:S(2)}, u32[]{:S(2)}) collective-permute-start(bf16[96,1280]{1,0:T(8,128)(2,1)S(1)} %get-tuple-element.47.refs_0_), channel_id=1, source_target_pairs={{0,16},{1,5},{2,18},{3,7},{4,20},{5,1},{6,22},{7,3},{8,24},{9,13},... | collective-permute-start | bytes 737288 | tf_op jit(solution)/shard_map/ppermute | solution.py:32
  63.1 16.3 %collective-permute-start.16 = (bf16[8,48,624]{2,1,0:T(8,128)(2,1)S(1)}, bf16[8,48,624]{2,1,0:T(8,128)(2,1)S(1)}, u32[]{:S(2)}, u32[]{:S(2)}) collective-permute-start(bf16[8,48,624]{2,1,0:T(8,128)(2,1)S(1)} %slice.25), channel_id=1, source_target_pairs={{0,96},{32,0},{64,32},{96,64},{1,97},{33,1},{65,33},{97,65},{2,98}... | collective-permute-start | bytes 1437704 | tf_op jit(solution)/shard_map/ppermute | solution.py:18
  63.7 17.1 %collective-permute-start.22 = (bf16[288,1280]{1,0:T(8,128)(2,1)S(1)}, bf16[288,1280]{1,0:T(8,128)(2,1)S(1)}, u32[]{:S(2)}, u32[]{:S(2)}) collective-permute-start(bf16[288,1280]{1,0:T(8,128)(2,1)S(1)} %join.13.refs_0_), channel_id=1, source_target_pairs={{0,24},{1,7},{2,26},{3,1},{4,28},{5,3},{6,30},{7,5},{8,0},{9,15},{... | collective-permute-start | bytes 2211848 | tf_op jit(solution)/shard_map/ppermute | solution.py:32
  71.5 12.1 %collective-permute-start.6 = (bf16[16,48,624]{2,1,0:T(8,128)(2,1)S(1)}, bf16[16,48,624]{2,1,0:T(8,128)(2,1)S(1)}, u32[]{:S(2)}, u32[]{:S(2)}) collective-permute-start(bf16[16,48,624]{2,1,0:T(8,128)(2,1)S(1)} %join.9.refs_0_), channel_id=1, source_target_pairs={{0,1},{1,0},{2,3},{3,2},{4,5},{5,4},{6,7},{7,6},{8,9},{9,8},{10,11... | collective-permute-start | bytes 2875400 | tf_op jit(solution)/shard_map/ppermute | solution.py:22
  79.4 22.4 %collective-permute-start.11 = (bf16[384,1280]{1,0:T(8,128)(2,1)S(1)}, bf16[384,1280]{1,0:T(8,128)(2,1)S(1)}, u32[]{:S(2)}, u32[]{:S(2)}) collective-permute-start(bf16[384,1280]{1,0:T(8,128)(2,1)S(1)} %join.10.refs_0_), channel_id=1, source_target_pairs={{0,2},{1,9},{2,4},{3,11},{4,6},{5,13},{6,0},{7,15},{8,10},{9,17},{... | collective-permute-start | bytes 2949128 | tf_op jit(solution)/shard_map/ppermute | solution.py:32
  79.7 70.9 %collective-permute-start.17 = (bf16[48,48,624]{2,1,0:T(8,128)(2,1)S(1)}, bf16[48,48,624]{2,1,0:T(8,128)(2,1)S(1)}, u32[]{:S(2)}, u32[]{:S(2)}) collective-permute-start(bf16[48,48,624]{2,1,0:T(8,128)(2,1)S(1)} %join.12.refs_0_), channel_id=1, source_target_pairs={{0,1},{1,0},{2,3},{3,2},{4,5},{5,4},{6,7},{7,6},{8,9},{9,8},{10,11... | collective-permute-start | bytes 8626184 | tf_op jit(solution)/shard_map/ppermute | solution.py:22
  80.8 21.0 %collective-permute-start.28 = (bf16[288,1280]{1,0:T(8,128)(2,1)S(1)}, bf16[288,1280]{1,0:T(8,128)(2,1)S(1)}, u32[]{:S(2)}, u32[]{:S(2)}) collective-permute-start(bf16[288,1280]{1,0:T(8,128)(2,1)S(1)} %join.13.refs_0_), channel_id=1, source_target_pairs={{0,2},{1,9},{2,4},{3,11},{4,6},{5,13},{6,0},{7,15},{8,10},{9,17},{... | collective-permute-start | bytes 2211848 | tf_op jit(solution)/shard_map/ppermute | solution.py:32
  80.8 21.5 %collective-permute-start.12 = (bf16[384,1280]{1,0:T(8,128)(2,1)S(1)}, bf16[384,1280]{1,0:T(8,128)(2,1)S(1)}, u32[]{:S(2)}, u32[]{:S(2)}) collective-permute-start(bf16[384,1280]{1,0:T(8,128)(2,1)S(1)} %join.10.refs_0_), channel_id=1, source_target_pairs={{0,6},{1,25},{2,0},{3,27},{4,2},{5,29},{6,4},{7,31},{8,14},{9,1},{... | collective-permute-start | bytes 2949128 | tf_op jit(solution)/shard_map/ppermute | solution.py:32
  83.6 51.1 %collective-permute-start.23 = (bf16[576,1280]{1,0:T(8,128)(2,1)S(1)}, bf16[576,1280]{1,0:T(8,128)(2,1)S(1)}, u32[]{:S(2)}, u32[]{:S(2)}) collective-permute-start(bf16[576,1280]{1,0:T(8,128)(2,1)S(1)} %join.14.refs_1_), channel_id=1, source_target_pairs={{0,2},{1,9},{2,4},{3,11},{4,6},{5,13},{6,0},{7,15},{8,10},{9,17},{... | collective-permute-start | bytes 4423688 | tf_op jit(solution)/shard_map/ppermute | solution.py:32
  101.8 10.6 %collective-permute-start.29 = (bf16[288,1280]{1,0:T(8,128)(2,1)S(1)}, bf16[288,1280]{1,0:T(8,128)(2,1)S(1)}, u32[]{:S(2)}, u32[]{:S(2)}) collective-permute-start(bf16[288,1280]{1,0:T(8,128)(2,1)S(1)} %join.13.refs_0_), channel_id=1, source_target_pairs={{0,6},{1,25},{2,0},{3,27},{4,2},{5,29},{6,4},{7,31},{8,14},{9,1},{... | collective-permute-start | bytes 2211848 | tf_op jit(solution)/shard_map/ppermute | solution.py:32
  101.8 19.7 %collective-permute-start.27 = (bf16[288,1280]{1,0:T(8,128)(2,1)S(1)}, bf16[288,1280]{1,0:T(8,128)(2,1)S(1)}, u32[]{:S(2)}, u32[]{:S(2)}) collective-permute-start(bf16[288,1280]{1,0:T(8,128)(2,1)S(1)} %collective-permute-done.21.refs_0_), channel_id=1, source_target_pairs={{0,8},{1,3},{2,10},{3,5},{4,12},{5,7},{6,14},{7,1},{8,16},{9,11},{... | collective-permute-start | bytes 2211848 | tf_op jit(solution)/shard_map/ppermute | solution.py:32
  102.2 34.5 %collective-permute-start.24 = (bf16[576,1280]{1,0:T(8,128)(2,1)S(1)}, bf16[576,1280]{1,0:T(8,128)(2,1)S(1)}, u32[]{:S(2)}, u32[]{:S(2)}) collective-permute-start(bf16[576,1280]{1,0:T(8,128)(2,1)S(1)} %join.14.refs_1_), channel_id=1, source_target_pairs={{0,6},{1,25},{2,0},{3,27},{4,2},{5,29},{6,4},{7,31},{8,14},{9,1},{... | collective-permute-start | bytes 4423688 | tf_op jit(solution)/shard_map/ppermute | solution.py:32
  112.4 18.4 %collective-permute-start.25 = (bf16[192,1280]{1,0:T(8,128)(2,1)S(1)}, bf16[192,1280]{1,0:T(8,128)(2,1)S(1)}, u32[]{:S(2)}, u32[]{:S(2)}) collective-permute-start(bf16[192,1280]{1,0:T(8,128)(2,1)S(1)} %slice.26), channel_id=1, source_target_pairs={{0,2},{1,9},{2,4},{3,11},{4,6},{5,13},{6,0},{7,15},{8,10},{9,17},{... | collective-permute-start | bytes 1474568 | tf_op jit(solution)/shard_map/ppermute | solution.py:32
  121.5 11.9 %collective-permute-start.26 = (bf16[192,1280]{1,0:T(8,128)(2,1)S(1)}, bf16[192,1280]{1,0:T(8,128)(2,1)S(1)}, u32[]{:S(2)}, u32[]{:S(2)}) collective-permute-start(bf16[192,1280]{1,0:T(8,128)(2,1)S(1)} %slice.27), channel_id=1, source_target_pairs={{0,6},{1,25},{2,0},{3,27},{4,2},{5,29},{6,4},{7,31},{8,14},{9,1},{... | collective-permute-start | bytes 1474568 | tf_op jit(solution)/shard_map/ppermute | solution.py:32
  130.8 11.8 %collective-permute-start.34 = (bf16[288,1280]{1,0:T(8,128)(2,1)S(1)}, bf16[288,1280]{1,0:T(8,128)(2,1)S(1)}, u32[]{:S(2)}, u32[]{:S(2)}) collective-permute-start(bf16[288,1280]{1,0:T(8,128)(2,1)S(1)} %collective-permute-done.28.refs_3_), channel_id=1, source_target_pairs={{0,2},{1,9},{2,4},{3,11},{4,6},{5,13},{6,0},{7,15},{8,10},{9,17},{... | collective-permute-start | bytes 2211848 | tf_op jit(solution)/shard_map/ppermute | solution.py:32
  133.5 10.6 %collective-permute-start.33 = (bf16[288,1280]{1,0:T(8,128)(2,1)S(1)}, bf16[288,1280]{1,0:T(8,128)(2,1)S(1)}, u32[]{:S(2)}, u32[]{:S(2)}) collective-permute-start(bf16[288,1280]{1,0:T(8,128)(2,1)S(1)} %collective-permute-done.27.refs_2_), channel_id=1, source_target_pairs={{0,6},{1,25},{2,0},{3,27},{4,2},{5,29},{6,4},{7,31},{8,14},{9,1},{... | collective-permute-start | bytes 2211848 | tf_op jit(solution)/shard_map/ppermute | solution.py:32
  134.7 15.8 %collective-permute-start.32 = (bf16[288,1280]{1,0:T(8,128)(2,1)S(1)}, bf16[288,1280]{1,0:T(8,128)(2,1)S(1)}, u32[]{:S(2)}, u32[]{:S(2)}) collective-permute-start(bf16[288,1280]{1,0:T(8,128)(2,1)S(1)} %collective-permute-done.27.refs_2_), channel_id=1, source_target_pairs={{0,2},{1,9},{2,4},{3,11},{4,6},{5,13},{6,0},{7,15},{8,10},{9,17},{... | collective-permute-start | bytes 2211848 | tf_op jit(solution)/shard_map/ppermute | solution.py:32
  136.8 23.7 %collective-permute-start.30 = (bf16[144,1280]{1,0:T(8,128)(2,1)S(1)}, bf16[144,1280]{1,0:T(8,128)(2,1)S(1)}, u32[]{:S(2)}, u32[]{:S(2)}) collective-permute-start(bf16[144,1280]{1,0:T(8,128)(2,1)S(1)} %slice.28), channel_id=1, source_target_pairs={{0,2},{1,9},{2,4},{3,11},{4,6},{5,13},{6,0},{7,15},{8,10},{9,17},{... | collective-permute-start | bytes 1105928 | tf_op jit(solution)/shard_map/ppermute | solution.py:32
  142.6 18.9 %collective-permute-start.31 = (bf16[432,1280]{1,0:T(8,128)(2,1)S(1)}, bf16[432,1280]{1,0:T(8,128)(2,1)S(1)}, u32[]{:S(2)}, u32[]{:S(2)}) collective-permute-start(bf16[432,1280]{1,0:T(8,128)(2,1)S(1)} %slice.29), channel_id=1, source_target_pairs={{0,6},{1,25},{2,0},{3,27},{4,2},{5,29},{6,4},{7,31},{8,14},{9,1},{... | collective-permute-start | bytes 3317768 | tf_op jit(solution)/shard_map/ppermute | solution.py:32
  144.1 21.0 %collective-permute-start.35 = (bf16[288,1280]{1,0:T(8,128)(2,1)S(1)}, bf16[288,1280]{1,0:T(8,128)(2,1)S(1)}, u32[]{:S(2)}, u32[]{:S(2)}) collective-permute-start(bf16[288,1280]{1,0:T(8,128)(2,1)S(1)} %collective-permute-done.33.refs_1_), channel_id=1, source_target_pairs={{0,6},{1,25},{2,0},{3,27},{4,2},{5,29},{6,4},{7,31},{8,14},{9,1},{... | collective-permute-start | bytes 2211848 | tf_op jit(solution)/shard_map/ppermute | solution.py:32
  (7 other events, 33.5 us)

commit v2 on v1

--- a/solution.py
+++ b/solution.py
@@ -169,23 +169,20 @@
 
 
 def gathered(own):
-    cut = own.shape[0] // 2
-    before, after = along_plane(own, 0, 1), along_plane(own, 0, -1)
+    before, after, far = (along_plane(own, 0, step) for step in (1, -1, 2))
     near = join([before, after])
-    far = along_plane(before, 0, 1)
     near_sides = along_plane(near, 1, 1), along_plane(near, 1, -1)
     own_sides = along_plane(own, 1, 1), along_plane(own, 1, -1)
     far_sides = along_plane(far, 1, 1), along_plane(far, 1, -1)
     own_opposite = along_plane(own_sides[0], 1, 1)
-    near_opposite = along_plane(near_sides[0][:cut], 1, 1), along_plane(near_sides[1][cut:], 1, -1)
+    near_opposite = along_plane(near_sides[1], 1, -1)
     far_opposite = along_plane(far_sides[1], 1, -1)
 
     first = at(0, 0, -1, 1, 2) + at(-1, 0) + at(1, 0)
-    parts = [(first, 0, join([own, near, far, *own_sides]))]
-    parts += [(at(v, -1, 1), 0, block) for v, block in zip((-1, 1), near_sides)]
-    parts += [(at(-1, 2) + at(1, 2) + at(2, 0), 0, join([*far_sides, own_opposite]))]
-    parts += [(at(2, -1, 1), 0, near_opposite[0]), (at(2, -1, 1), len(OTHERS) // 2, near_opposite[1])]
-    parts += [(at(2, 2), 0, far_opposite)]
+    parts = [(first, join([own, near, far, *own_sides]))]
+    parts += [(at(v, -1, 1), block) for v, block in zip((-1, 1), near_sides)]
+    parts += [(at(-1, 2) + at(1, 2) + at(2, 0), join([*far_sides, own_opposite]))]
+    parts += [(at(2, -1, 1), near_opposite), (at(2, 2), far_opposite)]
     return parts
 
 
@@ -284,13 +281,10 @@
     layout = [[(u, v, dcore, dy) for u, v in offsets for dcore, dy in OWN] for offsets, _ in early]
     weights = arrange(layout, rows, other_rows)
     tile = product(weights[0], early[0][1])
-    layout = []
-    for offsets, skipped, block in parts:
-        blocks = [(u, v, dcore, dy - 1) for u, v in offsets for dcore, dy in OTHERS]
-        layout.append(blocks[skipped : skipped + block.shape[0] // rows.shape[1]])
+    layout = [[(u, v, dcore, dy - 1) for u, v in offsets for dcore, dy in OTHERS] for offsets, _ in parts]
     weights = (*arrange(layout, rest, other_rest), weights[1])
-    blocks = [block for *_, block in parts] + [early[1][1]]
-    for i in (1, 2, len(parts), 0, 4, 5, 3, *range(6, len(parts))):
+    blocks = [block for _, block in parts] + [early[1][1]]
+    for i in (1, 2, len(parts), 0, 3, 4, 5):
         tile = lax.optimization_barrier(tile + product(weights[i], blocks[i]))
 
     kept, sent = halve(tile)

time: 174 us -> 198 us (1.14)
  starting transfers between devices: 49.8 us -> 63.3 us
  waiting for transfers between devices: 101 us -> 111 us
    ppermute x4, starting transfers between devices: 14.6 us -> 27.3 us  [swap_cores(): return lax.ppermute(block, 'core', [(0, 1), (1, 0)])]
    ppermute x26 -> x25, waiting for transfers between devices: 78.5 us -> 84.9 us  [along_plane(): return lax.ppermute(block, ('x', 'z', 'core'), route)]
    ppermute x7, waiting for transfers between devices: 17.5 us -> 23.1 us  [along_y(): lax.ppermute(block, 'y', [(i, (i + step) % SIDE) for i in range(SIDE)])]
    ppermute x26 -> x25, starting transfers between devices: 23.8 us -> 24.1 us  [along_plane(): return lax.ppermute(block, ('x', 'z', 'core'), route)]
    dot_general x9 -> x8, matrix products: 14.3 us -> 14.1 us  [product(): lax.dot_general(weight, block, (((0,), (0,)), ((), ())), preferred_elemen...]
  transfers between devices with their start and end apart: 37 -> 36, of which waited for: 20 -> 18; matrix products, arithmetic and copies ran while one was open for 9% -> 7% of each run, Pallas kernels for 1% -> 1%
where the time goes in v2:
time: 198 us
  waiting for transfers between devices  111 us (56%)
  starting transfers between devices  63.3 us (32%)
  matrix products  14.1 us (7%)
  Pallas kernels  5.25 us (3%)
  local copies, waits for them, and re-layouts  2 us (1%)
    ppermute x25, waiting for transfers between devices, along_plane(): return lax.ppermute(block, ('x', 'z', 'core'), route)  84.9 us
    ppermute x4, starting transfers between devices, swap_cores(): return lax.ppermute(block, 'core', [(0, 1), (1, 0)])  27.3 us
    ppermute x25, starting transfers between devices, along_plane(): return lax.ppermute(block, ('x', 'z', 'core'), route)  24.1 us
    ppermute x7, waiting for transfers between devices, along_y(): lax.ppermute(block, 'y', [(i, (i + step) % SIDE) for i in range(SIDE)])  23.1 us
    dot_general x8, matrix products, product(): lax.dot_general(weight, block, (((0,), (0,)), ((), ())), preferred_elemen...  14.1 us
    ppermute x7, starting transfers between devices, along_y(): lax.ppermute(block, 'y', [(i, (i + step) % SIDE) for i in range(SIDE)])  11.9 us
  transfers between devices with their start and end apart: 36, of which 18 were waited for; matrix products, arithmetic and copies ran while one was open for 7% of the time, Pallas kernels for 1%

profile of v2, /device:TPU:1, one launch (start us, length us, event | category | flops | bytes accessed | tf_op | source)
XLA Modules:
  0.0 197.6 jit_solution(18314778474942984181)
XLA Ops:
  3.0 2.5 %collective-permute-start = (bf16[4,48,624]{2,1,0:T(8,128)(2,1)S(1)}, bf16[4,48,624]{2,1,0:T(8,128)(2,1)S(1)}, u32[]{:S(2)}, u32[]{:S(2)}) collective-permute-start(bf16[4,48,624]{2,1,0:T(8,128)(2,1)S(1)} %get-tuple-element.33), channel_id=1, source_target_pairs={{0,8},{1,3},{2,10},{3,5},{4,12},{5,7},{6,14},{7,1},{8,16},{9,11},{... | collective-permute-start | bytes 718856 | tf_op jit(solution)/shard_map/ppermute | solution.py:32
  5.6 2.2 %collective-permute-start.1 = (bf16[4,48,624]{2,1,0:T(8,128)(2,1)S(1)}, bf16[4,48,624]{2,1,0:T(8,128)(2,1)S(1)}, u32[]{:S(2)}, u32[]{:S(2)}) collective-permute-start(bf16[4,48,624]{2,1,0:T(8,128)(2,1)S(1)} %get-tuple-element.34), channel_id=1, source_target_pairs={{0,24},{1,7},{2,26},{3,1},{4,28},{5,3},{6,30},{7,5},{8,0},{9,15},{... | collective-permute-start | bytes 718856 | tf_op jit(solution)/shard_map/ppermute | solution.py:32
  9.0 2.5 %collective-permute-done.refs_1_ = bf16[4,48,624]{2,1,0:T(8,128)(2,1)S(1)} collective-permute-done((bf16[4,48,624]{2,1,0:T(8,128)(2,1)S(1)}, bf16[4,48,624]{2,1,0:T(8,128)(2,1)S(1)}, u32[]{:S(2)}, u32[]{:S(2)}) %collective-permute-start) | collective-permute-done | bytes 239648 | tf_op jit(solution)/shard_map/ppermute | solution.py:32
  11.5 2.0 %collective-permute-done.1.refs_2_ = bf16[4,48,624]{2,1,0:T(8,128)(2,1)S(1)} collective-permute-done((bf16[4,48,624]{2,1,0:T(8,128)(2,1)S(1)}, bf16[4,48,624]{2,1,0:T(8,128)(2,1)S(1)}, u32[]{:S(2)}, u32[]{:S(2)}) %collective-permute-start.1) | collective-permute-done | bytes 239648 | tf_op jit(solution)/shard_map/ppermute | solution.py:32
  13.5 1.7 collective-permute-done.2.refs_3_
  16.4 1.6 collective-permute-start.4
  19.4 2.2 %collective-permute-start.7 = (bf16[4,48,1280]{2,1,0:T(8,128)(2,1)S(1)}, bf16[4,48,1280]{2,1,0:T(8,128)(2,1)S(1)}, u32[]{:S(2)}, u32[]{:S(2)}) collective-permute-start(bf16[4,48,1280]{2,1,0:T(8,128)(2,1)S(1)} %get-tuple-element.45), channel_id=1, source_target_pairs={{0,1},{1,0},{2,3},{3,2},{4,5},{5,4},{6,7},{7,6},{8,9},{9,8},{10,11... | collective-permute-start | bytes 1474568 | tf_op jit(solution)/shard_map/ppermute | solution.py:22
  21.9 1.9 collective-permute-done.4.refs_2_
  30.3 3.8 %collective-permute-start.6 = (bf16[16,48,624]{2,1,0:T(8,128)(2,1)S(1)}, bf16[16,48,624]{2,1,0:T(8,128)(2,1)S(1)}, u32[]{:S(2)}, u32[]{:S(2)}) collective-permute-start(bf16[16,48,624]{2,1,0:T(8,128)(2,1)S(1)} %join.9.refs_0_), channel_id=1, source_target_pairs={{0,1},{1,0},{2,3},{3,2},{4,5},{5,4},{6,7},{7,6},{8,9},{9,8},{10,11... | collective-permute-start | bytes 2875400 | tf_op jit(solution)/shard_map/ppermute | solution.py:22
  34.1 18.4 %collective-permute-done.18.refs_0_ = bf16[96,1280]{1,0:T(8,128)(2,1)S(1)} collective-permute-done((bf16[96,1280]{1,0:T(8,128)(2,1)S(1)}, bf16[96,1280]{1,0:T(8,128)(2,1)S(1)}, u32[]{:S(2)}, u32[]{:S(2)}) %collective-permute-start.18) | collective-permute-done | bytes 245792 | tf_op jit(solution)/shard_map/ppermute | solution.py:18
  54.4 2.1 %collective-permute-start.9 = (bf16[96,1280]{1,0:T(8,128)(2,1)S(1)}, bf16[96,1280]{1,0:T(8,128)(2,1)S(1)}, u32[]{:S(2)}, u32[]{:S(2)}) collective-permute-start(bf16[96,1280]{1,0:T(8,128)(2,1)S(1)} %get-tuple-element.46.refs_0_), channel_id=1, source_target_pairs={{0,24},{1,7},{2,26},{3,1},{4,28},{5,3},{6,30},{7,5},{8,0},{9,15},{... | collective-permute-start | bytes 737288 | tf_op jit(solution)/shard_map/ppermute | solution.py:32
  56.5 2.9 %collective-permute-done.20.refs_2_ = bf16[96,1280]{1,0:T(8,128)(2,1)S(1)} collective-permute-done((bf16[96,1280]{1,0:T(8,128)(2,1)S(1)}, bf16[96,1280]{1,0:T(8,128)(2,1)S(1)}, u32[]{:S(2)}, u32[]{:S(2)}) %collective-permute-start.20) | collective-permute-done | bytes 245792 | tf_op jit(solution)/shard_map/ppermute | solution.py:18
  59.4 2.9 %collective-permute-start.15 = (bf16[8,48,624]{2,1,0:T(8,128)(2,1)S(1)}, bf16[8,48,624]{2,1,0:T(8,128)(2,1)S(1)}, u32[]{:S(2)}, u32[]{:S(2)}) collective-permute-start(bf16[8,48,624]{2,1,0:T(8,128)(2,1)S(1)} %slice.16), channel_id=1, source_target_pairs={{0,32},{32,64},{64,96},{96,0},{1,33},{33,65},{65,97},{97,1},{2,34}... | collective-permute-start | bytes 1437704 | tf_op jit(solution)/shard_map/ppermute | solution.py:18
  63.0 3.1 %collective-permute-start.16 = (bf16[8,48,624]{2,1,0:T(8,128)(2,1)S(1)}, bf16[8,48,624]{2,1,0:T(8,128)(2,1)S(1)}, u32[]{:S(2)}, u32[]{:S(2)}) collective-permute-start(bf16[8,48,624]{2,1,0:T(8,128)(2,1)S(1)} %slice.17), channel_id=1, source_target_pairs={{0,96},{32,0},{64,32},{96,64},{1,97},{33,1},{65,33},{97,65},{2,98}... | collective-permute-start | bytes 1437704 | tf_op jit(solution)/shard_map/ppermute | solution.py:18
  66.2 2.6 %collective-permute-done.10.refs_3_ = bf16[96,1280]{1,0:T(8,128)(2,1)S(1)} collective-permute-done((bf16[96,1280]{1,0:T(8,128)(2,1)S(1)}, bf16[96,1280]{1,0:T(8,128)(2,1)S(1)}, u32[]{:S(2)}, u32[]{:S(2)}) %collective-permute-start.10) | collective-permute-done | bytes 245792 | tf_op jit(solution)/shard_map/ppermute | solution.py:32
  69.8 1.7 collective-permute-done.15.refs_1_
  73.0 11.0 %collective-permute-start.17 = (bf16[48,48,624]{2,1,0:T(8,128)(2,1)S(1)}, bf16[48,48,624]{2,1,0:T(8,128)(2,1)S(1)}, u32[]{:S(2)}, u32[]{:S(2)}) collective-permute-start(bf16[48,48,624]{2,1,0:T(8,128)(2,1)S(1)} %join.12.refs_0_), channel_id=1, source_target_pairs={{0,1},{1,0},{2,3},{3,2},{4,5},{5,4},{6,7},{7,6},{8,9},{9,8},{10,11... | collective-permute-start | bytes 8626184 | tf_op jit(solution)/shard_map/ppermute | solution.py:22
  84.1 1.8 collective-permute-done.21.refs_0_
  86.2 2.4 %collective-permute-start.12 = (bf16[384,1280]{1,0:T(8,128)(2,1)S(1)}, bf16[384,1280]{1,0:T(8,128)(2,1)S(1)}, u32[]{:S(2)}, u32[]{:S(2)}) collective-permute-start(bf16[384,1280]{1,0:T(8,128)(2,1)S(1)} %join.10.refs_0_), channel_id=1, source_target_pairs={{0,6},{1,25},{2,0},{3,27},{4,2},{5,29},{6,4},{7,31},{8,14},{9,1},{... | collective-permute-start | bytes 2949128 | tf_op jit(solution)/shard_map/ppermute | solution.py:32
  89.1 3.3 %collective-permute-done.28.refs_3_ = bf16[288,1280]{1,0:T(8,128)(2,1)S(1)} collective-permute-done((bf16[288,1280]{1,0:T(8,128)(2,1)S(1)}, bf16[288,1280]{1,0:T(8,128)(2,1)S(1)}, u32[]{:S(2)}, u32[]{:S(2)}) %collective-permute-start.28) | collective-permute-done | bytes 737312 | tf_op jit(solution)/shard_map/ppermute | solution.py:32
  92.5 26.6 %collective-permute-done.29.refs_4_ = bf16[288,1280]{1,0:T(8,128)(2,1)S(1)} collective-permute-done((bf16[288,1280]{1,0:T(8,128)(2,1)S(1)}, bf16[288,1280]{1,0:T(8,128)(2,1)S(1)}, u32[]{:S(2)}, u32[]{:S(2)}) %collective-permute-start.29) | collective-permute-done | bytes 737312 | tf_op jit(solution)/shard_map/ppermute | solution.py:32
  120.7 2.1 %collective-permute-start.24 = (bf16[576,1280]{1,0:T(8,128)(2,1)S(1)}, bf16[576,1280]{1,0:T(8,128)(2,1)S(1)}, u32[]{:S(2)}, u32[]{:S(2)}) collective-permute-start(bf16[576,1280]{1,0:T(8,128)(2,1)S(1)} %join.14.refs_1_), channel_id=1, source_target_pairs={{0,6},{1,25},{2,0},{3,27},{4,2},{5,29},{6,4},{7,31},{8,14},{9,1},{... | collective-permute-start | bytes 4423688 | tf_op jit(solution)/shard_map/ppermute | solution.py:32
  122.9 6.8 %collective-permute-done.31.refs_1_ = bf16[288,1280]{1,0:T(8,128)(2,1)S(1)} collective-permute-done((bf16[288,1280]{1,0:T(8,128)(2,1)S(1)}, bf16[288,1280]{1,0:T(8,128)(2,1)S(1)}, u32[]{:S(2)}, u32[]{:S(2)}) %collective-permute-start.31) | collective-permute-done | bytes 737312 | tf_op jit(solution)/shard_map/ppermute | solution.py:32
  133.2 19.4 %collective-permute-done.25.refs_0_ = bf16[192,1280]{1,0:T(8,128)(2,1)S(1)} collective-permute-done((bf16[192,1280]{1,0:T(8,128)(2,1)S(1)}, bf16[192,1280]{1,0:T(8,128)(2,1)S(1)}, u32[]{:S(2)}, u32[]{:S(2)}) %collective-permute-start.25) | collective-permute-done | bytes 491552 | tf_op jit(solution)/shard_map/ppermute | solution.py:32
  156.2 2.4 %convolution_add_fusion.2 = f32[624,1280]{1,0:T(8,128)S(1)} fusion(f32[624,1280]{1,0:T(8,128)S(1)} %fusion, bf16[1152,624]{1,0:T(8,128)(2,1)S(1)} %get-tuple-element.40, bf16[1152,1280]{1,0:T(8,128)(2,1)S(1)} %join.11), kind=kOutput, calls=%fused_computation.2 | convolution fusion | flops 1841049600 | bytes 10776576 | tf_op jit(solution)/shard_map/dot_general | solution.py:279
  160.8 3.2 %fusion.3 = f32[624,1280]{1,0:T(8,128)S(1)} fusion(bf16[1728,624]{1,0:T(8,128)(2,1)S(1)} %get-tuple-element.53, bf16[1728,1280]{1,0:T(8,128)(2,1)S(1)} %join.16), kind=kOutput, calls=%fused_computation.6 | convolution fusion | flops 2760376320 | bytes 9775104 | tf_op jit(solution)/shard_map/dot_general | solution.py:279
  164.4 1.9 convolution_add_fusion.1
  166.3 12.8 %collective-permute-done.33 = bf16[576,1280]{1,0:T(8,128)(2,1)S(1)} collective-permute-done((bf16[576,1280]{1,0:T(8,128)(2,1)S(1)}, bf16[576,1280]{1,0:T(8,128)(2,1)S(1)}, u32[]{:S(2)}, u32[]{:S(2)}) %collective-permute-start.33) | collective-permute-done | bytes 1474592 | tf_op jit(solution)/shard_map/ppermute | solution.py:32
  179.0 1.7 fusion.4
  182.4 10.2 %collective-permute-start.35 = (f32[312,1280]{1,0:T(8,128)S(1)}, f32[312,1280]{1,0:T(8,128)S(1)}, u32[]{:S(2)}, u32[]{:S(2)}) collective-permute-start(f32[312,1280]{1,0:T(8,128)S(1)} %get-tuple-element.58), channel_id=1, source_target_pairs={{0,1},{1,0},{2,3},{3,2},{4,5},{5,4},{6,7},{7,6},{8,9},{9,8},{10,11... | collective-permute-start | bytes 4792328 | tf_op jit(solution)/shard_map/ppermute | solution.py:22
  192.6 3.1 %collective-permute-done.35.got_ref = f32[312,1280]{1,0:T(8,128)S(1)} collective-permute-done((f32[312,1280]{1,0:T(8,128)S(1)}, f32[312,1280]{1,0:T(8,128)S(1)}, u32[]{:S(2)}, u32[]{:S(2)}) %collective-permute-start.35) | collective-permute-done | bytes 1597472 | tf_op jit(solution)/shard_map/ppermute | solution.py:22
  195.7 1.9 assemble.1
  (76 shorter events, 32.5 us)
Async XLA Ops:
  3.0 8.5 %collective-permute-start = (bf16[4,48,624]{2,1,0:T(8,128)(2,1)S(1)}, bf16[4,48,624]{2,1,0:T(8,128)(2,1)S(1)}, u32[]{:S(2)}, u32[]{:S(2)}) collective-permute-start(bf16[4,48,624]{2,1,0:T(8,128)(2,1)S(1)} %get-tuple-element.33), channel_id=1, source_target_pairs={{0,8},{1,3},{2,10},{3,5},{4,12},{5,7},{6,14},{7,1},{8,16},{9,11},{... | collective-permute-start | bytes 718856 | tf_op jit(solution)/shard_map/ppermute | solution.py:32
  5.6 8.0 %collective-permute-start.1 = (bf16[4,48,624]{2,1,0:T(8,128)(2,1)S(1)}, bf16[4,48,624]{2,1,0:T(8,128)(2,1)S(1)}, u32[]{:S(2)}, u32[]{:S(2)}) collective-permute-start(bf16[4,48,624]{2,1,0:T(8,128)(2,1)S(1)} %get-tuple-element.34), channel_id=1, source_target_pairs={{0,24},{1,7},{2,26},{3,1},{4,28},{5,3},{6,30},{7,5},{8,0},{9,15},{... | collective-permute-start | bytes 718856 | tf_op jit(solution)/shard_map/ppermute | solution.py:32
  7.8 7.5 %collective-permute-start.2 = (bf16[4,48,624]{2,1,0:T(8,128)(2,1)S(1)}, bf16[4,48,624]{2,1,0:T(8,128)(2,1)S(1)}, u32[]{:S(2)}, u32[]{:S(2)}) collective-permute-start(bf16[4,48,624]{2,1,0:T(8,128)(2,1)S(1)} %get-tuple-element.35), channel_id=1, source_target_pairs={{0,16},{1,5},{2,18},{3,7},{4,20},{5,1},{6,22},{7,3},{8,24},{9,13},... | collective-permute-start | bytes 718856 | tf_op jit(solution)/shard_map/ppermute | solution.py:32
  16.4 7.4 %collective-permute-start.4 = (bf16[4,48,624]{2,1,0:T(8,128)(2,1)S(1)}, bf16[4,48,624]{2,1,0:T(8,128)(2,1)S(1)}, u32[]{:S(2)}, u32[]{:S(2)}) collective-permute-start(bf16[4,48,624]{2,1,0:T(8,128)(2,1)S(1)} %get-tuple-element.38), channel_id=1, source_target_pairs={{0,6},{1,25},{2,0},{3,27},{4,2},{5,29},{6,4},{7,31},{8,14},{9,1},{... | collective-permute-start | bytes 718856 | tf_op jit(solution)/shard_map/ppermute | solution.py:32
  19.4 8.9 %collective-permute-start.7 = (bf16[4,48,1280]{2,1,0:T(8,128)(2,1)S(1)}, bf16[4,48,1280]{2,1,0:T(8,128)(2,1)S(1)}, u32[]{:S(2)}, u32[]{:S(2)}) collective-permute-start(bf16[4,48,1280]{2,1,0:T(8,128)(2,1)S(1)} %get-tuple-element.45), channel_id=1, source_target_pairs={{0,1},{1,0},{2,3},{3,2},{4,5},{5,4},{6,7},{7,6},{8,9},{9,8},{10,11... | collective-permute-start | bytes 1474568 | tf_op jit(solution)/shard_map/ppermute | solution.py:22
  25.5 28.9 %collective-permute-start.14 = (bf16[16,48,624]{2,1,0:T(8,128)(2,1)S(1)}, bf16[16,48,624]{2,1,0:T(8,128)(2,1)S(1)}, u32[]{:S(2)}, u32[]{:S(2)}) collective-permute-start(bf16[16,48,624]{2,1,0:T(8,128)(2,1)S(1)} %join.9.refs_0_), channel_id=1, source_target_pairs={{0,32},{32,64},{64,96},{96,0},{1,33},{33,65},{65,97},{97,1},{2,34}... | collective-permute-start | bytes 2875400 | tf_op jit(solution)/shard_map/ppermute | solution.py:18
  26.9 35.4 %collective-permute-start.13 = (bf16[16,48,624]{2,1,0:T(8,128)(2,1)S(1)}, bf16[16,48,624]{2,1,0:T(8,128)(2,1)S(1)}, u32[]{:S(2)}, u32[]{:S(2)}) collective-permute-start(bf16[16,48,624]{2,1,0:T(8,128)(2,1)S(1)} %join.9.refs_0_), channel_id=1, source_target_pairs={{0,96},{32,0},{64,32},{96,64},{1,97},{33,1},{65,33},{97,65},{2,98}... | collective-permute-start | bytes 2875400 | tf_op jit(solution)/shard_map/ppermute | solution.py:18
  28.4 24.0 %collective-permute-start.18 = (bf16[96,1280]{1,0:T(8,128)(2,1)S(1)}, bf16[96,1280]{1,0:T(8,128)(2,1)S(1)}, u32[]{:S(2)}, u32[]{:S(2)}) collective-permute-start(bf16[96,1280]{1,0:T(8,128)(2,1)S(1)} %get-tuple-element.48), channel_id=1, source_target_pairs={{0,96},{32,0},{64,32},{96,64},{1,97},{33,1},{65,33},{97,65},{2,98}... | collective-permute-start | bytes 737288 | tf_op jit(solution)/shard_map/ppermute | solution.py:18
  29.9 23.9 %collective-permute-start.19 = (bf16[96,1280]{1,0:T(8,128)(2,1)S(1)}, bf16[96,1280]{1,0:T(8,128)(2,1)S(1)}, u32[]{:S(2)}, u32[]{:S(2)}) collective-permute-start(bf16[96,1280]{1,0:T(8,128)(2,1)S(1)} %get-tuple-element.49), channel_id=1, source_target_pairs={{0,64},{32,96},{64,0},{96,32},{1,65},{33,97},{65,1},{97,33},{2,66}... | collective-permute-start | bytes 737288 | tf_op jit(solution)/shard_map/ppermute | solution.py:18
  30.3 42.8 %collective-permute-start.6 = (bf16[16,48,624]{2,1,0:T(8,128)(2,1)S(1)}, bf16[16,48,624]{2,1,0:T(8,128)(2,1)S(1)}, u32[]{:S(2)}, u32[]{:S(2)}) collective-permute-start(bf16[16,48,624]{2,1,0:T(8,128)(2,1)S(1)} %join.9.refs_0_), channel_id=1, source_target_pairs={{0,1},{1,0},{2,3},{3,2},{4,5},{5,4},{6,7},{7,6},{8,9},{9,8},{10,11... | collective-permute-start | bytes 2875400 | tf_op jit(solution)/shard_map/ppermute | solution.py:22
  53.8 9.2 %collective-permute-start.8 = (bf16[96,1280]{1,0:T(8,128)(2,1)S(1)}, bf16[96,1280]{1,0:T(8,128)(2,1)S(1)}, u32[]{:S(2)}, u32[]{:S(2)}) collective-permute-start(bf16[96,1280]{1,0:T(8,128)(2,1)S(1)} %get-tuple-element.46.refs_0_), channel_id=1, source_target_pairs={{0,8},{1,3},{2,10},{3,5},{4,12},{5,7},{6,14},{7,1},{8,16},{9,11},{... | collective-permute-start | bytes 737288 | tf_op jit(solution)/shard_map/ppermute | solution.py:32
  54.4 11.8 %collective-permute-start.9 = (bf16[96,1280]{1,0:T(8,128)(2,1)S(1)}, bf16[96,1280]{1,0:T(8,128)(2,1)S(1)}, u32[]{:S(2)}, u32[]{:S(2)}) collective-permute-start(bf16[96,1280]{1,0:T(8,128)(2,1)S(1)} %get-tuple-element.46.refs_0_), channel_id=1, source_target_pairs={{0,24},{1,7},{2,26},{3,1},{4,28},{5,3},{6,30},{7,5},{8,0},{9,15},{... | collective-permute-start | bytes 737288 | tf_op jit(solution)/shard_map/ppermute | solution.py:32
  59.4 12.1 %collective-permute-start.15 = (bf16[8,48,624]{2,1,0:T(8,128)(2,1)S(1)}, bf16[8,48,624]{2,1,0:T(8,128)(2,1)S(1)}, u32[]{:S(2)}, u32[]{:S(2)}) collective-permute-start(bf16[8,48,624]{2,1,0:T(8,128)(2,1)S(1)} %slice.16), channel_id=1, source_target_pairs={{0,32},{32,64},{64,96},{96,0},{1,33},{33,65},{65,97},{97,1},{2,34}... | collective-permute-start | bytes 1437704 | tf_op jit(solution)/shard_map/ppermute | solution.py:18
  63.0 9.2 %collective-permute-start.16 = (bf16[8,48,624]{2,1,0:T(8,128)(2,1)S(1)}, bf16[8,48,624]{2,1,0:T(8,128)(2,1)S(1)}, u32[]{:S(2)}, u32[]{:S(2)}) collective-permute-start(bf16[8,48,624]{2,1,0:T(8,128)(2,1)S(1)} %slice.17), channel_id=1, source_target_pairs={{0,96},{32,0},{64,32},{96,64},{1,97},{33,1},{65,33},{97,65},{2,98}... | collective-permute-start | bytes 1437704 | tf_op jit(solution)/shard_map/ppermute | solution.py:18
  66.2 19.8 %collective-permute-start.21 = (bf16[288,1280]{1,0:T(8,128)(2,1)S(1)}, bf16[288,1280]{1,0:T(8,128)(2,1)S(1)}, u32[]{:S(2)}, u32[]{:S(2)}) collective-permute-start(bf16[288,1280]{1,0:T(8,128)(2,1)S(1)} %join.13.refs_0_), channel_id=1, source_target_pairs={{0,8},{1,3},{2,10},{3,5},{4,12},{5,7},{6,14},{7,1},{8,16},{9,11},{... | collective-permute-start | bytes 2211848 | tf_op jit(solution)/shard_map/ppermute | solution.py:32
  68.8 17.4 %collective-permute-start.22 = (bf16[288,1280]{1,0:T(8,128)(2,1)S(1)}, bf16[288,1280]{1,0:T(8,128)(2,1)S(1)}, u32[]{:S(2)}, u32[]{:S(2)}) collective-permute-start(bf16[288,1280]{1,0:T(8,128)(2,1)S(1)} %join.13.refs_0_), channel_id=1, source_target_pairs={{0,24},{1,7},{2,26},{3,1},{4,28},{5,3},{6,30},{7,5},{8,0},{9,15},{... | collective-permute-start | bytes 2211848 | tf_op jit(solution)/shard_map/ppermute | solution.py:32
  71.5 17.1 %collective-permute-start.27 = (bf16[288,1280]{1,0:T(8,128)(2,1)S(1)}, bf16[288,1280]{1,0:T(8,128)(2,1)S(1)}, u32[]{:S(2)}, u32[]{:S(2)}) collective-permute-start(bf16[288,1280]{1,0:T(8,128)(2,1)S(1)} %join.13.refs_0_), channel_id=1, source_target_pairs={{0,16},{1,5},{2,18},{3,7},{4,20},{5,1},{6,22},{7,3},{8,24},{9,13},... | collective-permute-start | bytes 2211848 | tf_op jit(solution)/shard_map/ppermute | solution.py:32
  72.2 20.3 %collective-permute-start.28 = (bf16[288,1280]{1,0:T(8,128)(2,1)S(1)}, bf16[288,1280]{1,0:T(8,128)(2,1)S(1)}, u32[]{:S(2)}, u32[]{:S(2)}) collective-permute-start(bf16[288,1280]{1,0:T(8,128)(2,1)S(1)} %join.13.refs_0_), channel_id=1, source_target_pairs={{0,2},{1,9},{2,4},{3,11},{4,6},{5,13},{6,0},{7,15},{8,10},{9,17},{... | collective-permute-start | bytes 2211848 | tf_op jit(solution)/shard_map/ppermute | solution.py:32
  73.0 81.2 %collective-permute-start.17 = (bf16[48,48,624]{2,1,0:T(8,128)(2,1)S(1)}, bf16[48,48,624]{2,1,0:T(8,128)(2,1)S(1)}, u32[]{:S(2)}, u32[]{:S(2)}) collective-permute-start(bf16[48,48,624]{2,1,0:T(8,128)(2,1)S(1)} %join.12.refs_0_), channel_id=1, source_target_pairs={{0,1},{1,0},{2,3},{3,2},{4,5},{5,4},{6,7},{7,6},{8,9},{9,8},{10,11... | collective-permute-start | bytes 8626184 | tf_op jit(solution)/shard_map/ppermute | solution.py:22
  86.0 33.8 %collective-permute-start.11 = (bf16[384,1280]{1,0:T(8,128)(2,1)S(1)}, bf16[384,1280]{1,0:T(8,128)(2,1)S(1)}, u32[]{:S(2)}, u32[]{:S(2)}) collective-permute-start(bf16[384,1280]{1,0:T(8,128)(2,1)S(1)} %join.10.refs_0_), channel_id=1, source_target_pairs={{0,2},{1,9},{2,4},{3,11},{4,6},{5,13},{6,0},{7,15},{8,10},{9,17},{... | collective-permute-start | bytes 2949128 | tf_op jit(solution)/shard_map/ppermute | solution.py:32
  86.2 34.4 %collective-permute-start.12 = (bf16[384,1280]{1,0:T(8,128)(2,1)S(1)}, bf16[384,1280]{1,0:T(8,128)(2,1)S(1)}, u32[]{:S(2)}, u32[]{:S(2)}) collective-permute-start(bf16[384,1280]{1,0:T(8,128)(2,1)S(1)} %join.10.refs_0_), channel_id=1, source_target_pairs={{0,6},{1,25},{2,0},{3,27},{4,2},{5,29},{6,4},{7,31},{8,14},{9,1},{... | collective-permute-start | bytes 2949128 | tf_op jit(solution)/shard_map/ppermute | solution.py:32
  88.6 30.5 %collective-permute-start.29 = (bf16[288,1280]{1,0:T(8,128)(2,1)S(1)}, bf16[288,1280]{1,0:T(8,128)(2,1)S(1)}, u32[]{:S(2)}, u32[]{:S(2)}) collective-permute-start(bf16[288,1280]{1,0:T(8,128)(2,1)S(1)} %join.13.refs_0_), channel_id=1, source_target_pairs={{0,6},{1,25},{2,0},{3,27},{4,2},{5,29},{6,4},{7,31},{8,14},{9,1},{... | collective-permute-start | bytes 2211848 | tf_op jit(solution)/shard_map/ppermute | solution.py:32
  92.5 30.3 %collective-permute-start.30 = (bf16[288,1280]{1,0:T(8,128)(2,1)S(1)}, bf16[288,1280]{1,0:T(8,128)(2,1)S(1)}, u32[]{:S(2)}, u32[]{:S(2)}) collective-permute-start(bf16[288,1280]{1,0:T(8,128)(2,1)S(1)} %collective-permute-done.27.refs_2_), channel_id=1, source_target_pairs={{0,2},{1,9},{2,4},{3,11},{4,6},{5,13},{6,0},{7,15},{8,10},{9,17},{... | collective-permute-start | bytes 2211848 | tf_op jit(solution)/shard_map/ppermute | solution.py:32
  119.1 10.6 %collective-permute-start.31 = (bf16[288,1280]{1,0:T(8,128)(2,1)S(1)}, bf16[288,1280]{1,0:T(8,128)(2,1)S(1)}, u32[]{:S(2)}, u32[]{:S(2)}) collective-permute-start(bf16[288,1280]{1,0:T(8,128)(2,1)S(1)} %collective-permute-done.27.refs_2_), channel_id=1, source_target_pairs={{0,6},{1,25},{2,0},{3,27},{4,2},{5,29},{6,4},{7,31},{8,14},{9,1},{... | collective-permute-start | bytes 2211848 | tf_op jit(solution)/shard_map/ppermute | solution.py:32
  119.7 11.5 %collective-permute-start.32 = (bf16[288,1280]{1,0:T(8,128)(2,1)S(1)}, bf16[288,1280]{1,0:T(8,128)(2,1)S(1)}, u32[]{:S(2)}, u32[]{:S(2)}) collective-permute-start(bf16[288,1280]{1,0:T(8,128)(2,1)S(1)} %collective-permute-done.28.refs_3_), channel_id=1, source_target_pairs={{0,2},{1,9},{2,4},{3,11},{4,6},{5,13},{6,0},{7,15},{8,10},{9,17},{... | collective-permute-start | bytes 2211848 | tf_op jit(solution)/shard_map/ppermute | solution.py:32
  120.7 33.1 %collective-permute-start.24 = (bf16[576,1280]{1,0:T(8,128)(2,1)S(1)}, bf16[576,1280]{1,0:T(8,128)(2,1)S(1)}, u32[]{:S(2)}, u32[]{:S(2)}) collective-permute-start(bf16[576,1280]{1,0:T(8,128)(2,1)S(1)} %join.14.refs_1_), channel_id=1, source_target_pairs={{0,6},{1,25},{2,0},{3,27},{4,2},{5,29},{6,4},{7,31},{8,14},{9,1},{... | collective-permute-start | bytes 4423688 | tf_op jit(solution)/shard_map/ppermute | solution.py:32
  122.8 31.9 %collective-permute-start.23 = (bf16[576,1280]{1,0:T(8,128)(2,1)S(1)}, bf16[576,1280]{1,0:T(8,128)(2,1)S(1)}, u32[]{:S(2)}, u32[]{:S(2)}) collective-permute-start(bf16[576,1280]{1,0:T(8,128)(2,1)S(1)} %join.14.refs_1_), channel_id=1, source_target_pairs={{0,2},{1,9},{2,4},{3,11},{4,6},{5,13},{6,0},{7,15},{8,10},{9,17},{... | collective-permute-start | bytes 4423688 | tf_op jit(solution)/shard_map/ppermute | solution.py:32
  129.7 22.9 %collective-permute-start.25 = (bf16[192,1280]{1,0:T(8,128)(2,1)S(1)}, bf16[192,1280]{1,0:T(8,128)(2,1)S(1)}, u32[]{:S(2)}, u32[]{:S(2)}) collective-permute-start(bf16[192,1280]{1,0:T(8,128)(2,1)S(1)} %slice.18), channel_id=1, source_target_pairs={{0,2},{1,9},{2,4},{3,11},{4,6},{5,13},{6,0},{7,15},{8,10},{9,17},{... | collective-permute-start | bytes 1474568 | tf_op jit(solution)/shard_map/ppermute | solution.py:32
  131.3 21.4 %collective-permute-start.26 = (bf16[192,1280]{1,0:T(8,128)(2,1)S(1)}, bf16[192,1280]{1,0:T(8,128)(2,1)S(1)}, u32[]{:S(2)}, u32[]{:S(2)}) collective-permute-start(bf16[192,1280]{1,0:T(8,128)(2,1)S(1)} %slice.19), channel_id=1, source_target_pairs={{0,6},{1,25},{2,0},{3,27},{4,2},{5,29},{6,4},{7,31},{8,14},{9,1},{... | collective-permute-start | bytes 1474568 | tf_op jit(solution)/shard_map/ppermute | solution.py:32
  152.6 28.6 %collective-permute-start.34 = (bf16[288,1280]{1,0:T(8,128)(2,1)S(1)}, bf16[288,1280]{1,0:T(8,128)(2,1)S(1)}, u32[]{:S(2)}, u32[]{:S(2)}) collective-permute-start(bf16[288,1280]{1,0:T(8,128)(2,1)S(1)} %collective-permute-done.31.refs_1_), channel_id=1, source_target_pairs={{0,6},{1,25},{2,0},{3,27},{4,2},{5,29},{6,4},{7,31},{8,14},{9,1},{... | collective-permute-start | bytes 2211848 | tf_op jit(solution)/shard_map/ppermute | solution.py:32
  153.7 25.3 %collective-permute-start.33 = (bf16[576,1280]{1,0:T(8,128)(2,1)S(1)}, bf16[576,1280]{1,0:T(8,128)(2,1)S(1)}, u32[]{:S(2)}, u32[]{:S(2)}) collective-permute-start(bf16[576,1280]{1,0:T(8,128)(2,1)S(1)} %collective-permute-done.24), channel_id=1, source_target_pairs={{0,6},{1,25},{2,0},{3,27},{4,2},{5,29},{6,4},{7,31},{8,14},{9,1},{... | collective-permute-start | bytes 4423688 | tf_op jit(solution)/shard_map/ppermute | solution.py:32
  182.4 13.2 %collective-permute-start.35 = (f32[312,1280]{1,0:T(8,128)S(1)}, f32[312,1280]{1,0:T(8,128)S(1)}, u32[]{:S(2)}, u32[]{:S(2)}) collective-permute-start(f32[312,1280]{1,0:T(8,128)S(1)} %get-tuple-element.58), channel_id=1, source_target_pairs={{0,1},{1,0},{2,3},{3,2},{4,5},{5,4},{6,7},{7,6},{8,9},{9,8},{10,11... | collective-permute-start | bytes 4792328 | tf_op jit(solution)/shard_map/ppermute | solution.py:22
  (6 other events, 29.3 us)

commit v3 on v1

--- a/solution.py
+++ b/solution.py
@@ -51,6 +51,13 @@
         cost_estimate=pl.CostEstimate(flops=0, bytes_accessed=2 * size, transcendentals=0),
         name="join",
     )(*blocks)
+
+
+def place_on_line(out_refs, u, i, block):
+    if u == 2:
+        out_refs[2 if i < SIDE // 2 else 1][SIDE + i % (SIDE // 2)] = block
+    else:
+        out_refs[OFFSETS.index(u)][i] = block
 
 
 def pack_kernel(count_ref, terms_ref, *refs):
@@ -77,10 +84,11 @@
         plane = lax.rem(y + dy, SIDE) * CORES
         mine_refs[dy][...] = windows[plane + core]
         theirs_ref[dy] = windows[plane + 1 - core]
-    for u, rows_ref in zip(OFFSETS, rows_refs):
+    for u in OFFSETS:
         for i, v in enumerate(OFFSETS):
             dx, dz = jnp.where(core == 0, u, v), jnp.where(core == 0, v, u)
-            rows_ref[i] = rows[lax.rem(x + dx + SIDE, SIDE) * SIDE + lax.rem(z + dz + SIDE, SIDE)]
+            block = rows[lax.rem(x + dx + SIDE, SIDE) * SIDE + lax.rem(z + dz + SIDE, SIDE)]
+            place_on_line(rows_refs, u, i, block)
 
 
 def pack(counts, terms):
@@ -88,12 +96,12 @@
     depth = slots * orbitals
     window = jax.ShapeDtypeStruct((depth, WIDE), terms.dtype)
     other_windows = jax.ShapeDtypeStruct((SIDE, depth, WIDE), terms.dtype)
-    line_rows = jax.ShapeDtypeStruct((SIDE, depth, basis // PLANE), terms.dtype)
-    *mine, theirs, rows_0, rows_1, rows_2, rows_3 = pl.pallas_call(
+    line_rows = line_shapes(depth, basis // PLANE, terms.dtype)
+    *mine, theirs, kept, back, ahead = pl.pallas_call(
         pack_kernel,
-        out_shape=(window,) * SIDE + (other_windows,) + (line_rows,) * SIDE,
+        out_shape=(window,) * SIDE + (other_windows,) + line_rows,
         in_specs=[SMEM, VMEM],
-        out_specs=(VMEM,) * (2 * SIDE + 1),
+        out_specs=(VMEM,) * (SIDE + 4),
         scratch_shapes=[
             pltpu.VMEM((CORES * SIDE, depth, WIDE), terms.dtype),
             pltpu.VMEM((PLANE, depth, basis // PLANE), terms.dtype),
@@ -101,31 +109,66 @@
         compiler_params=pltpu.CompilerParams(vmem_limit_bytes=12 << 20),
         name="pack",
     )(counts, terms)
-    return mine, theirs, (rows_0, rows_1, rows_2, rows_3)
+    return mine, theirs, (kept, back, ahead)
+
+
+def line_shapes(depth, chip_rows, dtype):
+    return tuple(jax.ShapeDtypeStruct((n, depth, chip_rows), dtype) for n in (SIDE, SIDE + SIDE // 2, SIDE + SIDE // 2))
+
+
+def by_sender(refs):
+    kept, ahead, behind, far_behind, far_ahead = refs
+    half = SIDE // 2
+    return {
+        0: [kept[i] for i in range(SIDE)],
+        -1: [behind[i] for i in range(SIDE)],
+        1: [ahead[i] for i in range(SIDE)],
+        2: [far_behind[i] for i in range(half)] + [far_ahead[i] for i in range(half)],
+    }
 
 
 def regroup_kernel(*refs):
-    for i, in_ref in enumerate(refs[:SIDE]):
-        for j, out_ref in enumerate(refs[SIDE:]):
-            out_ref[i] = in_ref[j]
-
-
-def regroup(blocks):
+    for j, blocks in enumerate(by_sender(refs[:5])[offset] for offset in OFFSETS):
+        for u, block in zip(OFFSETS, blocks):
+            place_on_line(refs[5:], u, j, block)
+
+
+def regroup(got):
+    depth, chip_rows = got[0].shape[1:]
     return pl.pallas_call(
         regroup_kernel,
-        out_shape=tuple(jax.ShapeDtypeStruct(block.shape, block.dtype) for block in blocks),
-        in_specs=[VMEM] * SIDE,
-        out_specs=(VMEM,) * SIDE,
-        compiler_params=pltpu.CompilerParams(vmem_limit_bytes=6 << 20),
+        out_shape=line_shapes(depth, chip_rows, got[0].dtype),
+        in_specs=[VMEM] * 5,
+        out_specs=(VMEM,) * 3,
+        compiler_params=pltpu.CompilerParams(vmem_limit_bytes=8 << 20),
         name="regroup",
-    )(*blocks)
+    )(*got)
+
+
+def collect_kernel(*refs):
+    for j, blocks in enumerate(by_sender(refs[:5])[offset] for offset in OFFSETS):
+        for i, block in enumerate(blocks):
+            refs[5][j * SIDE + i] = block
+
+
+def collect(got):
+    depth, chip_rows = got[0].shape[1:]
+    return pl.pallas_call(
+        collect_kernel,
+        out_shape=jax.ShapeDtypeStruct((PLANE, depth, chip_rows), got[0].dtype),
+        in_specs=[VMEM] * 5,
+        out_specs=VMEM,
+        compiler_params=pltpu.CompilerParams(vmem_limit_bytes=8 << 20),
+        name="collect",
+    )(*got)
 
 
 def along_line(blocks, order):
-    got = {0: blocks[0]}
-    for offset, block in zip(OFFSETS[1:], blocks[1:]):
-        got[-offset if offset < 2 else 2] = along_plane(block, order, offset)
-    return [got[offset] for offset in OFFSETS]
+    kept, back, ahead = blocks
+    from_ahead, from_behind = along_plane(back, order, -1), along_plane(ahead, order, 1)
+    far_behind = along_plane(from_behind[SIDE:], order, 1)
+    far_ahead = along_plane(from_ahead[SIDE:], order, -1)
+    return kept, from_ahead, from_behind, far_behind, far_ahead
 
 
 def pair_kernel(*refs):
@@ -158,7 +201,8 @@
 
 
 def gathered_briefly(own):
-    before, after, far = (along_plane(own, 0, step) for step in (1, -1, 2))
+    before, after = along_plane(own, 0, 1), along_plane(own, 0, -1)
+    far = along_plane(before, 0, 1)
     line = join([own, before, after, far])
     left, right = along_plane(line, 1, 1), along_plane(line, 1, -1)
     cut = line.shape[0] // 2
@@ -267,7 +311,7 @@
     rows = along_line(rows, 0)
     rows = regroup(rows)
     rows = along_line(rows, 1)
-    rows = join(rows)
+    rows = collect(rows)
     early = gathered_briefly(windows[0])
     parts = gathered(others)
 

time: 174 us -> 194 us (1.11)
  starting transfers between devices: 49.8 us -> 74.7 us
  waiting for transfers between devices: 101 us -> 95.5 us
    ppermute x4, starting transfers between devices: 14.6 us -> 40.1 us  [swap_cores(): return lax.ppermute(block, 'core', [(0, 1), (1, 0)])]
    ppermute x26 -> x28, waiting for transfers between devices: 78.5 us -> 71.7 us  [along_plane(): return lax.ppermute(block, ('x', 'z', 'core'), route)]
    ppermute x26 -> x28, starting transfers between devices: 23.8 us -> 24.8 us  [along_plane(): return lax.ppermute(block, ('x', 'z', 'core'), route)]
  transfers between devices with their start and end apart: 37 -> 39, of which waited for: 20 -> 20; matrix products, arithmetic and copies ran while one was open for 9% -> 8% of each run, Pallas kernels for 1% -> 1%
where the time goes in v3:
time: 194 us
  waiting for transfers between devices  95.5 us (49%)
  starting transfers between devices  74.7 us (39%)
  matrix products  14.3 us (7%)
  Pallas kernels  5.28 us (3%)
  local copies, waits for them, and re-layouts  2.15 us (1%)
    ppermute x28, waiting for transfers between devices, along_plane(): return lax.ppermute(block, ('x', 'z', 'core'), route)  71.7 us
    ppermute x4, starting transfers between devices, swap_cores(): return lax.ppermute(block, 'core', [(0, 1), (1, 0)])  40.1 us
    ppermute x28, starting transfers between devices, along_plane(): return lax.ppermute(block, ('x', 'z', 'core'), route)  24.8 us
    ppermute x7, waiting for transfers between devices, along_y(): lax.ppermute(block, 'y', [(i, (i + step) % SIDE) for i in range(SIDE)])  17.3 us
    dot_general x9, matrix products, product(): lax.dot_general(weight, block, (((0,), (0,)), ((), ())), preferred_elemen...  14.3 us
    ppermute x7, starting transfers between devices, along_y(): lax.ppermute(block, 'y', [(i, (i + step) % SIDE) for i in range(SIDE)])  9.77 us
    ppermute x4, waiting for transfers between devices, swap_cores(): return lax.ppermute(block, 'core', [(0, 1), (1, 0)])  6.48 us
  transfers between devices with their start and end apart: 39, of which 20 were waited for; matrix products, arithmetic and copies ran while one was open for 8% of the time, Pallas kernels for 1%

profile of v3, /device:TPU:1, one launch (start us, length us, event | category | flops | bytes accessed | tf_op | source)
XLA Modules:
  0.0 193.9 jit_solution(7824346888838676646)
XLA Ops:
  3.0 2.5 %collective-permute-start.1 = (bf16[6,48,624]{2,1,0:T(8,128)(2,1)S(1)}, bf16[6,48,624]{2,1,0:T(8,128)(2,1)S(1)}, u32[]{:S(2)}, u32[]{:S(2)}) collective-permute-start(bf16[6,48,624]{2,1,0:T(8,128)(2,1)S(1)} %get-tuple-element.33), channel_id=1, source_target_pairs={{0,8},{1,3},{2,10},{3,5},{4,12},{5,7},{6,14},{7,1},{8,16},{9,11},{... | collective-permute-start | bytes 1078280 | tf_op jit(solution)/shard_map/ppermute | solution.py:32
  5.6 2.2 %collective-permute-start = (bf16[6,48,624]{2,1,0:T(8,128)(2,1)S(1)}, bf16[6,48,624]{2,1,0:T(8,128)(2,1)S(1)}, u32[]{:S(2)}, u32[]{:S(2)}) collective-permute-start(bf16[6,48,624]{2,1,0:T(8,128)(2,1)S(1)} %get-tuple-element.32), channel_id=1, source_target_pairs={{0,24},{1,7},{2,26},{3,1},{4,28},{5,3},{6,30},{7,5},{8,0},{9,15},{... | collective-permute-start | bytes 1078280 | tf_op jit(solution)/shard_map/ppermute | solution.py:32
  7.8 5.1 %collective-permute-done.1.refs_2_ = bf16[6,48,624]{2,1,0:T(8,128)(2,1)S(1)} collective-permute-done((bf16[6,48,624]{2,1,0:T(8,128)(2,1)S(1)}, bf16[6,48,624]{2,1,0:T(8,128)(2,1)S(1)}, u32[]{:S(2)}, u32[]{:S(2)}) %collective-permute-start.1) | collective-permute-done | bytes 359456 | tf_op jit(solution)/shard_map/ppermute | solution.py:32
  13.0 2.8 %collective-permute-start.3 = (bf16[2,48,624]{2,1,0:T(8,128)(2,1)S(1)}, bf16[2,48,624]{2,1,0:T(8,128)(2,1)S(1)}, u32[]{:S(2)}, u32[]{:S(2)}) collective-permute-start(bf16[2,48,624]{2,1,0:T(8,128)(2,1)S(1)} %slice.41), channel_id=1, source_target_pairs={{0,24},{1,7},{2,26},{3,1},{4,28},{5,3},{6,30},{7,5},{8,0},{9,15},{... | collective-permute-start | bytes 359432 | tf_op jit(solution)/shard_map/ppermute | solution.py:32
  15.7 2.4 %collective-permute-done.2.refs_3_ = bf16[2,48,624]{2,1,0:T(8,128)(2,1)S(1)} collective-permute-done((bf16[2,48,624]{2,1,0:T(8,128)(2,1)S(1)}, bf16[2,48,624]{2,1,0:T(8,128)(2,1)S(1)}, u32[]{:S(2)}, u32[]{:S(2)}) %collective-permute-start.2) | collective-permute-done | bytes 119840 | tf_op jit(solution)/shard_map/ppermute | solution.py:32
  19.0 2.0 %collective-permute-start.4 = (bf16[6,48,624]{2,1,0:T(8,128)(2,1)S(1)}, bf16[6,48,624]{2,1,0:T(8,128)(2,1)S(1)}, u32[]{:S(2)}, u32[]{:S(2)}) collective-permute-start(bf16[6,48,624]{2,1,0:T(8,128)(2,1)S(1)} %get-tuple-element.35), channel_id=1, source_target_pairs={{0,6},{1,25},{2,0},{3,27},{4,2},{5,29},{6,4},{7,31},{8,14},{9,1},{... | collective-permute-start | bytes 1078280 | tf_op jit(solution)/shard_map/ppermute | solution.py:32
  21.0 5.2 %collective-permute-done.5.refs_2_ = bf16[6,48,624]{2,1,0:T(8,128)(2,1)S(1)} collective-permute-done((bf16[6,48,624]{2,1,0:T(8,128)(2,1)S(1)}, bf16[6,48,624]{2,1,0:T(8,128)(2,1)S(1)}, u32[]{:S(2)}, u32[]{:S(2)}) %collective-permute-start.5) | collective-permute-done | bytes 359456 | tf_op jit(solution)/shard_map/ppermute | solution.py:32
  26.3 2.7 %collective-permute-start.7 = (bf16[2,48,624]{2,1,0:T(8,128)(2,1)S(1)}, bf16[2,48,624]{2,1,0:T(8,128)(2,1)S(1)}, u32[]{:S(2)}, u32[]{:S(2)}) collective-permute-start(bf16[2,48,624]{2,1,0:T(8,128)(2,1)S(1)} %slice.43), channel_id=1, source_target_pairs={{0,6},{1,25},{2,0},{3,27},{4,2},{5,29},{6,4},{7,31},{8,14},{9,1},{... | collective-permute-start | bytes 359432 | tf_op jit(solution)/shard_map/ppermute | solution.py:32
  29.0 2.2 %collective-permute-done.6.refs_3_ = bf16[2,48,624]{2,1,0:T(8,128)(2,1)S(1)} collective-permute-done((bf16[2,48,624]{2,1,0:T(8,128)(2,1)S(1)}, bf16[2,48,624]{2,1,0:T(8,128)(2,1)S(1)}, u32[]{:S(2)}, u32[]{:S(2)}) %collective-permute-start.6) | collective-permute-done | bytes 119840 | tf_op jit(solution)/shard_map/ppermute | solution.py:32
  34.2 4.5 %collective-permute-start.9 = (bf16[4,48,1280]{2,1,0:T(8,128)(2,1)S(1)}, bf16[4,48,1280]{2,1,0:T(8,128)(2,1)S(1)}, u32[]{:S(2)}, u32[]{:S(2)}) collective-permute-start(bf16[4,48,1280]{2,1,0:T(8,128)(2,1)S(1)} %get-tuple-element.42), channel_id=1, source_target_pairs={{0,1},{1,0},{2,3},{3,2},{4,5},{5,4},{6,7},{7,6},{8,9},{9,8},{10,11... | collective-permute-start | bytes 1474568 | tf_op jit(solution)/shard_map/ppermute | solution.py:22
  42.9 14.0 %collective-permute-done.20.refs_0_ = bf16[96,1280]{1,0:T(8,128)(2,1)S(1)} collective-permute-done((bf16[96,1280]{1,0:T(8,128)(2,1)S(1)}, bf16[96,1280]{1,0:T(8,128)(2,1)S(1)}, u32[]{:S(2)}, u32[]{:S(2)}) %collective-permute-start.20) | collective-permute-done | bytes 245792 | tf_op jit(solution)/shard_map/ppermute | solution.py:18
  58.0 2.2 %collective-permute-done.22.refs_2_ = bf16[96,1280]{1,0:T(8,128)(2,1)S(1)} collective-permute-done((bf16[96,1280]{1,0:T(8,128)(2,1)S(1)}, bf16[96,1280]{1,0:T(8,128)(2,1)S(1)}, u32[]{:S(2)}, u32[]{:S(2)}) %collective-permute-start.22) | collective-permute-done | bytes 245792 | tf_op jit(solution)/shard_map/ppermute | solution.py:18
  60.5 2.7 %collective-permute-start.11 = (bf16[96,1280]{1,0:T(8,128)(2,1)S(1)}, bf16[96,1280]{1,0:T(8,128)(2,1)S(1)}, u32[]{:S(2)}, u32[]{:S(2)}) collective-permute-start(bf16[96,1280]{1,0:T(8,128)(2,1)S(1)} %get-tuple-element.43.refs_0_), channel_id=1, source_target_pairs={{0,24},{1,7},{2,26},{3,1},{4,28},{5,3},{6,30},{7,5},{8,0},{9,15},{... | collective-permute-start | bytes 737288 | tf_op jit(solution)/shard_map/ppermute | solution.py:32
  63.2 3.7 %collective-permute-start.17 = (bf16[8,48,624]{2,1,0:T(8,128)(2,1)S(1)}, bf16[8,48,624]{2,1,0:T(8,128)(2,1)S(1)}, u32[]{:S(2)}, u32[]{:S(2)}) collective-permute-start(bf16[8,48,624]{2,1,0:T(8,128)(2,1)S(1)} %slice.44), channel_id=1, source_target_pairs={{0,32},{32,64},{64,96},{96,0},{1,33},{33,65},{65,97},{97,1},{2,34}... | collective-permute-start | bytes 1437704 | tf_op jit(solution)/shard_map/ppermute | solution.py:18
  67.4 7.4 %collective-permute-done.10.refs_1_ = bf16[96,1280]{1,0:T(8,128)(2,1)S(1)} collective-permute-done((bf16[96,1280]{1,0:T(8,128)(2,1)S(1)}, bf16[96,1280]{1,0:T(8,128)(2,1)S(1)}, u32[]{:S(2)}, u32[]{:S(2)}) %collective-permute-start.10) | collective-permute-done | bytes 245792 | tf_op jit(solution)/shard_map/ppermute | solution.py:32
  76.3 5.8 %collective-permute-done.12.refs_3_ = bf16[96,1280]{1,0:T(8,128)(2,1)S(1)} collective-permute-done((bf16[96,1280]{1,0:T(8,128)(2,1)S(1)}, bf16[96,1280]{1,0:T(8,128)(2,1)S(1)}, u32[]{:S(2)}, u32[]{:S(2)}) %collective-permute-start.12) | collective-permute-done | bytes 245792 | tf_op jit(solution)/shard_map/ppermute | solution.py:32
  82.9 2.0 %collective-permute-start.31 = (bf16[288,1280]{1,0:T(8,128)(2,1)S(1)}, bf16[288,1280]{1,0:T(8,128)(2,1)S(1)}, u32[]{:S(2)}, u32[]{:S(2)}) collective-permute-start(bf16[288,1280]{1,0:T(8,128)(2,1)S(1)} %join.11.refs_0_), channel_id=1, source_target_pairs={{0,6},{1,25},{2,0},{3,27},{4,2},{5,29},{6,4},{7,31},{8,14},{9,1},{... | collective-permute-start | bytes 2211848 | tf_op jit(solution)/shard_map/ppermute | solution.py:32
  85.2 13.3 %collective-permute-start.19 = (bf16[48,48,624]{2,1,0:T(8,128)(2,1)S(1)}, bf16[48,48,624]{2,1,0:T(8,128)(2,1)S(1)}, u32[]{:S(2)}, u32[]{:S(2)}) collective-permute-start(bf16[48,48,624]{2,1,0:T(8,128)(2,1)S(1)} %join.10.refs_0_), channel_id=1, source_target_pairs={{0,1},{1,0},{2,3},{3,2},{4,5},{5,4},{6,7},{7,6},{8,9},{9,8},{10,11... | collective-permute-start | bytes 8626184 | tf_op jit(solution)/shard_map/ppermute | solution.py:22
  98.6 8.6 %collective-permute-done.30.refs_3_ = bf16[288,1280]{1,0:T(8,128)(2,1)S(1)} collective-permute-done((bf16[288,1280]{1,0:T(8,128)(2,1)S(1)}, bf16[288,1280]{1,0:T(8,128)(2,1)S(1)}, u32[]{:S(2)}, u32[]{:S(2)}) %collective-permute-start.30) | collective-permute-done | bytes 737312 | tf_op jit(solution)/shard_map/ppermute | solution.py:32
  107.2 10.9 %collective-permute-start.8 = (bf16[16,48,624]{2,1,0:T(8,128)(2,1)S(1)}, bf16[16,48,624]{2,1,0:T(8,128)(2,1)S(1)}, u32[]{:S(2)}, u32[]{:S(2)}) collective-permute-start(bf16[16,48,624]{2,1,0:T(8,128)(2,1)S(1)} %collect.1.refs_0_), channel_id=1, source_target_pairs={{0,1},{1,0},{2,3},{3,2},{4,5},{5,4},{6,7},{7,6},{8,9},{9,8},{10,11... | collective-permute-start | bytes 2875400 | tf_op jit(solution)/shard_map/ppermute | solution.py:22
  118.3 1.9 collective-permute-done.8.refs_1_
  120.2 17.6 %collective-permute-done.29.refs_2_ = bf16[288,1280]{1,0:T(8,128)(2,1)S(1)} collective-permute-done((bf16[288,1280]{1,0:T(8,128)(2,1)S(1)}, bf16[288,1280]{1,0:T(8,128)(2,1)S(1)}, u32[]{:S(2)}, u32[]{:S(2)}) %collective-permute-start.29) | collective-permute-done | bytes 737312 | tf_op jit(solution)/shard_map/ppermute | solution.py:32
  137.9 2.2 %collective-permute-done.27.refs_0_ = bf16[192,1280]{1,0:T(8,128)(2,1)S(1)} collective-permute-done((bf16[192,1280]{1,0:T(8,128)(2,1)S(1)}, bf16[192,1280]{1,0:T(8,128)(2,1)S(1)}, u32[]{:S(2)}, u32[]{:S(2)}) %collective-permute-start.27) | collective-permute-done | bytes 491552 | tf_op jit(solution)/shard_map/ppermute | solution.py:32
  140.1 5.8 %collective-permute-done.28.refs_1_ = bf16[192,1280]{1,0:T(8,128)(2,1)S(1)} collective-permute-done((bf16[192,1280]{1,0:T(8,128)(2,1)S(1)}, bf16[192,1280]{1,0:T(8,128)(2,1)S(1)}, u32[]{:S(2)}, u32[]{:S(2)}) %collective-permute-start.28) | collective-permute-done | bytes 491552 | tf_op jit(solution)/shard_map/ppermute | solution.py:32
  149.3 2.3 %collective-permute-done.36.refs_2_ = bf16[288,1280]{1,0:T(8,128)(2,1)S(1)} collective-permute-done((bf16[288,1280]{1,0:T(8,128)(2,1)S(1)}, bf16[288,1280]{1,0:T(8,128)(2,1)S(1)}, u32[]{:S(2)}, u32[]{:S(2)}) %collective-permute-start.36) | collective-permute-done | bytes 737312 | tf_op jit(solution)/shard_map/ppermute | solution.py:32
  152.0 4.4 %collective-permute-done.35.refs_1_ = bf16[288,1280]{1,0:T(8,128)(2,1)S(1)} collective-permute-done((bf16[288,1280]{1,0:T(8,128)(2,1)S(1)}, bf16[288,1280]{1,0:T(8,128)(2,1)S(1)}, u32[]{:S(2)}, u32[]{:S(2)}) %collective-permute-start.35) | collective-permute-done | bytes 737312 | tf_op jit(solution)/shard_map/ppermute | solution.py:32
  156.5 2.4 %collective-permute-start.37 = (bf16[288,1280]{1,0:T(8,128)(2,1)S(1)}, bf16[288,1280]{1,0:T(8,128)(2,1)S(1)}, u32[]{:S(2)}, u32[]{:S(2)}) collective-permute-start(bf16[288,1280]{1,0:T(8,128)(2,1)S(1)} %collective-permute-done.35.refs_1_), channel_id=1, source_target_pairs={{0,6},{1,25},{2,0},{3,27},{4,2},{5,29},{6,4},{7,31},{8,14},{9,1},{... | collective-permute-start | bytes 2211848 | tf_op jit(solution)/shard_map/ppermute | solution.py:32
  161.9 2.4 %convolution_add_fusion.3 = f32[624,1280]{1,0:T(8,128)S(1)} fusion(f32[624,1280]{1,0:T(8,128)S(1)} %fusion, bf16[1152,624]{1,0:T(8,128)(2,1)S(1)} %get-tuple-element.37, bf16[1152,1280]{1,0:T(8,128)(2,1)S(1)} %join.9), kind=kOutput, calls=%fused_computation.3 | convolution fusion | flops 1841049600 | bytes 10776576 | tf_op jit(solution)/shard_map/dot_general | solution.py:326
  166.5 3.2 %convolution_add_fusion.2 = f32[624,1280]{1,0:T(8,128)S(1)} fusion(f32[624,1280]{1,0:T(8,128)S(1)} %add.26, bf16[1728,624]{1,0:T(8,128)(2,1)S(1)} %get-tuple-element.50, bf16[1728,1280]{1,0:T(8,128)(2,1)S(1)} %join.14), kind=kOutput, calls=%fused_computation.2 | convolution fusion | flops 2761175040 | bytes 12969984 | tf_op jit(solution)/shard_map/dot_general | solution.py:326
  172.2 2.2 %convolution_add_fusion.1 = f32[624,1280]{1,0:T(8,128)S(1)} fusion(f32[624,1280]{1,0:T(8,128)S(1)} %add.29, bf16[864,624]{1,0:T(8,128)(2,1)S(1)} %get-tuple-element.53, bf16[864,1280]{1,0:T(8,128)(2,1)S(1)} %join.15), kind=kOutput, calls=%fused_computation.1 | convolution fusion | flops 1380986880 | bytes 9679872 | tf_op jit(solution)/shard_map/dot_general | solution.py:326
  177.5 11.5 %collective-permute-start.38 = (f32[312,1280]{1,0:T(8,128)S(1)}, f32[312,1280]{1,0:T(8,128)S(1)}, u32[]{:S(2)}, u32[]{:S(2)}) collective-permute-start(f32[312,1280]{1,0:T(8,128)S(1)} %get-tuple-element.56), channel_id=1, source_target_pairs={{0,1},{1,0},{2,3},{3,2},{4,5},{5,4},{6,7},{7,6},{8,9},{9,8},{10,11... | collective-permute-start | bytes 4792328 | tf_op jit(solution)/shard_map/ppermute | solution.py:22
  188.9 3.1 %collective-permute-done.38.got_ref = f32[312,1280]{1,0:T(8,128)S(1)} collective-permute-done((f32[312,1280]{1,0:T(8,128)S(1)}, f32[312,1280]{1,0:T(8,128)S(1)}, u32[]{:S(2)}, u32[]{:S(2)}) %collective-permute-start.38) | collective-permute-done | bytes 1597472 | tf_op jit(solution)/shard_map/ppermute | solution.py:22
  (89 shorter events, 32.6 us)
Async XLA Ops:
  3.0 9.8 %collective-permute-start.1 = (bf16[6,48,624]{2,1,0:T(8,128)(2,1)S(1)}, bf16[6,48,624]{2,1,0:T(8,128)(2,1)S(1)}, u32[]{:S(2)}, u32[]{:S(2)}) collective-permute-start(bf16[6,48,624]{2,1,0:T(8,128)(2,1)S(1)} %get-tuple-element.33), channel_id=1, source_target_pairs={{0,8},{1,3},{2,10},{3,5},{4,12},{5,7},{6,14},{7,1},{8,16},{9,11},{... | collective-permute-start | bytes 1078280 | tf_op jit(solution)/shard_map/ppermute | solution.py:32
  5.6 7.4 %collective-permute-start = (bf16[6,48,624]{2,1,0:T(8,128)(2,1)S(1)}, bf16[6,48,624]{2,1,0:T(8,128)(2,1)S(1)}, u32[]{:S(2)}, u32[]{:S(2)}) collective-permute-start(bf16[6,48,624]{2,1,0:T(8,128)(2,1)S(1)} %get-tuple-element.32), channel_id=1, source_target_pairs={{0,24},{1,7},{2,26},{3,1},{4,28},{5,3},{6,30},{7,5},{8,0},{9,15},{... | collective-permute-start | bytes 1078280 | tf_op jit(solution)/shard_map/ppermute | solution.py:32
  18.2 7.9 %collective-permute-start.5 = (bf16[6,48,624]{2,1,0:T(8,128)(2,1)S(1)}, bf16[6,48,624]{2,1,0:T(8,128)(2,1)S(1)}, u32[]{:S(2)}, u32[]{:S(2)}) collective-permute-start(bf16[6,48,624]{2,1,0:T(8,128)(2,1)S(1)} %get-tuple-element.36), channel_id=1, source_target_pairs={{0,2},{1,9},{2,4},{3,11},{4,6},{5,13},{6,0},{7,15},{8,10},{9,17},{... | collective-permute-start | bytes 1078280 | tf_op jit(solution)/shard_map/ppermute | solution.py:32
  31.3 31.9 %collective-permute-start.16 = (bf16[16,48,624]{2,1,0:T(8,128)(2,1)S(1)}, bf16[16,48,624]{2,1,0:T(8,128)(2,1)S(1)}, u32[]{:S(2)}, u32[]{:S(2)}) collective-permute-start(bf16[16,48,624]{2,1,0:T(8,128)(2,1)S(1)} %collect.1.refs_0_), channel_id=1, source_target_pairs={{0,32},{32,64},{64,96},{96,0},{1,33},{33,65},{65,97},{97,1},{2,34}... | collective-permute-start | bytes 2875400 | tf_op jit(solution)/shard_map/ppermute | solution.py:18
  32.7 34.2 %collective-permute-start.15 = (bf16[16,48,624]{2,1,0:T(8,128)(2,1)S(1)}, bf16[16,48,624]{2,1,0:T(8,128)(2,1)S(1)}, u32[]{:S(2)}, u32[]{:S(2)}) collective-permute-start(bf16[16,48,624]{2,1,0:T(8,128)(2,1)S(1)} %collect.1.refs_0_), channel_id=1, source_target_pairs={{0,96},{32,0},{64,32},{96,64},{1,97},{33,1},{65,33},{97,65},{2,98}... | collective-permute-start | bytes 2875400 | tf_op jit(solution)/shard_map/ppermute | solution.py:18
  40.3 16.6 %collective-permute-start.20 = (bf16[96,1280]{1,0:T(8,128)(2,1)S(1)}, bf16[96,1280]{1,0:T(8,128)(2,1)S(1)}, u32[]{:S(2)}, u32[]{:S(2)}) collective-permute-start(bf16[96,1280]{1,0:T(8,128)(2,1)S(1)} %get-tuple-element.45), channel_id=1, source_target_pairs={{0,96},{32,0},{64,32},{96,64},{1,97},{33,1},{65,33},{97,65},{2,98}... | collective-permute-start | bytes 737288 | tf_op jit(solution)/shard_map/ppermute | solution.py:18
  41.9 16.1 %collective-permute-start.21 = (bf16[96,1280]{1,0:T(8,128)(2,1)S(1)}, bf16[96,1280]{1,0:T(8,128)(2,1)S(1)}, u32[]{:S(2)}, u32[]{:S(2)}) collective-permute-start(bf16[96,1280]{1,0:T(8,128)(2,1)S(1)} %get-tuple-element.46), channel_id=1, source_target_pairs={{0,64},{32,96},{64,0},{96,32},{1,65},{33,97},{65,1},{97,33},{2,66}... | collective-permute-start | bytes 737288 | tf_op jit(solution)/shard_map/ppermute | solution.py:18
  42.3 18.0 %collective-permute-start.22 = (bf16[96,1280]{1,0:T(8,128)(2,1)S(1)}, bf16[96,1280]{1,0:T(8,128)(2,1)S(1)}, u32[]{:S(2)}, u32[]{:S(2)}) collective-permute-start(bf16[96,1280]{1,0:T(8,128)(2,1)S(1)} %get-tuple-element.47), channel_id=1, source_target_pairs={{0,32},{32,64},{64,96},{96,0},{1,33},{33,65},{65,97},{97,1},{2,34}... | collective-permute-start | bytes 737288 | tf_op jit(solution)/shard_map/ppermute | solution.py:18
  60.3 24.9 %collective-permute-start.23 = (bf16[288,1280]{1,0:T(8,128)(2,1)S(1)}, bf16[288,1280]{1,0:T(8,128)(2,1)S(1)}, u32[]{:S(2)}, u32[]{:S(2)}) collective-permute-start(bf16[288,1280]{1,0:T(8,128)(2,1)S(1)} %join.11.refs_0_), channel_id=1, source_target_pairs={{0,8},{1,3},{2,10},{3,5},{4,12},{5,7},{6,14},{7,1},{8,16},{9,11},{... | collective-permute-start | bytes 2211848 | tf_op jit(solution)/shard_map/ppermute | solution.py:32
  60.4 14.4 %collective-permute-start.10 = (bf16[96,1280]{1,0:T(8,128)(2,1)S(1)}, bf16[96,1280]{1,0:T(8,128)(2,1)S(1)}, u32[]{:S(2)}, u32[]{:S(2)}) collective-permute-start(bf16[96,1280]{1,0:T(8,128)(2,1)S(1)} %get-tuple-element.43.refs_0_), channel_id=1, source_target_pairs={{0,8},{1,3},{2,10},{3,5},{4,12},{5,7},{6,14},{7,1},{8,16},{9,11},{... | collective-permute-start | bytes 737288 | tf_op jit(solution)/shard_map/ppermute | solution.py:32
  60.5 15.0 %collective-permute-start.11 = (bf16[96,1280]{1,0:T(8,128)(2,1)S(1)}, bf16[96,1280]{1,0:T(8,128)(2,1)S(1)}, u32[]{:S(2)}, u32[]{:S(2)}) collective-permute-start(bf16[96,1280]{1,0:T(8,128)(2,1)S(1)} %get-tuple-element.43.refs_0_), channel_id=1, source_target_pairs={{0,24},{1,7},{2,26},{3,1},{4,28},{5,3},{6,30},{7,5},{8,0},{9,15},{... | collective-permute-start | bytes 737288 | tf_op jit(solution)/shard_map/ppermute | solution.py:32
  63.2 19.0 %collective-permute-start.17 = (bf16[8,48,624]{2,1,0:T(8,128)(2,1)S(1)}, bf16[8,48,624]{2,1,0:T(8,128)(2,1)S(1)}, u32[]{:S(2)}, u32[]{:S(2)}) collective-permute-start(bf16[8,48,624]{2,1,0:T(8,128)(2,1)S(1)} %slice.44), channel_id=1, source_target_pairs={{0,32},{32,64},{64,96},{96,0},{1,33},{33,65},{65,97},{97,1},{2,34}... | collective-permute-start | bytes 1437704 | tf_op jit(solution)/shard_map/ppermute | solution.py:18
  66.9 16.0 %collective-permute-start.18 = (bf16[8,48,624]{2,1,0:T(8,128)(2,1)S(1)}, bf16[8,48,624]{2,1,0:T(8,128)(2,1)S(1)}, u32[]{:S(2)}, u32[]{:S(2)}) collective-permute-start(bf16[8,48,624]{2,1,0:T(8,128)(2,1)S(1)} %slice.45), channel_id=1, source_target_pairs={{0,96},{32,0},{64,32},{96,64},{1,97},{33,1},{65,33},{97,65},{2,98}... | collective-permute-start | bytes 1437704 | tf_op jit(solution)/shard_map/ppermute | solution.py:18
  74.8 23.7 %collective-permute-start.24 = (bf16[288,1280]{1,0:T(8,128)(2,1)S(1)}, bf16[288,1280]{1,0:T(8,128)(2,1)S(1)}, u32[]{:S(2)}, u32[]{:S(2)}) collective-permute-start(bf16[288,1280]{1,0:T(8,128)(2,1)S(1)} %join.11.refs_0_), channel_id=1, source_target_pairs={{0,24},{1,7},{2,26},{3,1},{4,28},{5,3},{6,30},{7,5},{8,0},{9,15},{... | collective-permute-start | bytes 2211848 | tf_op jit(solution)/shard_map/ppermute | solution.py:32
  82.1 35.9 %collective-permute-start.13 = (bf16[384,1280]{1,0:T(8,128)(2,1)S(1)}, bf16[384,1280]{1,0:T(8,128)(2,1)S(1)}, u32[]{:S(2)}, u32[]{:S(2)}) collective-permute-start(bf16[384,1280]{1,0:T(8,128)(2,1)S(1)} %join.8.refs_0_), channel_id=1, source_target_pairs={{0,2},{1,9},{2,4},{3,11},{4,6},{5,13},{6,0},{7,15},{8,10},{9,17},{... | collective-permute-start | bytes 2949128 | tf_op jit(solution)/shard_map/ppermute | solution.py:32
  82.2 25.0 %collective-permute-start.30 = (bf16[288,1280]{1,0:T(8,128)(2,1)S(1)}, bf16[288,1280]{1,0:T(8,128)(2,1)S(1)}, u32[]{:S(2)}, u32[]{:S(2)}) collective-permute-start(bf16[288,1280]{1,0:T(8,128)(2,1)S(1)} %join.11.refs_0_), channel_id=1, source_target_pairs={{0,2},{1,9},{2,4},{3,11},{4,6},{5,13},{6,0},{7,15},{8,10},{9,17},{... | collective-permute-start | bytes 2211848 | tf_op jit(solution)/shard_map/ppermute | solution.py:32
  82.9 24.3 %collective-permute-start.31 = (bf16[288,1280]{1,0:T(8,128)(2,1)S(1)}, bf16[288,1280]{1,0:T(8,128)(2,1)S(1)}, u32[]{:S(2)}, u32[]{:S(2)}) collective-permute-start(bf16[288,1280]{1,0:T(8,128)(2,1)S(1)} %join.11.refs_0_), channel_id=1, source_target_pairs={{0,6},{1,25},{2,0},{3,27},{4,2},{5,29},{6,4},{7,31},{8,14},{9,1},{... | collective-permute-start | bytes 2211848 | tf_op jit(solution)/shard_map/ppermute | solution.py:32
  85.2 74.7 %collective-permute-start.19 = (bf16[48,48,624]{2,1,0:T(8,128)(2,1)S(1)}, bf16[48,48,624]{2,1,0:T(8,128)(2,1)S(1)}, u32[]{:S(2)}, u32[]{:S(2)}) collective-permute-start(bf16[48,48,624]{2,1,0:T(8,128)(2,1)S(1)} %join.10.refs_0_), channel_id=1, source_target_pairs={{0,1},{1,0},{2,3},{3,2},{4,5},{5,4},{6,7},{7,6},{8,9},{9,8},{10,11... | collective-permute-start | bytes 8626184 | tf_op jit(solution)/shard_map/ppermute | solution.py:22
  98.5 19.8 %collective-permute-start.14 = (bf16[384,1280]{1,0:T(8,128)(2,1)S(1)}, bf16[384,1280]{1,0:T(8,128)(2,1)S(1)}, u32[]{:S(2)}, u32[]{:S(2)}) collective-permute-start(bf16[384,1280]{1,0:T(8,128)(2,1)S(1)} %join.8.refs_0_), channel_id=1, source_target_pairs={{0,6},{1,25},{2,0},{3,27},{4,2},{5,29},{6,4},{7,31},{8,14},{9,1},{... | collective-permute-start | bytes 2949128 | tf_op jit(solution)/shard_map/ppermute | solution.py:32
  107.2 39.9 %collective-permute-start.25 = (bf16[576,1280]{1,0:T(8,128)(2,1)S(1)}, bf16[576,1280]{1,0:T(8,128)(2,1)S(1)}, u32[]{:S(2)}, u32[]{:S(2)}) collective-permute-start(bf16[576,1280]{1,0:T(8,128)(2,1)S(1)} %join.12.refs_1_), channel_id=1, source_target_pairs={{0,2},{1,9},{2,4},{3,11},{4,6},{5,13},{6,0},{7,15},{8,10},{9,17},{... | collective-permute-start | bytes 4423688 | tf_op jit(solution)/shard_map/ppermute | solution.py:32
  107.2 13.0 %collective-permute-start.8 = (bf16[16,48,624]{2,1,0:T(8,128)(2,1)S(1)}, bf16[16,48,624]{2,1,0:T(8,128)(2,1)S(1)}, u32[]{:S(2)}, u32[]{:S(2)}) collective-permute-start(bf16[16,48,624]{2,1,0:T(8,128)(2,1)S(1)} %collect.1.refs_0_), channel_id=1, source_target_pairs={{0,1},{1,0},{2,3},{3,2},{4,5},{5,4},{6,7},{7,6},{8,9},{9,8},{10,11... | collective-permute-start | bytes 2875400 | tf_op jit(solution)/shard_map/ppermute | solution.py:22
  118.0 19.8 %collective-permute-start.29 = (bf16[288,1280]{1,0:T(8,128)(2,1)S(1)}, bf16[288,1280]{1,0:T(8,128)(2,1)S(1)}, u32[]{:S(2)}, u32[]{:S(2)}) collective-permute-start(bf16[288,1280]{1,0:T(8,128)(2,1)S(1)} %collective-permute-done.23.refs_0_), channel_id=1, source_target_pairs={{0,8},{1,3},{2,10},{3,5},{4,12},{5,7},{6,14},{7,1},{8,16},{9,11},{... | collective-permute-start | bytes 2211848 | tf_op jit(solution)/shard_map/ppermute | solution.py:32
  118.2 30.9 %collective-permute-start.26 = (bf16[576,1280]{1,0:T(8,128)(2,1)S(1)}, bf16[576,1280]{1,0:T(8,128)(2,1)S(1)}, u32[]{:S(2)}, u32[]{:S(2)}) collective-permute-start(bf16[576,1280]{1,0:T(8,128)(2,1)S(1)} %join.12.refs_1_), channel_id=1, source_target_pairs={{0,6},{1,25},{2,0},{3,27},{4,2},{5,29},{6,4},{7,31},{8,14},{9,1},{... | collective-permute-start | bytes 4423688 | tf_op jit(solution)/shard_map/ppermute | solution.py:32
  120.2 19.8 %collective-permute-start.27 = (bf16[192,1280]{1,0:T(8,128)(2,1)S(1)}, bf16[192,1280]{1,0:T(8,128)(2,1)S(1)}, u32[]{:S(2)}, u32[]{:S(2)}) collective-permute-start(bf16[192,1280]{1,0:T(8,128)(2,1)S(1)} %slice.46), channel_id=1, source_target_pairs={{0,2},{1,9},{2,4},{3,11},{4,6},{5,13},{6,0},{7,15},{8,10},{9,17},{... | collective-permute-start | bytes 1474568 | tf_op jit(solution)/shard_map/ppermute | solution.py:32
  137.9 8.0 %collective-permute-start.28 = (bf16[192,1280]{1,0:T(8,128)(2,1)S(1)}, bf16[192,1280]{1,0:T(8,128)(2,1)S(1)}, u32[]{:S(2)}, u32[]{:S(2)}) collective-permute-start(bf16[192,1280]{1,0:T(8,128)(2,1)S(1)} %slice.47), channel_id=1, source_target_pairs={{0,6},{1,25},{2,0},{3,27},{4,2},{5,29},{6,4},{7,31},{8,14},{9,1},{... | collective-permute-start | bytes 1474568 | tf_op jit(solution)/shard_map/ppermute | solution.py:32
  140.1 11.5 %collective-permute-start.36 = (bf16[288,1280]{1,0:T(8,128)(2,1)S(1)}, bf16[288,1280]{1,0:T(8,128)(2,1)S(1)}, u32[]{:S(2)}, u32[]{:S(2)}) collective-permute-start(bf16[288,1280]{1,0:T(8,128)(2,1)S(1)} %collective-permute-done.30.refs_3_), channel_id=1, source_target_pairs={{0,2},{1,9},{2,4},{3,11},{4,6},{5,13},{6,0},{7,15},{8,10},{9,17},{... | collective-permute-start | bytes 2211848 | tf_op jit(solution)/shard_map/ppermute | solution.py:32
  145.8 10.6 %collective-permute-start.35 = (bf16[288,1280]{1,0:T(8,128)(2,1)S(1)}, bf16[288,1280]{1,0:T(8,128)(2,1)S(1)}, u32[]{:S(2)}, u32[]{:S(2)}) collective-permute-start(bf16[288,1280]{1,0:T(8,128)(2,1)S(1)} %collective-permute-done.29.refs_2_), channel_id=1, source_target_pairs={{0,6},{1,25},{2,0},{3,27},{4,2},{5,29},{6,4},{7,31},{8,14},{9,1},{... | collective-permute-start | bytes 2211848 | tf_op jit(solution)/shard_map/ppermute | solution.py:32
  147.1 12.7 %collective-permute-start.34 = (bf16[288,1280]{1,0:T(8,128)(2,1)S(1)}, bf16[288,1280]{1,0:T(8,128)(2,1)S(1)}, u32[]{:S(2)}, u32[]{:S(2)}) collective-permute-start(bf16[288,1280]{1,0:T(8,128)(2,1)S(1)} %collective-permute-done.29.refs_2_), channel_id=1, source_target_pairs={{0,2},{1,9},{2,4},{3,11},{4,6},{5,13},{6,0},{7,15},{8,10},{9,17},{... | collective-permute-start | bytes 2211848 | tf_op jit(solution)/shard_map/ppermute | solution.py:32
  149.1 20.6 %collective-permute-start.32 = (bf16[144,1280]{1,0:T(8,128)(2,1)S(1)}, bf16[144,1280]{1,0:T(8,128)(2,1)S(1)}, u32[]{:S(2)}, u32[]{:S(2)}) collective-permute-start(bf16[144,1280]{1,0:T(8,128)(2,1)S(1)} %slice.48), channel_id=1, source_target_pairs={{0,2},{1,9},{2,4},{3,11},{4,6},{5,13},{6,0},{7,15},{8,10},{9,17},{... | collective-permute-start | bytes 1105928 | tf_op jit(solution)/shard_map/ppermute | solution.py:32
  151.6 19.2 %collective-permute-start.33 = (bf16[432,1280]{1,0:T(8,128)(2,1)S(1)}, bf16[432,1280]{1,0:T(8,128)(2,1)S(1)}, u32[]{:S(2)}, u32[]{:S(2)}) collective-permute-start(bf16[432,1280]{1,0:T(8,128)(2,1)S(1)} %slice.49), channel_id=1, source_target_pairs={{0,6},{1,25},{2,0},{3,27},{4,2},{5,29},{6,4},{7,31},{8,14},{9,1},{... | collective-permute-start | bytes 3317768 | tf_op jit(solution)/shard_map/ppermute | solution.py:32
  156.5 19.7 %collective-permute-start.37 = (bf16[288,1280]{1,0:T(8,128)(2,1)S(1)}, bf16[288,1280]{1,0:T(8,128)(2,1)S(1)}, u32[]{:S(2)}, u32[]{:S(2)}) collective-permute-start(bf16[288,1280]{1,0:T(8,128)(2,1)S(1)} %collective-permute-done.35.refs_1_), channel_id=1, source_target_pairs={{0,6},{1,25},{2,0},{3,27},{4,2},{5,29},{6,4},{7,31},{8,14},{9,1},{... | collective-permute-start | bytes 2211848 | tf_op jit(solution)/shard_map/ppermute | solution.py:32
  177.5 14.5 %collective-permute-start.38 = (f32[312,1280]{1,0:T(8,128)S(1)}, f32[312,1280]{1,0:T(8,128)S(1)}, u32[]{:S(2)}, u32[]{:S(2)}) collective-permute-start(f32[312,1280]{1,0:T(8,128)S(1)} %get-tuple-element.56), channel_id=1, source_target_pairs={{0,1},{1,0},{2,3},{3,2},{4,5},{5,4},{6,7},{7,6},{8,9},{9,8},{10,11... | collective-permute-start | bytes 4792328 | tf_op jit(solution)/shard_map/ppermute | solution.py:22
  (9 other events, 42.1 us)

commit v4 on v2

--- a/solution.py
+++ b/solution.py
@@ -153,47 +153,55 @@
 OTHERS = tuple((dcore, dy) for dy in range(1, SIDE) for dcore in range(CORES))
 
 
-def at(v, *us):
-    return tuple((u, v) for u in us)
-
-
-def gathered_briefly(own):
-    before, after, far = (along_plane(own, 0, step) for step in (1, -1, 2))
-    line = join([own, before, after, far])
+def at(sources, v, *us):
+    return tuple((u, v, *source) for u in us for source in sources)
+
+
+def gathered(early, late):
+    early_before, early_after = along_plane(early, 0, 1), along_plane(early, 0, -1)
+    line = join([early, early_before, early_after])
     left, right = along_plane(line, 1, 1), along_plane(line, 1, -1)
     cut = line.shape[0] // 2
     opposite = along_plane(left[:cut], 1, 1), along_plane(right[cut:], 1, -1)
-    first = sum((at(v, 0, -1, 1, 2) for v in (0, -1, 1)), ())
-    last = join(opposite)
-    return (first, join([line, left, right])), (at(2, 0, -1, 1, 2), last)
-
-
-def gathered(own):
-    before, after, far = (along_plane(own, 0, step) for step in (1, -1, 2))
+
+    before, after = along_plane(late, 0, 1), along_plane(late, 0, -1)
     near = join([before, after])
+    both_before = join([early_before, before])
+    far = along_plane(both_before, 0, 1)
     near_sides = along_plane(near, 1, 1), along_plane(near, 1, -1)
-    own_sides = along_plane(own, 1, 1), along_plane(own, 1, -1)
+    own_sides = along_plane(late, 1, 1), along_plane(late, 1, -1)
     far_sides = along_plane(far, 1, 1), along_plane(far, 1, -1)
     own_opposite = along_plane(own_sides[0], 1, 1)
-    near_opposite = along_plane(near_sides[1], 1, -1)
+    cut = late.shape[0] // 2
+    near_opposite = along_plane(near_sides[0][:cut], 1, 1), along_plane(near_sides[1][cut:], 1, -1)
     far_opposite = along_plane(far_sides[1], 1, -1)
 
-    first = at(0, 0, -1, 1, 2) + at(-1, 0) + at(1, 0)
-    parts = [(first, join([own, near, far, *own_sides]))]
-    parts += [(at(v, -1, 1), block) for v, block in zip((-1, 1), near_sides)]
-    parts += [(at(-1, 2) + at(1, 2) + at(2, 0), join([*far_sides, own_opposite]))]
-    parts += [(at(2, -1, 1), near_opposite), (at(2, 2), far_opposite)]
-    return parts
+    early_opposite = join(opposite)
+    first = join([late, near, far, *own_sides])
+    middle = join([*far_sides, own_opposite])
+    ends = at(OTHERS, 2, -1, 1)
+    return (
+        (sum((at(OWN, v, 0, -1, 1) for v in (0, -1, 1)), ()), join([line, left, right])),
+        (at(OWN, 2, 0, -1, 1), early_opposite),
+        (at(OTHERS, 0, 0, -1, 1) + at(OWN + OTHERS, 0, 2) + at(OTHERS, -1, 0) + at(OTHERS, 1, 0), first),
+        (at(OTHERS, -1, -1, 1), near_sides[0]),
+        (at(OTHERS, 1, -1, 1), near_sides[1]),
+        (at(OWN + OTHERS, -1, 2) + at(OWN + OTHERS, 1, 2) + at(OTHERS, 2, 0), middle),
+        (ends[: len(ends) // 4], near_opposite[0]),
+        (ends[len(ends) // 4 :], near_opposite[1]),
+        (at(OWN + OTHERS, 2, 2), far_opposite),
+    )
 
 
 def arrange_kernel(layout, *refs):
     in_refs, out_refs = refs[: -len(layout)], refs[-len(layout) :]
     depth = in_refs[0].shape[1]
     for blocks, out_ref in zip(layout, out_refs):
-        for i, (u, v, dcore, place) in enumerate(blocks):
+        for i, (u, v, dcore, dy) in enumerate(blocks):
             first, second = (u, v) if dcore == 0 else (v, u)
             chip = OFFSETS.index(second) * SIDE + OFFSETS.index(first)
-            out_ref[i * depth : (i + 1) * depth, :] = in_refs[dcore][place * PLANE + chip]
+            source = in_refs[dcore][chip] if dy == 0 else in_refs[CORES + dcore][(dy - 1) * PLANE + chip]
+            out_ref[i * depth : (i + 1) * depth, :] = source
 
 
 def arrange(layout, *rows):
@@ -202,7 +210,7 @@
     return pl.pallas_call(
         lambda *refs: arrange_kernel(layout, *refs),
         out_shape=tuple(jax.ShapeDtypeStruct((len(blocks) * depth, chip_rows), rows[0].dtype) for blocks in layout),
-        in_specs=[VMEM] * CORES,
+        in_specs=[VMEM] * len(rows),
         out_specs=(VMEM,) * len(layout),
         compiler_params=pltpu.CompilerParams(vmem_limit_bytes=2 * size + (1 << 20)),
         cost_estimate=pl.CostEstimate(flops=0, bytes_accessed=2 * size, transcendentals=0),
@@ -265,8 +273,7 @@
     rows = regroup(rows)
     rows = along_line(rows, 1)
     rows = join(rows)
-    early = gathered_briefly(windows[0])
-    parts = gathered(others)
+    parts = gathered(windows[0], others)
 
     left, right = along_y(rows, 1), along_y(rows, -1)
     half = PLANE // 2
@@ -278,14 +285,11 @@
     def product(weight, block):
         return lax.dot_general(weight, block, (((0,), (0,)), ((), ())), preferred_element_type=jnp.float32)
 
-    layout = [[(u, v, dcore, dy) for u, v in offsets for dcore, dy in OWN] for offsets, _ in early]
-    weights = arrange(layout, rows, other_rows)
-    tile = product(weights[0], early[0][1])
-    layout = [[(u, v, dcore, dy - 1) for u, v in offsets for dcore, dy in OTHERS] for offsets, _ in parts]
-    weights = (*arrange(layout, rest, other_rest), weights[1])
-    blocks = [block for _, block in parts] + [early[1][1]]
-    for i in (1, 2, len(parts), 0, 3, 4, 5):
-        tile = lax.optimization_barrier(tile + product(weights[i], blocks[i]))
+    weights = arrange([terms for terms, _ in parts[:2]], rows, other_rows)
+    weights += arrange([terms for terms, _ in parts[2:]], rows, other_rows, rest, other_rest)
+    tile = product(weights[0], parts[0][1])
+    for i in (3, 4, 1, 2, 6, 7, 5, 8):
+        tile = lax.optimization_barrier(tile + product(weights[i], parts[i][1]))
 
     kept, sent = halve(tile)
     return assemble(kept, swap_cores(sent), basis // SIDE)

time: 198 us -> 197 us (level)
  starting transfers between devices: 63.3 us -> 60.8 us
    ppermute x7, waiting for transfers between devices: 23.1 us -> 16.9 us  [along_y(): lax.ppermute(block, 'y', [(i, (i + step) % SIDE) for i in range(SIDE)])]
    ppermute x25, waiting for transfers between devices: 84.9 us -> 90.4 us  [along_plane(): return lax.ppermute(block, ('x', 'z', 'core'), route)]
    ppermute x4, starting transfers between devices: 27.3 us -> 23.4 us  [swap_cores(): return lax.ppermute(block, 'core', [(0, 1), (1, 0)])]
    dot_general x8 -> x9, matrix products: 14.1 us -> 14.9 us  [product(): lax.dot_general(weight, block, (((0,), (0,)), ((), ())), preferred_elemen...]
  transfers between devices with their start and end apart: 36 -> 36, of which waited for: 18 -> 19; matrix products, arithmetic and copies ran while one was open for 7% -> 8% of each run, Pallas kernels for 1% -> 1%
where the time goes in v4:
time: 197 us
  waiting for transfers between devices  112 us (57%)
  starting transfers between devices  60.8 us (31%)
  matrix products  14.9 us (8%)
  Pallas kernels  5.3 us (3%)
  local copies, waits for them, and re-layouts  2.08 us (1%)
  other arithmetic  2.01 us (1%)
    ppermute x25, waiting for transfers between devices, along_plane(): return lax.ppermute(block, ('x', 'z', 'core'), route)  90.4 us
    ppermute x25, starting transfers between devices, along_plane(): return lax.ppermute(block, ('x', 'z', 'core'), route)  25.9 us
    ppermute x4, starting transfers between devices, swap_cores(): return lax.ppermute(block, 'core', [(0, 1), (1, 0)])  23.4 us
    ppermute x7, waiting for transfers between devices, along_y(): lax.ppermute(block, 'y', [(i, (i + step) % SIDE) for i in range(SIDE)])  16.9 us
    dot_general x9, matrix products, product(): lax.dot_general(weight, block, (((0,), (0,)), ((), ())), preferred_elemen...  14.9 us
    ppermute x7, starting transfers between devices, along_y(): lax.ppermute(block, 'y', [(i, (i + step) % SIDE) for i in range(SIDE)])  11.5 us
    ppermute x4, waiting for transfers between devices, swap_cores(): return lax.ppermute(block, 'core', [(0, 1), (1, 0)])  4.57 us
  transfers between devices with their start and end apart: 36, of which 19 were waited for; matrix products, arithmetic and copies ran while one was open for 8% of the time, Pallas kernels for 1%

profile of v4, /device:TPU:1, one launch (start us, length us, event | category | flops | bytes accessed | tf_op | source)
XLA Modules:
  0.0 197.2 jit_solution(4780319529225045422)
XLA Ops:
  3.0 2.5 %collective-permute-start = (bf16[4,48,624]{2,1,0:T(8,128)(2,1)S(1)}, bf16[4,48,624]{2,1,0:T(8,128)(2,1)S(1)}, u32[]{:S(2)}, u32[]{:S(2)}) collective-permute-start(bf16[4,48,624]{2,1,0:T(8,128)(2,1)S(1)} %get-tuple-element.34), channel_id=1, source_target_pairs={{0,8},{1,3},{2,10},{3,5},{4,12},{5,7},{6,14},{7,1},{8,16},{9,11},{... | collective-permute-start | bytes 718856 | tf_op jit(solution)/shard_map/ppermute | solution.py:32
  5.6 2.2 %collective-permute-start.1 = (bf16[4,48,624]{2,1,0:T(8,128)(2,1)S(1)}, bf16[4,48,624]{2,1,0:T(8,128)(2,1)S(1)}, u32[]{:S(2)}, u32[]{:S(2)}) collective-permute-start(bf16[4,48,624]{2,1,0:T(8,128)(2,1)S(1)} %get-tuple-element.35), channel_id=1, source_target_pairs={{0,24},{1,7},{2,26},{3,1},{4,28},{5,3},{6,30},{7,5},{8,0},{9,15},{... | collective-permute-start | bytes 718856 | tf_op jit(solution)/shard_map/ppermute | solution.py:32
  9.0 2.5 %collective-permute-done.refs_1_ = bf16[4,48,624]{2,1,0:T(8,128)(2,1)S(1)} collective-permute-done((bf16[4,48,624]{2,1,0:T(8,128)(2,1)S(1)}, bf16[4,48,624]{2,1,0:T(8,128)(2,1)S(1)}, u32[]{:S(2)}, u32[]{:S(2)}) %collective-permute-start) | collective-permute-done | bytes 239648 | tf_op jit(solution)/shard_map/ppermute | solution.py:32
  11.5 2.0 %collective-permute-done.1.refs_2_ = bf16[4,48,624]{2,1,0:T(8,128)(2,1)S(1)} collective-permute-done((bf16[4,48,624]{2,1,0:T(8,128)(2,1)S(1)}, bf16[4,48,624]{2,1,0:T(8,128)(2,1)S(1)}, u32[]{:S(2)}, u32[]{:S(2)}) %collective-permute-start.1) | collective-permute-done | bytes 239648 | tf_op jit(solution)/shard_map/ppermute | solution.py:32
  13.5 1.7 collective-permute-done.2.refs_3_
  16.4 1.6 collective-permute-start.4
  19.4 2.5 %collective-permute-done.3.refs_1_ = bf16[4,48,624]{2,1,0:T(8,128)(2,1)S(1)} collective-permute-done((bf16[4,48,624]{2,1,0:T(8,128)(2,1)S(1)}, bf16[4,48,624]{2,1,0:T(8,128)(2,1)S(1)}, u32[]{:S(2)}, u32[]{:S(2)}) %collective-permute-start.3) | collective-permute-done | bytes 239648 | tf_op jit(solution)/shard_map/ppermute | solution.py:32
  21.9 1.9 collective-permute-done.4.refs_2_
  28.4 3.1 %collective-permute-start.7 = (bf16[4,48,1280]{2,1,0:T(8,128)(2,1)S(1)}, bf16[4,48,1280]{2,1,0:T(8,128)(2,1)S(1)}, u32[]{:S(2)}, u32[]{:S(2)}) collective-permute-start(bf16[4,48,1280]{2,1,0:T(8,128)(2,1)S(1)} %get-tuple-element.46), channel_id=1, source_target_pairs={{0,1},{1,0},{2,3},{3,2},{4,5},{5,4},{6,7},{7,6},{8,9},{9,8},{10,11... | collective-permute-start | bytes 1474568 | tf_op jit(solution)/shard_map/ppermute | solution.py:22
  33.0 1.6 collective-permute-start.17
  35.6 16.8 %collective-permute-done.17.refs_0_ = bf16[96,1280]{1,0:T(8,128)(2,1)S(1)} collective-permute-done((bf16[96,1280]{1,0:T(8,128)(2,1)S(1)}, bf16[96,1280]{1,0:T(8,128)(2,1)S(1)}, u32[]{:S(2)}, u32[]{:S(2)}) %collective-permute-start.17) | collective-permute-done | bytes 245792 | tf_op jit(solution)/shard_map/ppermute | solution.py:18
  55.5 4.3 %collective-permute-start.15 = (bf16[8,48,624]{2,1,0:T(8,128)(2,1)S(1)}, bf16[8,48,624]{2,1,0:T(8,128)(2,1)S(1)}, u32[]{:S(2)}, u32[]{:S(2)}) collective-permute-start(bf16[8,48,624]{2,1,0:T(8,128)(2,1)S(1)} %slice.25), channel_id=1, source_target_pairs={{0,96},{32,0},{64,32},{96,64},{1,97},{33,1},{65,33},{97,65},{2,98}... | collective-permute-start | bytes 1437704 | tf_op jit(solution)/shard_map/ppermute | solution.py:18
  59.8 2.2 %collective-permute-start.9 = (bf16[96,1280]{1,0:T(8,128)(2,1)S(1)}, bf16[96,1280]{1,0:T(8,128)(2,1)S(1)}, u32[]{:S(2)}, u32[]{:S(2)}) collective-permute-start(bf16[96,1280]{1,0:T(8,128)(2,1)S(1)} %get-tuple-element.47.refs_0_), channel_id=1, source_target_pairs={{0,24},{1,7},{2,26},{3,1},{4,28},{5,3},{6,30},{7,5},{8,0},{9,15},{... | collective-permute-start | bytes 737288 | tf_op jit(solution)/shard_map/ppermute | solution.py:32
  62.2 3.0 %collective-permute-done.9.refs_2_ = bf16[96,1280]{1,0:T(8,128)(2,1)S(1)} collective-permute-done((bf16[96,1280]{1,0:T(8,128)(2,1)S(1)}, bf16[96,1280]{1,0:T(8,128)(2,1)S(1)}, u32[]{:S(2)}, u32[]{:S(2)}) %collective-permute-start.9) | collective-permute-done | bytes 245792 | tf_op jit(solution)/shard_map/ppermute | solution.py:32
  65.2 3.4 %collective-permute-start.21 = (bf16[288,1280]{1,0:T(8,128)(2,1)S(1)}, bf16[288,1280]{1,0:T(8,128)(2,1)S(1)}, u32[]{:S(2)}, u32[]{:S(2)}) collective-permute-start(bf16[288,1280]{1,0:T(8,128)(2,1)S(1)} %join.14.refs_0_), channel_id=1, source_target_pairs={{0,24},{1,7},{2,26},{3,1},{4,28},{5,3},{6,30},{7,5},{8,0},{9,15},{... | collective-permute-start | bytes 2211848 | tf_op jit(solution)/shard_map/ppermute | solution.py:32
  69.5 9.4 %collective-permute-start.16 = (bf16[48,48,624]{2,1,0:T(8,128)(2,1)S(1)}, bf16[48,48,624]{2,1,0:T(8,128)(2,1)S(1)}, u32[]{:S(2)}, u32[]{:S(2)}) collective-permute-start(bf16[48,48,624]{2,1,0:T(8,128)(2,1)S(1)} %join.13.refs_2_), channel_id=1, source_target_pairs={{0,1},{1,0},{2,3},{3,2},{4,5},{5,4},{6,7},{7,6},{8,9},{9,8},{10,11... | collective-permute-start | bytes 8626184 | tf_op jit(solution)/shard_map/ppermute | solution.py:22
  81.8 4.2 %collective-permute-done.10.refs_1_ = bf16[288,1280]{1,0:T(8,128)(2,1)S(1)} collective-permute-done((bf16[288,1280]{1,0:T(8,128)(2,1)S(1)}, bf16[288,1280]{1,0:T(8,128)(2,1)S(1)}, u32[]{:S(2)}, u32[]{:S(2)}) %collective-permute-start.10) | collective-permute-done | bytes 737312 | tf_op jit(solution)/shard_map/ppermute | solution.py:32
  86.3 8.1 %collective-permute-done.11.refs_2_ = bf16[288,1280]{1,0:T(8,128)(2,1)S(1)} collective-permute-done((bf16[288,1280]{1,0:T(8,128)(2,1)S(1)}, bf16[288,1280]{1,0:T(8,128)(2,1)S(1)}, u32[]{:S(2)}, u32[]{:S(2)}) %collective-permute-start.11) | collective-permute-done | bytes 737312 | tf_op jit(solution)/shard_map/ppermute | solution.py:32
  96.3 6.0 %collective-permute-done.28.refs_4_ = bf16[288,1280]{1,0:T(8,128)(2,1)S(1)} collective-permute-done((bf16[288,1280]{1,0:T(8,128)(2,1)S(1)}, bf16[288,1280]{1,0:T(8,128)(2,1)S(1)}, u32[]{:S(2)}, u32[]{:S(2)}) %collective-permute-start.28) | collective-permute-done | bytes 737312 | tf_op jit(solution)/shard_map/ppermute | solution.py:32
  102.3 3.4 %collective-permute-start.23 = (bf16[576,1280]{1,0:T(8,128)(2,1)S(1)}, bf16[576,1280]{1,0:T(8,128)(2,1)S(1)}, u32[]{:S(2)}, u32[]{:S(2)}) collective-permute-start(bf16[576,1280]{1,0:T(8,128)(2,1)S(1)} %join.15.refs_1_), channel_id=1, source_target_pairs={{0,6},{1,25},{2,0},{3,27},{4,2},{5,29},{6,4},{7,31},{8,14},{9,1},{... | collective-permute-start | bytes 4423688 | tf_op jit(solution)/shard_map/ppermute | solution.py:32
  105.8 20.8 %collective-permute-done.24.refs_0_ = bf16[144,1280]{1,0:T(8,128)(2,1)S(1)} collective-permute-done((bf16[144,1280]{1,0:T(8,128)(2,1)S(1)}, bf16[144,1280]{1,0:T(8,128)(2,1)S(1)}, u32[]{:S(2)}, u32[]{:S(2)}) %collective-permute-start.24) | collective-permute-done | bytes 368672 | tf_op jit(solution)/shard_map/ppermute | solution.py:32
  126.8 6.4 %collective-permute-done.25.refs_1_ = bf16[144,1280]{1,0:T(8,128)(2,1)S(1)} collective-permute-done((bf16[144,1280]{1,0:T(8,128)(2,1)S(1)}, bf16[144,1280]{1,0:T(8,128)(2,1)S(1)}, u32[]{:S(2)}, u32[]{:S(2)}) %collective-permute-start.25) | collective-permute-done | bytes 368672 | tf_op jit(solution)/shard_map/ppermute | solution.py:32
  135.0 2.0 %collective-permute-start.29 = (bf16[144,1280]{1,0:T(8,128)(2,1)S(1)}, bf16[144,1280]{1,0:T(8,128)(2,1)S(1)}, u32[]{:S(2)}, u32[]{:S(2)}) collective-permute-start(bf16[144,1280]{1,0:T(8,128)(2,1)S(1)} %slice.28), channel_id=1, source_target_pairs={{0,2},{1,9},{2,4},{3,11},{4,6},{5,13},{6,0},{7,15},{8,10},{9,17},{... | collective-permute-start | bytes 1105928 | tf_op jit(solution)/shard_map/ppermute | solution.py:32
  137.1 18.5 %collective-permute-done.33.refs_2_ = bf16[288,1280]{1,0:T(8,128)(2,1)S(1)} collective-permute-done((bf16[288,1280]{1,0:T(8,128)(2,1)S(1)}, bf16[288,1280]{1,0:T(8,128)(2,1)S(1)}, u32[]{:S(2)}, u32[]{:S(2)}) %collective-permute-start.33) | collective-permute-done | bytes 737312 | tf_op jit(solution)/shard_map/ppermute | solution.py:32
  156.3 3.7 %fusion.3 = f32[624,1280]{1,0:T(8,128)S(1)} fusion(bf16[1824,624]{1,0:T(8,128)(2,1)S(1)} %get-tuple-element.54, bf16[1824,1280]{1,0:T(8,128)(2,1)S(1)} %join.18), kind=kOutput, calls=%fused_computation.6 | convolution fusion | flops 2913730560 | bytes 10140672 | tf_op jit(solution)/shard_map/dot_general | solution.py:286
  161.5 2.0 %convolution_add_fusion.1 = f32[624,1280]{1,0:T(8,128)S(1)} fusion(f32[624,1280]{1,0:T(8,128)S(1)} %fusion, bf16[864,624]{1,0:T(8,128)(2,1)S(1)} %get-tuple-element.41, bf16[864,1280]{1,0:T(8,128)(2,1)S(1)} %join.12), kind=kOutput, calls=%fused_computation.1 | convolution fusion | flops 1380986880 | bytes 9679872 | tf_op jit(solution)/shard_map/dot_general | solution.py:286
  167.2 3.0 %collective-permute-done.30 = bf16[432,1280]{1,0:T(8,128)(2,1)S(1)} collective-permute-done((bf16[432,1280]{1,0:T(8,128)(2,1)S(1)}, bf16[432,1280]{1,0:T(8,128)(2,1)S(1)}, u32[]{:S(2)}, u32[]{:S(2)}) %collective-permute-start.30) | collective-permute-done | bytes 1105952 | tf_op jit(solution)/shard_map/ppermute | solution.py:32
  171.6 2.6 %convolution_add_fusion.2 = f32[624,1280]{1,0:T(8,128)S(1)} fusion(f32[624,1280]{1,0:T(8,128)S(1)} %add.29, bf16[1056,624]{1,0:T(8,128)(2,1)S(1)} %get-tuple-element.57, bf16[1056,1280]{1,0:T(8,128)(2,1)S(1)} %join.19), kind=kOutput, calls=%fused_computation.2 | convolution fusion | flops 1687695360 | bytes 10411008 | tf_op jit(solution)/shard_map/dot_general | solution.py:286
  174.2 6.5 %collective-permute-done.34 = bf16[384,1280]{1,0:T(8,128)(2,1)S(1)} collective-permute-done((bf16[384,1280]{1,0:T(8,128)(2,1)S(1)}, bf16[384,1280]{1,0:T(8,128)(2,1)S(1)}, u32[]{:S(2)}, u32[]{:S(2)}) %collective-permute-start.34) | collective-permute-done | bytes 983072 | tf_op jit(solution)/shard_map/ppermute | solution.py:32
  182.0 10.2 %collective-permute-start.35 = (f32[312,1280]{1,0:T(8,128)S(1)}, f32[312,1280]{1,0:T(8,128)S(1)}, u32[]{:S(2)}, u32[]{:S(2)}) collective-permute-start(f32[312,1280]{1,0:T(8,128)S(1)} %get-tuple-element.60), channel_id=1, source_target_pairs={{0,1},{1,0},{2,3},{3,2},{4,5},{5,4},{6,7},{7,6},{8,9},{9,8},{10,11... | collective-permute-start | bytes 4792328 | tf_op jit(solution)/shard_map/ppermute | solution.py:22
  192.2 3.1 %collective-permute-done.35.got_ref = f32[312,1280]{1,0:T(8,128)S(1)} collective-permute-done((f32[312,1280]{1,0:T(8,128)S(1)}, f32[312,1280]{1,0:T(8,128)S(1)}, u32[]{:S(2)}, u32[]{:S(2)}) %collective-permute-start.35) | collective-permute-done | bytes 1597472 | tf_op jit(solution)/shard_map/ppermute | solution.py:22
  195.3 1.9 assemble.1
  (81 shorter events, 33.6 us)
Async XLA Ops:
  3.0 8.5 %collective-permute-start = (bf16[4,48,624]{2,1,0:T(8,128)(2,1)S(1)}, bf16[4,48,624]{2,1,0:T(8,128)(2,1)S(1)}, u32[]{:S(2)}, u32[]{:S(2)}) collective-permute-start(bf16[4,48,624]{2,1,0:T(8,128)(2,1)S(1)} %get-tuple-element.34), channel_id=1, source_target_pairs={{0,8},{1,3},{2,10},{3,5},{4,12},{5,7},{6,14},{7,1},{8,16},{9,11},{... | collective-permute-start | bytes 718856 | tf_op jit(solution)/shard_map/ppermute | solution.py:32
  5.6 8.0 %collective-permute-start.1 = (bf16[4,48,624]{2,1,0:T(8,128)(2,1)S(1)}, bf16[4,48,624]{2,1,0:T(8,128)(2,1)S(1)}, u32[]{:S(2)}, u32[]{:S(2)}) collective-permute-start(bf16[4,48,624]{2,1,0:T(8,128)(2,1)S(1)} %get-tuple-element.35), channel_id=1, source_target_pairs={{0,24},{1,7},{2,26},{3,1},{4,28},{5,3},{6,30},{7,5},{8,0},{9,15},{... | collective-permute-start | bytes 718856 | tf_op jit(solution)/shard_map/ppermute | solution.py:32
  7.8 7.5 %collective-permute-start.2 = (bf16[4,48,624]{2,1,0:T(8,128)(2,1)S(1)}, bf16[4,48,624]{2,1,0:T(8,128)(2,1)S(1)}, u32[]{:S(2)}, u32[]{:S(2)}) collective-permute-start(bf16[4,48,624]{2,1,0:T(8,128)(2,1)S(1)} %get-tuple-element.36), channel_id=1, source_target_pairs={{0,16},{1,5},{2,18},{3,7},{4,20},{5,1},{6,22},{7,3},{8,24},{9,13},... | collective-permute-start | bytes 718856 | tf_op jit(solution)/shard_map/ppermute | solution.py:32
  16.4 7.4 %collective-permute-start.4 = (bf16[4,48,624]{2,1,0:T(8,128)(2,1)S(1)}, bf16[4,48,624]{2,1,0:T(8,128)(2,1)S(1)}, u32[]{:S(2)}, u32[]{:S(2)}) collective-permute-start(bf16[4,48,624]{2,1,0:T(8,128)(2,1)S(1)} %get-tuple-element.39), channel_id=1, source_target_pairs={{0,6},{1,25},{2,0},{3,27},{4,2},{5,29},{6,4},{7,31},{8,14},{9,1},{... | collective-permute-start | bytes 718856 | tf_op jit(solution)/shard_map/ppermute | solution.py:32
  18.1 7.3 %collective-permute-start.5 = (bf16[4,48,624]{2,1,0:T(8,128)(2,1)S(1)}, bf16[4,48,624]{2,1,0:T(8,128)(2,1)S(1)}, u32[]{:S(2)}, u32[]{:S(2)}) collective-permute-start(bf16[4,48,624]{2,1,0:T(8,128)(2,1)S(1)} %get-tuple-element.40), channel_id=1, source_target_pairs={{0,4},{1,17},{2,6},{3,19},{4,0},{5,21},{6,2},{7,23},{8,12},{9,25},... | collective-permute-start | bytes 718856 | tf_op jit(solution)/shard_map/ppermute | solution.py:32
  25.5 28.3 %collective-permute-start.13 = (bf16[16,48,624]{2,1,0:T(8,128)(2,1)S(1)}, bf16[16,48,624]{2,1,0:T(8,128)(2,1)S(1)}, u32[]{:S(2)}, u32[]{:S(2)}) collective-permute-start(bf16[16,48,624]{2,1,0:T(8,128)(2,1)S(1)} %join.10.refs_0_), channel_id=1, source_target_pairs={{0,32},{32,64},{64,96},{96,0},{1,33},{33,65},{65,97},{97,1},{2,34}... | collective-permute-start | bytes 2875400 | tf_op jit(solution)/shard_map/ppermute | solution.py:18
  26.9 27.5 %collective-permute-start.12 = (bf16[16,48,624]{2,1,0:T(8,128)(2,1)S(1)}, bf16[16,48,624]{2,1,0:T(8,128)(2,1)S(1)}, u32[]{:S(2)}, u32[]{:S(2)}) collective-permute-start(bf16[16,48,624]{2,1,0:T(8,128)(2,1)S(1)} %join.10.refs_0_), channel_id=1, source_target_pairs={{0,96},{32,0},{64,32},{96,64},{1,97},{33,1},{65,33},{97,65},{2,98}... | collective-permute-start | bytes 2875400 | tf_op jit(solution)/shard_map/ppermute | solution.py:18
  33.0 19.4 %collective-permute-start.17 = (bf16[96,1280]{1,0:T(8,128)(2,1)S(1)}, bf16[96,1280]{1,0:T(8,128)(2,1)S(1)}, u32[]{:S(2)}, u32[]{:S(2)}) collective-permute-start(bf16[96,1280]{1,0:T(8,128)(2,1)S(1)} %get-tuple-element.49), channel_id=1, source_target_pairs={{0,96},{32,0},{64,32},{96,64},{1,97},{33,1},{65,33},{97,65},{2,98}... | collective-permute-start | bytes 737288 | tf_op jit(solution)/shard_map/ppermute | solution.py:18
  34.6 44.3 %collective-permute-start.6 = (bf16[16,48,624]{2,1,0:T(8,128)(2,1)S(1)}, bf16[16,48,624]{2,1,0:T(8,128)(2,1)S(1)}, u32[]{:S(2)}, u32[]{:S(2)}) collective-permute-start(bf16[16,48,624]{2,1,0:T(8,128)(2,1)S(1)} %join.10.refs_0_), channel_id=1, source_target_pairs={{0,1},{1,0},{2,3},{3,2},{4,5},{5,4},{6,7},{7,6},{8,9},{9,8},{10,11... | collective-permute-start | bytes 2875400 | tf_op jit(solution)/shard_map/ppermute | solution.py:22
  35.3 20.2 %collective-permute-start.18 = (bf16[96,1280]{1,0:T(8,128)(2,1)S(1)}, bf16[96,1280]{1,0:T(8,128)(2,1)S(1)}, u32[]{:S(2)}, u32[]{:S(2)}) collective-permute-start(bf16[96,1280]{1,0:T(8,128)(2,1)S(1)} %get-tuple-element.50), channel_id=1, source_target_pairs={{0,64},{32,96},{64,0},{96,32},{1,65},{33,97},{65,1},{97,33},{2,66}... | collective-permute-start | bytes 737288 | tf_op jit(solution)/shard_map/ppermute | solution.py:18
  52.5 7.4 %collective-permute-start.19 = (bf16[96,1280]{1,0:T(8,128)(2,1)S(1)}, bf16[96,1280]{1,0:T(8,128)(2,1)S(1)}, u32[]{:S(2)}, u32[]{:S(2)}) collective-permute-start(bf16[96,1280]{1,0:T(8,128)(2,1)S(1)} %get-tuple-element.51), channel_id=1, source_target_pairs={{0,32},{32,64},{64,96},{96,0},{1,33},{33,65},{65,97},{97,1},{2,34}... | collective-permute-start | bytes 737288 | tf_op jit(solution)/shard_map/ppermute | solution.py:18
  53.8 8.3 %collective-permute-start.8 = (bf16[96,1280]{1,0:T(8,128)(2,1)S(1)}, bf16[96,1280]{1,0:T(8,128)(2,1)S(1)}, u32[]{:S(2)}, u32[]{:S(2)}) collective-permute-start(bf16[96,1280]{1,0:T(8,128)(2,1)S(1)} %get-tuple-element.47.refs_0_), channel_id=1, source_target_pairs={{0,8},{1,3},{2,10},{3,5},{4,12},{5,7},{6,14},{7,1},{8,16},{9,11},{... | collective-permute-start | bytes 737288 | tf_op jit(solution)/shard_map/ppermute | solution.py:32
  54.4 14.2 %collective-permute-start.14 = (bf16[8,48,624]{2,1,0:T(8,128)(2,1)S(1)}, bf16[8,48,624]{2,1,0:T(8,128)(2,1)S(1)}, u32[]{:S(2)}, u32[]{:S(2)}) collective-permute-start(bf16[8,48,624]{2,1,0:T(8,128)(2,1)S(1)} %slice.24), channel_id=1, source_target_pairs={{0,32},{32,64},{64,96},{96,0},{1,33},{33,65},{65,97},{97,1},{2,34}... | collective-permute-start | bytes 1437704 | tf_op jit(solution)/shard_map/ppermute | solution.py:18
  55.5 13.8 %collective-permute-start.15 = (bf16[8,48,624]{2,1,0:T(8,128)(2,1)S(1)}, bf16[8,48,624]{2,1,0:T(8,128)(2,1)S(1)}, u32[]{:S(2)}, u32[]{:S(2)}) collective-permute-start(bf16[8,48,624]{2,1,0:T(8,128)(2,1)S(1)} %slice.25), channel_id=1, source_target_pairs={{0,96},{32,0},{64,32},{96,64},{1,97},{33,1},{65,33},{97,65},{2,98}... | collective-permute-start | bytes 1437704 | tf_op jit(solution)/shard_map/ppermute | solution.py:18
  62.1 16.9 %collective-permute-start.20 = (bf16[288,1280]{1,0:T(8,128)(2,1)S(1)}, bf16[288,1280]{1,0:T(8,128)(2,1)S(1)}, u32[]{:S(2)}, u32[]{:S(2)}) collective-permute-start(bf16[288,1280]{1,0:T(8,128)(2,1)S(1)} %join.14.refs_0_), channel_id=1, source_target_pairs={{0,8},{1,3},{2,10},{3,5},{4,12},{5,7},{6,14},{7,1},{8,16},{9,11},{... | collective-permute-start | bytes 2211848 | tf_op jit(solution)/shard_map/ppermute | solution.py:32
  65.2 15.2 %collective-permute-start.21 = (bf16[288,1280]{1,0:T(8,128)(2,1)S(1)}, bf16[288,1280]{1,0:T(8,128)(2,1)S(1)}, u32[]{:S(2)}, u32[]{:S(2)}) collective-permute-start(bf16[288,1280]{1,0:T(8,128)(2,1)S(1)} %join.14.refs_0_), channel_id=1, source_target_pairs={{0,24},{1,7},{2,26},{3,1},{4,28},{5,3},{6,30},{7,5},{8,0},{9,15},{... | collective-permute-start | bytes 2211848 | tf_op jit(solution)/shard_map/ppermute | solution.py:32
  68.6 17.4 %collective-permute-start.10 = (bf16[288,1280]{1,0:T(8,128)(2,1)S(1)}, bf16[288,1280]{1,0:T(8,128)(2,1)S(1)}, u32[]{:S(2)}, u32[]{:S(2)}) collective-permute-start(bf16[288,1280]{1,0:T(8,128)(2,1)S(1)} %join.11.refs_0_), channel_id=1, source_target_pairs={{0,2},{1,9},{2,4},{3,11},{4,6},{5,13},{6,0},{7,15},{8,10},{9,17},{... | collective-permute-start | bytes 2211848 | tf_op jit(solution)/shard_map/ppermute | solution.py:32
  69.5 86.3 %collective-permute-start.16 = (bf16[48,48,624]{2,1,0:T(8,128)(2,1)S(1)}, bf16[48,48,624]{2,1,0:T(8,128)(2,1)S(1)}, u32[]{:S(2)}, u32[]{:S(2)}) collective-permute-start(bf16[48,48,624]{2,1,0:T(8,128)(2,1)S(1)} %join.13.refs_2_), channel_id=1, source_target_pairs={{0,1},{1,0},{2,3},{3,2},{4,5},{5,4},{6,7},{7,6},{8,9},{9,8},{10,11... | collective-permute-start | bytes 8626184 | tf_op jit(solution)/shard_map/ppermute | solution.py:22
  79.0 15.5 %collective-permute-start.11 = (bf16[288,1280]{1,0:T(8,128)(2,1)S(1)}, bf16[288,1280]{1,0:T(8,128)(2,1)S(1)}, u32[]{:S(2)}, u32[]{:S(2)}) collective-permute-start(bf16[288,1280]{1,0:T(8,128)(2,1)S(1)} %join.11.refs_0_), channel_id=1, source_target_pairs={{0,6},{1,25},{2,0},{3,27},{4,2},{5,29},{6,4},{7,31},{8,14},{9,1},{... | collective-permute-start | bytes 2211848 | tf_op jit(solution)/shard_map/ppermute | solution.py:32
  79.0 17.4 %collective-permute-start.27 = (bf16[288,1280]{1,0:T(8,128)(2,1)S(1)}, bf16[288,1280]{1,0:T(8,128)(2,1)S(1)}, u32[]{:S(2)}, u32[]{:S(2)}) collective-permute-start(bf16[288,1280]{1,0:T(8,128)(2,1)S(1)} %join.14.refs_0_), channel_id=1, source_target_pairs={{0,2},{1,9},{2,4},{3,11},{4,6},{5,13},{6,0},{7,15},{8,10},{9,17},{... | collective-permute-start | bytes 2211848 | tf_op jit(solution)/shard_map/ppermute | solution.py:32
  80.4 21.9 %collective-permute-start.28 = (bf16[288,1280]{1,0:T(8,128)(2,1)S(1)}, bf16[288,1280]{1,0:T(8,128)(2,1)S(1)}, u32[]{:S(2)}, u32[]{:S(2)}) collective-permute-start(bf16[288,1280]{1,0:T(8,128)(2,1)S(1)} %join.14.refs_0_), channel_id=1, source_target_pairs={{0,6},{1,25},{2,0},{3,27},{4,2},{5,29},{6,4},{7,31},{8,14},{9,1},{... | collective-permute-start | bytes 2211848 | tf_op jit(solution)/shard_map/ppermute | solution.py:32
  86.0 47.3 %collective-permute-start.22 = (bf16[576,1280]{1,0:T(8,128)(2,1)S(1)}, bf16[576,1280]{1,0:T(8,128)(2,1)S(1)}, u32[]{:S(2)}, u32[]{:S(2)}) collective-permute-start(bf16[576,1280]{1,0:T(8,128)(2,1)S(1)} %join.15.refs_1_), channel_id=1, source_target_pairs={{0,2},{1,9},{2,4},{3,11},{4,6},{5,13},{6,0},{7,15},{8,10},{9,17},{... | collective-permute-start | bytes 4423688 | tf_op jit(solution)/shard_map/ppermute | solution.py:32
  94.4 32.4 %collective-permute-start.26 = (bf16[384,1280]{1,0:T(8,128)(2,1)S(1)}, bf16[384,1280]{1,0:T(8,128)(2,1)S(1)}, u32[]{:S(2)}, u32[]{:S(2)}) collective-permute-start(bf16[384,1280]{1,0:T(8,128)(2,1)S(1)} %join.17), channel_id=1, source_target_pairs={{0,8},{1,3},{2,10},{3,5},{4,12},{5,7},{6,14},{7,1},{8,16},{9,11},{... | collective-permute-start | bytes 2949128 | tf_op jit(solution)/shard_map/ppermute | solution.py:32
  96.3 30.3 %collective-permute-start.24 = (bf16[144,1280]{1,0:T(8,128)(2,1)S(1)}, bf16[144,1280]{1,0:T(8,128)(2,1)S(1)}, u32[]{:S(2)}, u32[]{:S(2)}) collective-permute-start(bf16[144,1280]{1,0:T(8,128)(2,1)S(1)} %slice.26), channel_id=1, source_target_pairs={{0,2},{1,9},{2,4},{3,11},{4,6},{5,13},{6,0},{7,15},{8,10},{9,17},{... | collective-permute-start | bytes 1105928 | tf_op jit(solution)/shard_map/ppermute | solution.py:32
  102.3 32.7 %collective-permute-start.23 = (bf16[576,1280]{1,0:T(8,128)(2,1)S(1)}, bf16[576,1280]{1,0:T(8,128)(2,1)S(1)}, u32[]{:S(2)}, u32[]{:S(2)}) collective-permute-start(bf16[576,1280]{1,0:T(8,128)(2,1)S(1)} %join.15.refs_1_), channel_id=1, source_target_pairs={{0,6},{1,25},{2,0},{3,27},{4,2},{5,29},{6,4},{7,31},{8,14},{9,1},{... | collective-permute-start | bytes 4423688 | tf_op jit(solution)/shard_map/ppermute | solution.py:32
  126.8 28.8 %collective-permute-start.32 = (bf16[384,1280]{1,0:T(8,128)(2,1)S(1)}, bf16[384,1280]{1,0:T(8,128)(2,1)S(1)}, u32[]{:S(2)}, u32[]{:S(2)}) collective-permute-start(bf16[384,1280]{1,0:T(8,128)(2,1)S(1)} %collective-permute-done.26.refs_2_), channel_id=1, source_target_pairs={{0,6},{1,25},{2,0},{3,27},{4,2},{5,29},{6,4},{7,31},{8,14},{9,1},{... | collective-permute-start | bytes 2949128 | tf_op jit(solution)/shard_map/ppermute | solution.py:32
  133.3 22.4 %collective-permute-start.31 = (bf16[384,1280]{1,0:T(8,128)(2,1)S(1)}, bf16[384,1280]{1,0:T(8,128)(2,1)S(1)}, u32[]{:S(2)}, u32[]{:S(2)}) collective-permute-start(bf16[384,1280]{1,0:T(8,128)(2,1)S(1)} %collective-permute-done.26.refs_2_), channel_id=1, source_target_pairs={{0,2},{1,9},{2,4},{3,11},{4,6},{5,13},{6,0},{7,15},{8,10},{9,17},{... | collective-permute-start | bytes 2949128 | tf_op jit(solution)/shard_map/ppermute | solution.py:32
  133.3 22.3 %collective-permute-start.33 = (bf16[288,1280]{1,0:T(8,128)(2,1)S(1)}, bf16[288,1280]{1,0:T(8,128)(2,1)S(1)}, u32[]{:S(2)}, u32[]{:S(2)}) collective-permute-start(bf16[288,1280]{1,0:T(8,128)(2,1)S(1)} %collective-permute-done.27.refs_3_), channel_id=1, source_target_pairs={{0,2},{1,9},{2,4},{3,11},{4,6},{5,13},{6,0},{7,15},{8,10},{9,17},{... | collective-permute-start | bytes 2211848 | tf_op jit(solution)/shard_map/ppermute | solution.py:32
  135.0 31.2 %collective-permute-start.29 = (bf16[144,1280]{1,0:T(8,128)(2,1)S(1)}, bf16[144,1280]{1,0:T(8,128)(2,1)S(1)}, u32[]{:S(2)}, u32[]{:S(2)}) collective-permute-start(bf16[144,1280]{1,0:T(8,128)(2,1)S(1)} %slice.28), channel_id=1, source_target_pairs={{0,2},{1,9},{2,4},{3,11},{4,6},{5,13},{6,0},{7,15},{8,10},{9,17},{... | collective-permute-start | bytes 1105928 | tf_op jit(solution)/shard_map/ppermute | solution.py:32
  155.6 14.6 %collective-permute-start.30 = (bf16[432,1280]{1,0:T(8,128)(2,1)S(1)}, bf16[432,1280]{1,0:T(8,128)(2,1)S(1)}, u32[]{:S(2)}, u32[]{:S(2)}) collective-permute-start(bf16[432,1280]{1,0:T(8,128)(2,1)S(1)} %slice.29), channel_id=1, source_target_pairs={{0,6},{1,25},{2,0},{3,27},{4,2},{5,29},{6,4},{7,31},{8,14},{9,1},{... | collective-permute-start | bytes 3317768 | tf_op jit(solution)/shard_map/ppermute | solution.py:32
  155.6 25.1 %collective-permute-start.34 = (bf16[384,1280]{1,0:T(8,128)(2,1)S(1)}, bf16[384,1280]{1,0:T(8,128)(2,1)S(1)}, u32[]{:S(2)}, u32[]{:S(2)}) collective-permute-start(bf16[384,1280]{1,0:T(8,128)(2,1)S(1)} %collective-permute-done.32.refs_1_), channel_id=1, source_target_pairs={{0,6},{1,25},{2,0},{3,27},{4,2},{5,29},{6,4},{7,31},{8,14},{9,1},{... | collective-permute-start | bytes 2949128 | tf_op jit(solution)/shard_map/ppermute | solution.py:32
  182.0 13.3 %collective-permute-start.35 = (f32[312,1280]{1,0:T(8,128)S(1)}, f32[312,1280]{1,0:T(8,128)S(1)}, u32[]{:S(2)}, u32[]{:S(2)}) collective-permute-start(f32[312,1280]{1,0:T(8,128)S(1)} %get-tuple-element.60), channel_id=1, source_target_pairs={{0,1},{1,0},{2,3},{3,2},{4,5},{5,4},{6,7},{7,6},{8,9},{9,8},{10,11... | collective-permute-start | bytes 4792328 | tf_op jit(solution)/shard_map/ppermute | solution.py:22
  (6 other events, 25.1 us)

commit v5 on v4

--- a/solution.py
+++ b/solution.py
@@ -168,27 +168,30 @@
     near = join([before, after])
     both_before = join([early_before, before])
     far = along_plane(both_before, 0, 1)
-    near_sides = along_plane(near, 1, 1), along_plane(near, 1, -1)
+    near_right = along_plane(near, 1, -1)
+    far_sides = along_plane(far, 1, 1), along_plane(far, 1, -1)
+    near_left = along_plane(near, 1, 1)
     own_sides = along_plane(late, 1, 1), along_plane(late, 1, -1)
-    far_sides = along_plane(far, 1, 1), along_plane(far, 1, -1)
+    cut = late.shape[0] // 2
+    opposite_right = along_plane(near_right[cut:], 1, -1)
+    far_opposite = along_plane(far_sides[1], 1, -1)
+    opposite_left = along_plane(near_left[:cut], 1, 1)
     own_opposite = along_plane(own_sides[0], 1, 1)
-    cut = late.shape[0] // 2
-    near_opposite = along_plane(near_sides[0][:cut], 1, 1), along_plane(near_sides[1][cut:], 1, -1)
-    far_opposite = along_plane(far_sides[1], 1, -1)
 
     early_opposite = join(opposite)
     first = join([late, near, far, *own_sides])
-    middle = join([*far_sides, own_opposite])
+    end = join([opposite_left, own_opposite])
     ends = at(OTHERS, 2, -1, 1)
+    cut = len(ends) // 4
     return (
         (sum((at(OWN, v, 0, -1, 1) for v in (0, -1, 1)), ()), join([line, left, right])),
         (at(OWN, 2, 0, -1, 1), early_opposite),
         (at(OTHERS, 0, 0, -1, 1) + at(OWN + OTHERS, 0, 2) + at(OTHERS, -1, 0) + at(OTHERS, 1, 0), first),
-        (at(OTHERS, -1, -1, 1), near_sides[0]),
-        (at(OTHERS, 1, -1, 1), near_sides[1]),
-        (at(OWN + OTHERS, -1, 2) + at(OWN + OTHERS, 1, 2) + at(OTHERS, 2, 0), middle),
-        (ends[: len(ends) // 4], near_opposite[0]),
-        (ends[len(ends) // 4 :], near_opposite[1]),
+        (at(OTHERS, -1, -1, 1), near_left),
+        (at(OTHERS, 1, -1, 1), near_right),
+        (at(OWN + OTHERS, -1, 2) + at(OWN + OTHERS, 1, 2), join(far_sides)),
+        (ends[:cut] + at(OTHERS, 2, 0), end),
+        (ends[cut:], opposite_right),
         (at(OWN + OTHERS, 2, 2), far_opposite),
     )
 
@@ -288,7 +291,7 @@
     weights = arrange([terms for terms, _ in parts[:2]], rows, other_rows)
     weights += arrange([terms for terms, _ in parts[2:]], rows, other_rows, rest, other_rest)
     tile = product(weights[0], parts[0][1])
-    for i in (3, 4, 1, 2, 6, 7, 5, 8):
+    for i in (4, 1, 5, 3, 2, 7, 6, 8):
         tile = lax.optimization_barrier(tile + product(weights[i], parts[i][1]))
 
     kept, sent = halve(tile)

time: 197 us -> 199 us (1.010)
  waiting for transfers between devices: 112 us -> 118 us
  starting transfers between devices: 60.8 us -> 57 us
    ppermute x7, waiting for transfers between devices: 16.9 us -> 23.5 us  [along_y(): lax.ppermute(block, 'y', [(i, (i + step) % SIDE) for i in range(SIDE)])]
    ppermute x4, starting transfers between devices: 23.4 us -> 19.7 us  [swap_cores(): return lax.ppermute(block, 'core', [(0, 1), (1, 0)])]
where the time goes in v5:
time: 199 us
  waiting for transfers between devices  118 us (59%)
  starting transfers between devices  57 us (29%)
  matrix products  14.1 us (7%)
  Pallas kernels  5.33 us (3%)
  local copies, waits for them, and re-layouts  2.08 us (1%)
    ppermute x25, waiting for transfers between devices, along_plane(): return lax.ppermute(block, ('x', 'z', 'core'), route)  90.3 us
    ppermute x25, starting transfers between devices, along_plane(): return lax.ppermute(block, ('x', 'z', 'core'), route)  25 us
    ppermute x7, waiting for transfers between devices, along_y(): lax.ppermute(block, 'y', [(i, (i + step) % SIDE) for i in range(SIDE)])  23.5 us
    ppermute x4, starting transfers between devices, swap_cores(): return lax.ppermute(block, 'core', [(0, 1), (1, 0)])  19.7 us
    dot_general x9, matrix products, product(): lax.dot_general(weight, block, (((0,), (0,)), ((), ())), preferred_elemen...  14.1 us
    ppermute x7, starting transfers between devices, along_y(): lax.ppermute(block, 'y', [(i, (i + step) % SIDE) for i in range(SIDE)])  12.3 us
    ppermute x4, waiting for transfers between devices, swap_cores(): return lax.ppermute(block, 'core', [(0, 1), (1, 0)])  4.57 us
  transfers between devices with their start and end apart: 36, of which 19 were waited for; matrix products, arithmetic and copies ran while one was open for 8% of the time, Pallas kernels for 1%

profile of v5, /device:TPU:1, one launch (start us, length us, event | category | flops | bytes accessed | tf_op | source)
XLA Modules:
  0.0 199.1 jit_solution(9379401041174224208)
XLA Ops:
  3.0 2.5 %collective-permute-start = (bf16[4,48,624]{2,1,0:T(8,128)(2,1)S(1)}, bf16[4,48,624]{2,1,0:T(8,128)(2,1)S(1)}, u32[]{:S(2)}, u32[]{:S(2)}) collective-permute-start(bf16[4,48,624]{2,1,0:T(8,128)(2,1)S(1)} %get-tuple-element.34), channel_id=1, source_target_pairs={{0,8},{1,3},{2,10},{3,5},{4,12},{5,7},{6,14},{7,1},{8,16},{9,11},{... | collective-permute-start | bytes 718856 | tf_op jit(solution)/shard_map/ppermute | solution.py:32
  5.6 2.2 %collective-permute-start.1 = (bf16[4,48,624]{2,1,0:T(8,128)(2,1)S(1)}, bf16[4,48,624]{2,1,0:T(8,128)(2,1)S(1)}, u32[]{:S(2)}, u32[]{:S(2)}) collective-permute-start(bf16[4,48,624]{2,1,0:T(8,128)(2,1)S(1)} %get-tuple-element.35), channel_id=1, source_target_pairs={{0,24},{1,7},{2,26},{3,1},{4,28},{5,3},{6,30},{7,5},{8,0},{9,15},{... | collective-permute-start | bytes 718856 | tf_op jit(solution)/shard_map/ppermute | solution.py:32
  9.0 2.5 %collective-permute-done.refs_1_ = bf16[4,48,624]{2,1,0:T(8,128)(2,1)S(1)} collective-permute-done((bf16[4,48,624]{2,1,0:T(8,128)(2,1)S(1)}, bf16[4,48,624]{2,1,0:T(8,128)(2,1)S(1)}, u32[]{:S(2)}, u32[]{:S(2)}) %collective-permute-start) | collective-permute-done | bytes 239648 | tf_op jit(solution)/shard_map/ppermute | solution.py:32
  11.5 2.0 %collective-permute-done.1.refs_2_ = bf16[4,48,624]{2,1,0:T(8,128)(2,1)S(1)} collective-permute-done((bf16[4,48,624]{2,1,0:T(8,128)(2,1)S(1)}, bf16[4,48,624]{2,1,0:T(8,128)(2,1)S(1)}, u32[]{:S(2)}, u32[]{:S(2)}) %collective-permute-start.1) | collective-permute-done | bytes 239648 | tf_op jit(solution)/shard_map/ppermute | solution.py:32
  13.5 1.7 collective-permute-done.2.refs_3_
  16.4 1.6 collective-permute-start.4
  19.4 2.5 %collective-permute-done.3.refs_1_ = bf16[4,48,624]{2,1,0:T(8,128)(2,1)S(1)} collective-permute-done((bf16[4,48,624]{2,1,0:T(8,128)(2,1)S(1)}, bf16[4,48,624]{2,1,0:T(8,128)(2,1)S(1)}, u32[]{:S(2)}, u32[]{:S(2)}) %collective-permute-start.3) | collective-permute-done | bytes 239648 | tf_op jit(solution)/shard_map/ppermute | solution.py:32
  21.9 1.9 collective-permute-done.4.refs_2_
  28.4 3.1 %collective-permute-start.7 = (bf16[4,48,1280]{2,1,0:T(8,128)(2,1)S(1)}, bf16[4,48,1280]{2,1,0:T(8,128)(2,1)S(1)}, u32[]{:S(2)}, u32[]{:S(2)}) collective-permute-start(bf16[4,48,1280]{2,1,0:T(8,128)(2,1)S(1)} %get-tuple-element.46), channel_id=1, source_target_pairs={{0,1},{1,0},{2,3},{3,2},{4,5},{5,4},{6,7},{7,6},{8,9},{9,8},{10,11... | collective-permute-start | bytes 1474568 | tf_op jit(solution)/shard_map/ppermute | solution.py:22
  33.0 1.6 collective-permute-start.17
  35.9 16.6 %collective-permute-done.17.refs_0_ = bf16[96,1280]{1,0:T(8,128)(2,1)S(1)} collective-permute-done((bf16[96,1280]{1,0:T(8,128)(2,1)S(1)}, bf16[96,1280]{1,0:T(8,128)(2,1)S(1)}, u32[]{:S(2)}, u32[]{:S(2)}) %collective-permute-start.17) | collective-permute-done | bytes 245792 | tf_op jit(solution)/shard_map/ppermute | solution.py:18
  54.4 2.1 %collective-permute-start.9 = (bf16[96,1280]{1,0:T(8,128)(2,1)S(1)}, bf16[96,1280]{1,0:T(8,128)(2,1)S(1)}, u32[]{:S(2)}, u32[]{:S(2)}) collective-permute-start(bf16[96,1280]{1,0:T(8,128)(2,1)S(1)} %get-tuple-element.47.refs_0_), channel_id=1, source_target_pairs={{0,24},{1,7},{2,26},{3,1},{4,28},{5,3},{6,30},{7,5},{8,0},{9,15},{... | collective-permute-start | bytes 737288 | tf_op jit(solution)/shard_map/ppermute | solution.py:32
  56.5 5.8 %collective-permute-start.14 = (bf16[8,48,624]{2,1,0:T(8,128)(2,1)S(1)}, bf16[8,48,624]{2,1,0:T(8,128)(2,1)S(1)}, u32[]{:S(2)}, u32[]{:S(2)}) collective-permute-start(bf16[8,48,624]{2,1,0:T(8,128)(2,1)S(1)} %slice.24), channel_id=1, source_target_pairs={{0,32},{32,64},{64,96},{96,0},{1,33},{33,65},{65,97},{97,1},{2,34}... | collective-permute-start | bytes 1437704 | tf_op jit(solution)/shard_map/ppermute | solution.py:18
  62.9 2.7 %collective-permute-start.21 = (bf16[288,1280]{1,0:T(8,128)(2,1)S(1)}, bf16[288,1280]{1,0:T(8,128)(2,1)S(1)}, u32[]{:S(2)}, u32[]{:S(2)}) collective-permute-start(bf16[288,1280]{1,0:T(8,128)(2,1)S(1)} %join.15.refs_0_), channel_id=1, source_target_pairs={{0,24},{1,7},{2,26},{3,1},{4,28},{5,3},{6,30},{7,5},{8,0},{9,15},{... | collective-permute-start | bytes 2211848 | tf_op jit(solution)/shard_map/ppermute | solution.py:32
  65.7 7.0 %collective-permute-done.14.refs_1_ = bf16[8,48,624]{2,1,0:T(8,128)(2,1)S(1)} collective-permute-done((bf16[8,48,624]{2,1,0:T(8,128)(2,1)S(1)}, bf16[8,48,624]{2,1,0:T(8,128)(2,1)S(1)}, u32[]{:S(2)}, u32[]{:S(2)}) %collective-permute-start.14) | collective-permute-done | bytes 479264 | tf_op jit(solution)/shard_map/ppermute | solution.py:18
  73.4 7.1 %collective-permute-start.16 = (bf16[48,48,624]{2,1,0:T(8,128)(2,1)S(1)}, bf16[48,48,624]{2,1,0:T(8,128)(2,1)S(1)}, u32[]{:S(2)}, u32[]{:S(2)}) collective-permute-start(bf16[48,48,624]{2,1,0:T(8,128)(2,1)S(1)} %join.14.refs_2_), channel_id=1, source_target_pairs={{0,1},{1,0},{2,3},{3,2},{4,5},{5,4},{6,7},{7,6},{8,9},{9,8},{10,11... | collective-permute-start | bytes 8626184 | tf_op jit(solution)/shard_map/ppermute | solution.py:22
  80.5 1.8 collective-permute-start.11
  82.4 2.7 %collective-permute-start.30 = (bf16[288,1280]{1,0:T(8,128)(2,1)S(1)}, bf16[288,1280]{1,0:T(8,128)(2,1)S(1)}, u32[]{:S(2)}, u32[]{:S(2)}) collective-permute-start(bf16[288,1280]{1,0:T(8,128)(2,1)S(1)} %join.15.refs_0_), channel_id=1, source_target_pairs={{0,6},{1,25},{2,0},{3,27},{4,2},{5,29},{6,4},{7,31},{8,14},{9,1},{... | collective-permute-start | bytes 2211848 | tf_op jit(solution)/shard_map/ppermute | solution.py:32
  85.2 5.8 %collective-permute-done.10.refs_1_ = bf16[288,1280]{1,0:T(8,128)(2,1)S(1)} collective-permute-done((bf16[288,1280]{1,0:T(8,128)(2,1)S(1)}, bf16[288,1280]{1,0:T(8,128)(2,1)S(1)}, u32[]{:S(2)}, u32[]{:S(2)}) %collective-permute-start.10) | collective-permute-done | bytes 737312 | tf_op jit(solution)/shard_map/ppermute | solution.py:32
  91.0 2.6 %collective-permute-done.11.refs_2_ = bf16[288,1280]{1,0:T(8,128)(2,1)S(1)} collective-permute-done((bf16[288,1280]{1,0:T(8,128)(2,1)S(1)}, bf16[288,1280]{1,0:T(8,128)(2,1)S(1)}, u32[]{:S(2)}, u32[]{:S(2)}) %collective-permute-start.11) | collective-permute-done | bytes 737312 | tf_op jit(solution)/shard_map/ppermute | solution.py:32
  93.6 6.6 %collective-permute-done.29.refs_3_ = bf16[288,1280]{1,0:T(8,128)(2,1)S(1)} collective-permute-done((bf16[288,1280]{1,0:T(8,128)(2,1)S(1)}, bf16[288,1280]{1,0:T(8,128)(2,1)S(1)}, u32[]{:S(2)}, u32[]{:S(2)}) %collective-permute-start.29) | collective-permute-done | bytes 737312 | tf_op jit(solution)/shard_map/ppermute | solution.py:32
  101.8 28.7 %collective-permute-done.23.refs_0_ = bf16[144,1280]{1,0:T(8,128)(2,1)S(1)} collective-permute-done((bf16[144,1280]{1,0:T(8,128)(2,1)S(1)}, bf16[144,1280]{1,0:T(8,128)(2,1)S(1)}, u32[]{:S(2)}, u32[]{:S(2)}) %collective-permute-start.23) | collective-permute-done | bytes 368672 | tf_op jit(solution)/shard_map/ppermute | solution.py:32
  130.9 6.0 %collective-permute-done.24.refs_1_ = bf16[144,1280]{1,0:T(8,128)(2,1)S(1)} collective-permute-done((bf16[144,1280]{1,0:T(8,128)(2,1)S(1)}, bf16[144,1280]{1,0:T(8,128)(2,1)S(1)}, u32[]{:S(2)}, u32[]{:S(2)}) %collective-permute-start.24) | collective-permute-done | bytes 368672 | tf_op jit(solution)/shard_map/ppermute | solution.py:32
  136.9 2.5 %collective-permute-start.32 = (bf16[144,1280]{1,0:T(8,128)(2,1)S(1)}, bf16[144,1280]{1,0:T(8,128)(2,1)S(1)}, u32[]{:S(2)}, u32[]{:S(2)}) collective-permute-start(bf16[144,1280]{1,0:T(8,128)(2,1)S(1)} %slice.29), channel_id=1, source_target_pairs={{0,2},{1,9},{2,4},{3,11},{4,6},{5,13},{6,0},{7,15},{8,10},{9,17},{... | collective-permute-start | bytes 1105928 | tf_op jit(solution)/shard_map/ppermute | solution.py:32
  141.2 18.0 %collective-permute-done.33.refs_1_ = bf16[288,1280]{1,0:T(8,128)(2,1)S(1)} collective-permute-done((bf16[288,1280]{1,0:T(8,128)(2,1)S(1)}, bf16[288,1280]{1,0:T(8,128)(2,1)S(1)}, u32[]{:S(2)}, u32[]{:S(2)}) %collective-permute-start.33) | collective-permute-done | bytes 737312 | tf_op jit(solution)/shard_map/ppermute | solution.py:32
  159.6 3.6 %collective-permute-done.32.refs_0_ = bf16[144,1280]{1,0:T(8,128)(2,1)S(1)} collective-permute-done((bf16[144,1280]{1,0:T(8,128)(2,1)S(1)}, bf16[144,1280]{1,0:T(8,128)(2,1)S(1)}, u32[]{:S(2)}, u32[]{:S(2)}) %collective-permute-start.32) | collective-permute-done | bytes 368672 | tf_op jit(solution)/shard_map/ppermute | solution.py:32
  165.8 2.0 convolution_add_fusion.3
  169.7 3.7 %fusion.3 = f32[624,1280]{1,0:T(8,128)S(1)} fusion(bf16[1824,624]{1,0:T(8,128)(2,1)S(1)} %get-tuple-element.55, bf16[1824,1280]{1,0:T(8,128)(2,1)S(1)} %join.20), kind=kOutput, calls=%fused_computation.7 | convolution fusion | flops 2913730560 | bytes 10140672 | tf_op jit(solution)/shard_map/dot_general | solution.py:289
  178.4 5.9 %collective-permute-done.34 = bf16[384,1280]{1,0:T(8,128)(2,1)S(1)} collective-permute-done((bf16[384,1280]{1,0:T(8,128)(2,1)S(1)}, bf16[384,1280]{1,0:T(8,128)(2,1)S(1)}, u32[]{:S(2)}, u32[]{:S(2)}) %collective-permute-start.34) | collective-permute-done | bytes 983072 | tf_op jit(solution)/shard_map/ppermute | solution.py:32
  185.6 8.6 %collective-permute-start.35 = (f32[312,1280]{1,0:T(8,128)S(1)}, f32[312,1280]{1,0:T(8,128)S(1)}, u32[]{:S(2)}, u32[]{:S(2)}) collective-permute-start(f32[312,1280]{1,0:T(8,128)S(1)} %get-tuple-element.60), channel_id=1, source_target_pairs={{0,1},{1,0},{2,3},{3,2},{4,5},{5,4},{6,7},{7,6},{8,9},{9,8},{10,11... | collective-permute-start | bytes 4792328 | tf_op jit(solution)/shard_map/ppermute | solution.py:22
  194.2 3.1 %collective-permute-done.35.got_ref = f32[312,1280]{1,0:T(8,128)S(1)} collective-permute-done((f32[312,1280]{1,0:T(8,128)S(1)}, f32[312,1280]{1,0:T(8,128)S(1)}, u32[]{:S(2)}, u32[]{:S(2)}) %collective-permute-start.35) | collective-permute-done | bytes 1597472 | tf_op jit(solution)/shard_map/ppermute | solution.py:22
  197.2 1.9 assemble.1
  (81 shorter events, 32.7 us)
Async XLA Ops:
  3.0 8.5 %collective-permute-start = (bf16[4,48,624]{2,1,0:T(8,128)(2,1)S(1)}, bf16[4,48,624]{2,1,0:T(8,128)(2,1)S(1)}, u32[]{:S(2)}, u32[]{:S(2)}) collective-permute-start(bf16[4,48,624]{2,1,0:T(8,128)(2,1)S(1)} %get-tuple-element.34), channel_id=1, source_target_pairs={{0,8},{1,3},{2,10},{3,5},{4,12},{5,7},{6,14},{7,1},{8,16},{9,11},{... | collective-permute-start | bytes 718856 | tf_op jit(solution)/shard_map/ppermute | solution.py:32
  5.6 8.0 %collective-permute-start.1 = (bf16[4,48,624]{2,1,0:T(8,128)(2,1)S(1)}, bf16[4,48,624]{2,1,0:T(8,128)(2,1)S(1)}, u32[]{:S(2)}, u32[]{:S(2)}) collective-permute-start(bf16[4,48,624]{2,1,0:T(8,128)(2,1)S(1)} %get-tuple-element.35), channel_id=1, source_target_pairs={{0,24},{1,7},{2,26},{3,1},{4,28},{5,3},{6,30},{7,5},{8,0},{9,15},{... | collective-permute-start | bytes 718856 | tf_op jit(solution)/shard_map/ppermute | solution.py:32
  7.8 7.5 %collective-permute-start.2 = (bf16[4,48,624]{2,1,0:T(8,128)(2,1)S(1)}, bf16[4,48,624]{2,1,0:T(8,128)(2,1)S(1)}, u32[]{:S(2)}, u32[]{:S(2)}) collective-permute-start(bf16[4,48,624]{2,1,0:T(8,128)(2,1)S(1)} %get-tuple-element.36), channel_id=1, source_target_pairs={{0,16},{1,5},{2,18},{3,7},{4,20},{5,1},{6,22},{7,3},{8,24},{9,13},... | collective-permute-start | bytes 718856 | tf_op jit(solution)/shard_map/ppermute | solution.py:32
  16.4 7.4 %collective-permute-start.4 = (bf16[4,48,624]{2,1,0:T(8,128)(2,1)S(1)}, bf16[4,48,624]{2,1,0:T(8,128)(2,1)S(1)}, u32[]{:S(2)}, u32[]{:S(2)}) collective-permute-start(bf16[4,48,624]{2,1,0:T(8,128)(2,1)S(1)} %get-tuple-element.39), channel_id=1, source_target_pairs={{0,6},{1,25},{2,0},{3,27},{4,2},{5,29},{6,4},{7,31},{8,14},{9,1},{... | collective-permute-start | bytes 718856 | tf_op jit(solution)/shard_map/ppermute | solution.py:32
  25.5 28.9 %collective-permute-start.13 = (bf16[16,48,624]{2,1,0:T(8,128)(2,1)S(1)}, bf16[16,48,624]{2,1,0:T(8,128)(2,1)S(1)}, u32[]{:S(2)}, u32[]{:S(2)}) collective-permute-start(bf16[16,48,624]{2,1,0:T(8,128)(2,1)S(1)} %join.11.refs_0_), channel_id=1, source_target_pairs={{0,32},{32,64},{64,96},{96,0},{1,33},{33,65},{65,97},{97,1},{2,34}... | collective-permute-start | bytes 2875400 | tf_op jit(solution)/shard_map/ppermute | solution.py:18
  26.9 29.6 %collective-permute-start.12 = (bf16[16,48,624]{2,1,0:T(8,128)(2,1)S(1)}, bf16[16,48,624]{2,1,0:T(8,128)(2,1)S(1)}, u32[]{:S(2)}, u32[]{:S(2)}) collective-permute-start(bf16[16,48,624]{2,1,0:T(8,128)(2,1)S(1)} %join.11.refs_0_), channel_id=1, source_target_pairs={{0,96},{32,0},{64,32},{96,64},{1,97},{33,1},{65,33},{97,65},{2,98}... | collective-permute-start | bytes 2875400 | tf_op jit(solution)/shard_map/ppermute | solution.py:18
  33.0 19.4 %collective-permute-start.17 = (bf16[96,1280]{1,0:T(8,128)(2,1)S(1)}, bf16[96,1280]{1,0:T(8,128)(2,1)S(1)}, u32[]{:S(2)}, u32[]{:S(2)}) collective-permute-start(bf16[96,1280]{1,0:T(8,128)(2,1)S(1)} %get-tuple-element.49), channel_id=1, source_target_pairs={{0,96},{32,0},{64,32},{96,64},{1,97},{33,1},{65,33},{97,65},{2,98}... | collective-permute-start | bytes 737288 | tf_op jit(solution)/shard_map/ppermute | solution.py:18
  34.6 19.1 %collective-permute-start.18 = (bf16[96,1280]{1,0:T(8,128)(2,1)S(1)}, bf16[96,1280]{1,0:T(8,128)(2,1)S(1)}, u32[]{:S(2)}, u32[]{:S(2)}) collective-permute-start(bf16[96,1280]{1,0:T(8,128)(2,1)S(1)} %get-tuple-element.50), channel_id=1, source_target_pairs={{0,64},{32,96},{64,0},{96,32},{1,65},{33,97},{65,1},{97,33},{2,66}... | collective-permute-start | bytes 737288 | tf_op jit(solution)/shard_map/ppermute | solution.py:18
  35.0 45.5 %collective-permute-start.6 = (bf16[16,48,624]{2,1,0:T(8,128)(2,1)S(1)}, bf16[16,48,624]{2,1,0:T(8,128)(2,1)S(1)}, u32[]{:S(2)}, u32[]{:S(2)}) collective-permute-start(bf16[16,48,624]{2,1,0:T(8,128)(2,1)S(1)} %join.11.refs_0_), channel_id=1, source_target_pairs={{0,1},{1,0},{2,3},{3,2},{4,5},{5,4},{6,7},{7,6},{8,9},{9,8},{10,11... | collective-permute-start | bytes 2875400 | tf_op jit(solution)/shard_map/ppermute | solution.py:22
  52.5 9.8 %collective-permute-start.19 = (bf16[96,1280]{1,0:T(8,128)(2,1)S(1)}, bf16[96,1280]{1,0:T(8,128)(2,1)S(1)}, u32[]{:S(2)}, u32[]{:S(2)}) collective-permute-start(bf16[96,1280]{1,0:T(8,128)(2,1)S(1)} %get-tuple-element.51), channel_id=1, source_target_pairs={{0,32},{32,64},{64,96},{96,0},{1,33},{33,65},{65,97},{97,1},{2,34}... | collective-permute-start | bytes 737288 | tf_op jit(solution)/shard_map/ppermute | solution.py:18
  53.8 9.1 %collective-permute-start.8 = (bf16[96,1280]{1,0:T(8,128)(2,1)S(1)}, bf16[96,1280]{1,0:T(8,128)(2,1)S(1)}, u32[]{:S(2)}, u32[]{:S(2)}) collective-permute-start(bf16[96,1280]{1,0:T(8,128)(2,1)S(1)} %get-tuple-element.47.refs_0_), channel_id=1, source_target_pairs={{0,8},{1,3},{2,10},{3,5},{4,12},{5,7},{6,14},{7,1},{8,16},{9,11},{... | collective-permute-start | bytes 737288 | tf_op jit(solution)/shard_map/ppermute | solution.py:32
  54.4 8.6 %collective-permute-start.9 = (bf16[96,1280]{1,0:T(8,128)(2,1)S(1)}, bf16[96,1280]{1,0:T(8,128)(2,1)S(1)}, u32[]{:S(2)}, u32[]{:S(2)}) collective-permute-start(bf16[96,1280]{1,0:T(8,128)(2,1)S(1)} %get-tuple-element.47.refs_0_), channel_id=1, source_target_pairs={{0,24},{1,7},{2,26},{3,1},{4,28},{5,3},{6,30},{7,5},{8,0},{9,15},{... | collective-permute-start | bytes 737288 | tf_op jit(solution)/shard_map/ppermute | solution.py:32
  56.5 16.1 %collective-permute-start.14 = (bf16[8,48,624]{2,1,0:T(8,128)(2,1)S(1)}, bf16[8,48,624]{2,1,0:T(8,128)(2,1)S(1)}, u32[]{:S(2)}, u32[]{:S(2)}) collective-permute-start(bf16[8,48,624]{2,1,0:T(8,128)(2,1)S(1)} %slice.24), channel_id=1, source_target_pairs={{0,32},{32,64},{64,96},{96,0},{1,33},{33,65},{65,97},{97,1},{2,34}... | collective-permute-start | bytes 1437704 | tf_op jit(solution)/shard_map/ppermute | solution.py:18
  62.3 10.8 %collective-permute-start.15 = (bf16[8,48,624]{2,1,0:T(8,128)(2,1)S(1)}, bf16[8,48,624]{2,1,0:T(8,128)(2,1)S(1)}, u32[]{:S(2)}, u32[]{:S(2)}) collective-permute-start(bf16[8,48,624]{2,1,0:T(8,128)(2,1)S(1)} %slice.25), channel_id=1, source_target_pairs={{0,96},{32,0},{64,32},{96,64},{1,97},{33,1},{65,33},{97,65},{2,98}... | collective-permute-start | bytes 1437704 | tf_op jit(solution)/shard_map/ppermute | solution.py:18
  62.9 19.5 %collective-permute-start.20 = (bf16[288,1280]{1,0:T(8,128)(2,1)S(1)}, bf16[288,1280]{1,0:T(8,128)(2,1)S(1)}, u32[]{:S(2)}, u32[]{:S(2)}) collective-permute-start(bf16[288,1280]{1,0:T(8,128)(2,1)S(1)} %join.15.refs_0_), channel_id=1, source_target_pairs={{0,8},{1,3},{2,10},{3,5},{4,12},{5,7},{6,14},{7,1},{8,16},{9,11},{... | collective-permute-start | bytes 2211848 | tf_op jit(solution)/shard_map/ppermute | solution.py:32
  62.9 19.4 %collective-permute-start.21 = (bf16[288,1280]{1,0:T(8,128)(2,1)S(1)}, bf16[288,1280]{1,0:T(8,128)(2,1)S(1)}, u32[]{:S(2)}, u32[]{:S(2)}) collective-permute-start(bf16[288,1280]{1,0:T(8,128)(2,1)S(1)} %join.15.refs_0_), channel_id=1, source_target_pairs={{0,24},{1,7},{2,26},{3,1},{4,28},{5,3},{6,30},{7,5},{8,0},{9,15},{... | collective-permute-start | bytes 2211848 | tf_op jit(solution)/shard_map/ppermute | solution.py:32
  72.6 18.3 %collective-permute-start.10 = (bf16[288,1280]{1,0:T(8,128)(2,1)S(1)}, bf16[288,1280]{1,0:T(8,128)(2,1)S(1)}, u32[]{:S(2)}, u32[]{:S(2)}) collective-permute-start(bf16[288,1280]{1,0:T(8,128)(2,1)S(1)} %join.12.refs_0_), channel_id=1, source_target_pairs={{0,2},{1,9},{2,4},{3,11},{4,6},{5,13},{6,0},{7,15},{8,10},{9,17},{... | collective-permute-start | bytes 2211848 | tf_op jit(solution)/shard_map/ppermute | solution.py:32
  73.4 90.5 %collective-permute-start.16 = (bf16[48,48,624]{2,1,0:T(8,128)(2,1)S(1)}, bf16[48,48,624]{2,1,0:T(8,128)(2,1)S(1)}, u32[]{:S(2)}, u32[]{:S(2)}) collective-permute-start(bf16[48,48,624]{2,1,0:T(8,128)(2,1)S(1)} %join.14.refs_2_), channel_id=1, source_target_pairs={{0,1},{1,0},{2,3},{3,2},{4,5},{5,4},{6,7},{7,6},{8,9},{9,8},{10,11... | collective-permute-start | bytes 8626184 | tf_op jit(solution)/shard_map/ppermute | solution.py:22
  80.5 13.1 %collective-permute-start.11 = (bf16[288,1280]{1,0:T(8,128)(2,1)S(1)}, bf16[288,1280]{1,0:T(8,128)(2,1)S(1)}, u32[]{:S(2)}, u32[]{:S(2)}) collective-permute-start(bf16[288,1280]{1,0:T(8,128)(2,1)S(1)} %join.12.refs_0_), channel_id=1, source_target_pairs={{0,6},{1,25},{2,0},{3,27},{4,2},{5,29},{6,4},{7,31},{8,14},{9,1},{... | collective-permute-start | bytes 2211848 | tf_op jit(solution)/shard_map/ppermute | solution.py:32
  82.4 17.9 %collective-permute-start.29 = (bf16[288,1280]{1,0:T(8,128)(2,1)S(1)}, bf16[288,1280]{1,0:T(8,128)(2,1)S(1)}, u32[]{:S(2)}, u32[]{:S(2)}) collective-permute-start(bf16[288,1280]{1,0:T(8,128)(2,1)S(1)} %join.15.refs_0_), channel_id=1, source_target_pairs={{0,2},{1,9},{2,4},{3,11},{4,6},{5,13},{6,0},{7,15},{8,10},{9,17},{... | collective-permute-start | bytes 2211848 | tf_op jit(solution)/shard_map/ppermute | solution.py:32
  82.4 19.2 %collective-permute-start.30 = (bf16[288,1280]{1,0:T(8,128)(2,1)S(1)}, bf16[288,1280]{1,0:T(8,128)(2,1)S(1)}, u32[]{:S(2)}, u32[]{:S(2)}) collective-permute-start(bf16[288,1280]{1,0:T(8,128)(2,1)S(1)} %join.15.refs_0_), channel_id=1, source_target_pairs={{0,6},{1,25},{2,0},{3,27},{4,2},{5,29},{6,4},{7,31},{8,14},{9,1},{... | collective-permute-start | bytes 2211848 | tf_op jit(solution)/shard_map/ppermute | solution.py:32
  91.0 45.9 %collective-permute-start.28 = (bf16[576,1280]{1,0:T(8,128)(2,1)S(1)}, bf16[576,1280]{1,0:T(8,128)(2,1)S(1)}, u32[]{:S(2)}, u32[]{:S(2)}) collective-permute-start(bf16[576,1280]{1,0:T(8,128)(2,1)S(1)} %join.16.refs_1_), channel_id=1, source_target_pairs={{0,2},{1,9},{2,4},{3,11},{4,6},{5,13},{6,0},{7,15},{8,10},{9,17},{... | collective-permute-start | bytes 4423688 | tf_op jit(solution)/shard_map/ppermute | solution.py:32
  93.6 37.3 %collective-permute-start.25 = (bf16[384,1280]{1,0:T(8,128)(2,1)S(1)}, bf16[384,1280]{1,0:T(8,128)(2,1)S(1)}, u32[]{:S(2)}, u32[]{:S(2)}) collective-permute-start(bf16[384,1280]{1,0:T(8,128)(2,1)S(1)} %join.18), channel_id=1, source_target_pairs={{0,8},{1,3},{2,10},{3,5},{4,12},{5,7},{6,14},{7,1},{8,16},{9,11},{... | collective-permute-start | bytes 2949128 | tf_op jit(solution)/shard_map/ppermute | solution.py:32
  100.2 36.7 %collective-permute-start.22 = (bf16[576,1280]{1,0:T(8,128)(2,1)S(1)}, bf16[576,1280]{1,0:T(8,128)(2,1)S(1)}, u32[]{:S(2)}, u32[]{:S(2)}) collective-permute-start(bf16[576,1280]{1,0:T(8,128)(2,1)S(1)} %join.16.refs_1_), channel_id=1, source_target_pairs={{0,6},{1,25},{2,0},{3,27},{4,2},{5,29},{6,4},{7,31},{8,14},{9,1},{... | collective-permute-start | bytes 4423688 | tf_op jit(solution)/shard_map/ppermute | solution.py:32
  101.5 29.0 %collective-permute-start.23 = (bf16[144,1280]{1,0:T(8,128)(2,1)S(1)}, bf16[144,1280]{1,0:T(8,128)(2,1)S(1)}, u32[]{:S(2)}, u32[]{:S(2)}) collective-permute-start(bf16[144,1280]{1,0:T(8,128)(2,1)S(1)} %slice.26), channel_id=1, source_target_pairs={{0,2},{1,9},{2,4},{3,11},{4,6},{5,13},{6,0},{7,15},{8,10},{9,17},{... | collective-permute-start | bytes 1105928 | tf_op jit(solution)/shard_map/ppermute | solution.py:32
  130.9 32.4 %collective-permute-start.27 = (bf16[384,1280]{1,0:T(8,128)(2,1)S(1)}, bf16[384,1280]{1,0:T(8,128)(2,1)S(1)}, u32[]{:S(2)}, u32[]{:S(2)}) collective-permute-start(bf16[384,1280]{1,0:T(8,128)(2,1)S(1)} %collective-permute-done.25.refs_2_), channel_id=1, source_target_pairs={{0,6},{1,25},{2,0},{3,27},{4,2},{5,29},{6,4},{7,31},{8,14},{9,1},{... | collective-permute-start | bytes 2949128 | tf_op jit(solution)/shard_map/ppermute | solution.py:32
  136.9 26.8 %collective-permute-start.26 = (bf16[384,1280]{1,0:T(8,128)(2,1)S(1)}, bf16[384,1280]{1,0:T(8,128)(2,1)S(1)}, u32[]{:S(2)}, u32[]{:S(2)}) collective-permute-start(bf16[384,1280]{1,0:T(8,128)(2,1)S(1)} %collective-permute-done.25.refs_2_), channel_id=1, source_target_pairs={{0,2},{1,9},{2,4},{3,11},{4,6},{5,13},{6,0},{7,15},{8,10},{9,17},{... | collective-permute-start | bytes 2949128 | tf_op jit(solution)/shard_map/ppermute | solution.py:32
  136.9 22.3 %collective-permute-start.33 = (bf16[288,1280]{1,0:T(8,128)(2,1)S(1)}, bf16[288,1280]{1,0:T(8,128)(2,1)S(1)}, u32[]{:S(2)}, u32[]{:S(2)}) collective-permute-start(bf16[288,1280]{1,0:T(8,128)(2,1)S(1)} %collective-permute-done.29.refs_3_), channel_id=1, source_target_pairs={{0,2},{1,9},{2,4},{3,11},{4,6},{5,13},{6,0},{7,15},{8,10},{9,17},{... | collective-permute-start | bytes 2211848 | tf_op jit(solution)/shard_map/ppermute | solution.py:32
  136.9 26.2 %collective-permute-start.32 = (bf16[144,1280]{1,0:T(8,128)(2,1)S(1)}, bf16[144,1280]{1,0:T(8,128)(2,1)S(1)}, u32[]{:S(2)}, u32[]{:S(2)}) collective-permute-start(bf16[144,1280]{1,0:T(8,128)(2,1)S(1)} %slice.29), channel_id=1, source_target_pairs={{0,2},{1,9},{2,4},{3,11},{4,6},{5,13},{6,0},{7,15},{8,10},{9,17},{... | collective-permute-start | bytes 1105928 | tf_op jit(solution)/shard_map/ppermute | solution.py:32
  159.2 16.4 %collective-permute-start.31 = (bf16[432,1280]{1,0:T(8,128)(2,1)S(1)}, bf16[432,1280]{1,0:T(8,128)(2,1)S(1)}, u32[]{:S(2)}, u32[]{:S(2)}) collective-permute-start(bf16[432,1280]{1,0:T(8,128)(2,1)S(1)} %slice.28), channel_id=1, source_target_pairs={{0,6},{1,25},{2,0},{3,27},{4,2},{5,29},{6,4},{7,31},{8,14},{9,1},{... | collective-permute-start | bytes 3317768 | tf_op jit(solution)/shard_map/ppermute | solution.py:32
  163.3 21.1 %collective-permute-start.34 = (bf16[384,1280]{1,0:T(8,128)(2,1)S(1)}, bf16[384,1280]{1,0:T(8,128)(2,1)S(1)}, u32[]{:S(2)}, u32[]{:S(2)}) collective-permute-start(bf16[384,1280]{1,0:T(8,128)(2,1)S(1)} %collective-permute-done.27.refs_1_), channel_id=1, source_target_pairs={{0,6},{1,25},{2,0},{3,27},{4,2},{5,29},{6,4},{7,31},{8,14},{9,1},{... | collective-permute-start | bytes 2949128 | tf_op jit(solution)/shard_map/ppermute | solution.py:32
  185.6 11.6 %collective-permute-start.35 = (f32[312,1280]{1,0:T(8,128)S(1)}, f32[312,1280]{1,0:T(8,128)S(1)}, u32[]{:S(2)}, u32[]{:S(2)}) collective-permute-start(f32[312,1280]{1,0:T(8,128)S(1)} %get-tuple-element.60), channel_id=1, source_target_pairs={{0,1},{1,0},{2,3},{3,2},{4,5},{5,4},{6,7},{7,6},{8,9},{9,8},{10,11... | collective-permute-start | bytes 4792328 | tf_op jit(solution)/shard_map/ppermute | solution.py:22
  (6 other events, 26.8 us)

commit v6 on v4

--- a/solution.py
+++ b/solution.py
@@ -161,13 +161,15 @@
     early_before, early_after = along_plane(early, 0, 1), along_plane(early, 0, -1)
     line = join([early, early_before, early_after])
     left, right = along_plane(line, 1, 1), along_plane(line, 1, -1)
-    cut = line.shape[0] // 2
-    opposite = along_plane(left[:cut], 1, 1), along_plane(right[cut:], 1, -1)
+    early_far = along_plane(early_before, 0, 1)
+    early_far_sides = along_plane(early_far, 1, 1), along_plane(early_far, 1, -1)
+    cut = 2 * early.shape[0]
+    back = join([right[cut:], early_far_sides[1]])
+    opposite = along_plane(left[:cut], 1, 1), along_plane(back, 1, -1)
 
     before, after = along_plane(late, 0, 1), along_plane(late, 0, -1)
     near = join([before, after])
-    both_before = join([early_before, before])
-    far = along_plane(both_before, 0, 1)
+    far = along_plane(before, 0, 1)
     near_sides = along_plane(near, 1, 1), along_plane(near, 1, -1)
     own_sides = along_plane(late, 1, 1), along_plane(late, 1, -1)
     far_sides = along_plane(far, 1, 1), along_plane(far, 1, -1)
@@ -180,16 +182,18 @@
     first = join([late, near, far, *own_sides])
     middle = join([*far_sides, own_opposite])
     ends = at(OTHERS, 2, -1, 1)
+    early_line = sum((at(OWN, v, 0, -1, 1) for v in (0, -1, 1)), ())
+    early_line += at(OWN, 0, 2) + at(OWN, -1, 2) + at(OWN, 1, 2)
     return (
-        (sum((at(OWN, v, 0, -1, 1) for v in (0, -1, 1)), ()), join([line, left, right])),
-        (at(OWN, 2, 0, -1, 1), early_opposite),
-        (at(OTHERS, 0, 0, -1, 1) + at(OWN + OTHERS, 0, 2) + at(OTHERS, -1, 0) + at(OTHERS, 1, 0), first),
+        (early_line, join([line, left, right, early_far, *early_far_sides])),
+        (at(OWN, 2, 0, -1, 1, 2), early_opposite),
+        (at(OTHERS, 0, 0, -1, 1, 2) + at(OTHERS, -1, 0) + at(OTHERS, 1, 0), first),
         (at(OTHERS, -1, -1, 1), near_sides[0]),
         (at(OTHERS, 1, -1, 1), near_sides[1]),
-        (at(OWN + OTHERS, -1, 2) + at(OWN + OTHERS, 1, 2) + at(OTHERS, 2, 0), middle),
+        (at(OTHERS, -1, 2) + at(OTHERS, 1, 2) + at(OTHERS, 2, 0), middle),
         (ends[: len(ends) // 4], near_opposite[0]),
         (ends[len(ends) // 4 :], near_opposite[1]),
-        (at(OWN + OTHERS, 2, 2), far_opposite),
+        (at(OTHERS, 2, 2), far_opposite),
     )
 
 

time: 197 us -> 187 us (0.949)
  waiting for transfers between devices: 112 us -> 101 us
    ppermute x25 -> x28, starting transfers between devices: 25.9 us -> 32.1 us  [along_plane(): return lax.ppermute(block, ('x', 'z', 'core'), route)]
    ppermute x25 -> x28, waiting for transfers between devices: 90.4 us -> 84.8 us  [along_plane(): return lax.ppermute(block, ('x', 'z', 'core'), route)]
    ppermute x7, waiting for transfers between devices: 16.9 us -> 11.7 us  [along_y(): lax.ppermute(block, 'y', [(i, (i + step) % SIDE) for i in range(SIDE)])]
    ppermute x7, starting transfers between devices: 11.5 us -> 8.53 us  [along_y(): lax.ppermute(block, 'y', [(i, (i + step) % SIDE) for i in range(SIDE)])]
  transfers between devices with their start and end apart: 36 -> 39, of which waited for: 19 -> 21; matrix products, arithmetic and copies ran while one was open for 8% -> 8% of each run, Pallas kernels for 1% -> 1%
where the time goes in v6:
time: 187 us
  waiting for transfers between devices  101 us (54%)
  starting transfers between devices  62.6 us (33%)
  matrix products  14.4 us (8%)
  Pallas kernels  5.29 us (3%)
  local copies, waits for them, and re-layouts  2.08 us (1%)
    ppermute x28, waiting for transfers between devices, along_plane(): return lax.ppermute(block, ('x', 'z', 'core'), route)  84.8 us
    ppermute x28, starting transfers between devices, along_plane(): return lax.ppermute(block, ('x', 'z', 'core'), route)  32.1 us
    ppermute x4, starting transfers between devices, swap_cores(): return lax.ppermute(block, 'core', [(0, 1), (1, 0)])  22 us
    dot_general x9, matrix products, product(): lax.dot_general(weight, block, (((0,), (0,)), ((), ())), preferred_elemen...  14.4 us
    ppermute x7, waiting for transfers between devices, along_y(): lax.ppermute(block, 'y', [(i, (i + step) % SIDE) for i in range(SIDE)])  11.7 us
    ppermute x7, starting transfers between devices, along_y(): lax.ppermute(block, 'y', [(i, (i + step) % SIDE) for i in range(SIDE)])  8.53 us
    ppermute x4, waiting for transfers between devices, swap_cores(): return lax.ppermute(block, 'core', [(0, 1), (1, 0)])  4.57 us
  transfers between devices with their start and end apart: 39, of which 21 were waited for; matrix products, arithmetic and copies ran while one was open for 8% of the time, Pallas kernels for 1%

profile of v6, /device:TPU:1, one launch (start us, length us, event | category | flops | bytes accessed | tf_op | source)
XLA Modules:
  0.0 187.3 jit_solution(10540260699528955391)
XLA Ops:
  3.0 2.5 %collective-permute-start = (bf16[4,48,624]{2,1,0:T(8,128)(2,1)S(1)}, bf16[4,48,624]{2,1,0:T(8,128)(2,1)S(1)}, u32[]{:S(2)}, u32[]{:S(2)}) collective-permute-start(bf16[4,48,624]{2,1,0:T(8,128)(2,1)S(1)} %get-tuple-element.34), channel_id=1, source_target_pairs={{0,8},{1,3},{2,10},{3,5},{4,12},{5,7},{6,14},{7,1},{8,16},{9,11},{... | collective-permute-start | bytes 718856 | tf_op jit(solution)/shard_map/ppermute | solution.py:32
  5.6 2.2 %collective-permute-start.1 = (bf16[4,48,624]{2,1,0:T(8,128)(2,1)S(1)}, bf16[4,48,624]{2,1,0:T(8,128)(2,1)S(1)}, u32[]{:S(2)}, u32[]{:S(2)}) collective-permute-start(bf16[4,48,624]{2,1,0:T(8,128)(2,1)S(1)} %get-tuple-element.35), channel_id=1, source_target_pairs={{0,24},{1,7},{2,26},{3,1},{4,28},{5,3},{6,30},{7,5},{8,0},{9,15},{... | collective-permute-start | bytes 718856 | tf_op jit(solution)/shard_map/ppermute | solution.py:32
  9.0 2.5 %collective-permute-done.refs_1_ = bf16[4,48,624]{2,1,0:T(8,128)(2,1)S(1)} collective-permute-done((bf16[4,48,624]{2,1,0:T(8,128)(2,1)S(1)}, bf16[4,48,624]{2,1,0:T(8,128)(2,1)S(1)}, u32[]{:S(2)}, u32[]{:S(2)}) %collective-permute-start) | collective-permute-done | bytes 239648 | tf_op jit(solution)/shard_map/ppermute | solution.py:32
  11.5 2.0 %collective-permute-done.1.refs_2_ = bf16[4,48,624]{2,1,0:T(8,128)(2,1)S(1)} collective-permute-done((bf16[4,48,624]{2,1,0:T(8,128)(2,1)S(1)}, bf16[4,48,624]{2,1,0:T(8,128)(2,1)S(1)}, u32[]{:S(2)}, u32[]{:S(2)}) %collective-permute-start.1) | collective-permute-done | bytes 239648 | tf_op jit(solution)/shard_map/ppermute | solution.py:32
  19.4 2.5 %collective-permute-done.3.refs_1_ = bf16[4,48,624]{2,1,0:T(8,128)(2,1)S(1)} collective-permute-done((bf16[4,48,624]{2,1,0:T(8,128)(2,1)S(1)}, bf16[4,48,624]{2,1,0:T(8,128)(2,1)S(1)}, u32[]{:S(2)}, u32[]{:S(2)}) %collective-permute-start.3) | collective-permute-done | bytes 239648 | tf_op jit(solution)/shard_map/ppermute | solution.py:32
  21.9 1.9 %collective-permute-done.4.refs_2_ = bf16[4,48,624]{2,1,0:T(8,128)(2,1)S(1)} collective-permute-done((bf16[4,48,624]{2,1,0:T(8,128)(2,1)S(1)}, bf16[4,48,624]{2,1,0:T(8,128)(2,1)S(1)}, u32[]{:S(2)}, u32[]{:S(2)}) %collective-permute-start.4) | collective-permute-done | bytes 239648 | tf_op jit(solution)/shard_map/ppermute | solution.py:32
  28.4 3.1 %collective-permute-start.7 = (bf16[4,48,1280]{2,1,0:T(8,128)(2,1)S(1)}, bf16[4,48,1280]{2,1,0:T(8,128)(2,1)S(1)}, u32[]{:S(2)}, u32[]{:S(2)}) collective-permute-start(bf16[4,48,1280]{2,1,0:T(8,128)(2,1)S(1)} %get-tuple-element.46), channel_id=1, source_target_pairs={{0,1},{1,0},{2,3},{3,2},{4,5},{5,4},{6,7},{7,6},{8,9},{9,8},{10,11... | collective-permute-start | bytes 1474568 | tf_op jit(solution)/shard_map/ppermute | solution.py:22
  36.1 3.5 %collective-permute-done.8.refs_1_ = bf16[96,1280]{1,0:T(8,128)(2,1)S(1)} collective-permute-done((bf16[96,1280]{1,0:T(8,128)(2,1)S(1)}, bf16[96,1280]{1,0:T(8,128)(2,1)S(1)}, u32[]{:S(2)}, u32[]{:S(2)}) %collective-permute-start.8) | collective-permute-done | bytes 245792 | tf_op jit(solution)/shard_map/ppermute | solution.py:32
  39.7 7.8 %collective-permute-done.16.refs_3_ = bf16[16,48,624]{2,1,0:T(8,128)(2,1)S(1)} collective-permute-done((bf16[16,48,624]{2,1,0:T(8,128)(2,1)S(1)}, bf16[16,48,624]{2,1,0:T(8,128)(2,1)S(1)}, u32[]{:S(2)}, u32[]{:S(2)}) %collective-permute-start.16) | collective-permute-done | bytes 958496 | tf_op jit(solution)/shard_map/ppermute | solution.py:18
  48.6 3.9 %collective-permute-done.20.refs_0_ = bf16[96,1280]{1,0:T(8,128)(2,1)S(1)} collective-permute-done((bf16[96,1280]{1,0:T(8,128)(2,1)S(1)}, bf16[96,1280]{1,0:T(8,128)(2,1)S(1)}, u32[]{:S(2)}, u32[]{:S(2)}) %collective-permute-start.20) | collective-permute-done | bytes 245792 | tf_op jit(solution)/shard_map/ppermute | solution.py:18
  52.5 3.3 %collective-permute-start.18 = (bf16[8,48,624]{2,1,0:T(8,128)(2,1)S(1)}, bf16[8,48,624]{2,1,0:T(8,128)(2,1)S(1)}, u32[]{:S(2)}, u32[]{:S(2)}) collective-permute-start(bf16[8,48,624]{2,1,0:T(8,128)(2,1)S(1)} %slice.25), channel_id=1, source_target_pairs={{0,96},{32,0},{64,32},{96,64},{1,97},{33,1},{65,33},{97,65},{2,98}... | collective-permute-start | bytes 1437704 | tf_op jit(solution)/shard_map/ppermute | solution.py:18
  55.8 8.3 %collective-permute-start.6 = (bf16[16,48,624]{2,1,0:T(8,128)(2,1)S(1)}, bf16[16,48,624]{2,1,0:T(8,128)(2,1)S(1)}, u32[]{:S(2)}, u32[]{:S(2)}) collective-permute-start(bf16[16,48,624]{2,1,0:T(8,128)(2,1)S(1)} %join.10.refs_0_), channel_id=1, source_target_pairs={{0,1},{1,0},{2,3},{3,2},{4,5},{5,4},{6,7},{7,6},{8,9},{9,8},{10,11... | collective-permute-start | bytes 2875400 | tf_op jit(solution)/shard_map/ppermute | solution.py:22
  66.9 2.6 %collective-permute-done.9.refs_2_ = bf16[96,1280]{1,0:T(8,128)(2,1)S(1)} collective-permute-done((bf16[96,1280]{1,0:T(8,128)(2,1)S(1)}, bf16[96,1280]{1,0:T(8,128)(2,1)S(1)}, u32[]{:S(2)}, u32[]{:S(2)}) %collective-permute-start.9) | collective-permute-done | bytes 245792 | tf_op jit(solution)/shard_map/ppermute | solution.py:32
  69.5 2.0 %collective-permute-start.14 = (bf16[96,1280]{1,0:T(8,128)(2,1)S(1)}, bf16[96,1280]{1,0:T(8,128)(2,1)S(1)}, u32[]{:S(2)}, u32[]{:S(2)}) collective-permute-start(bf16[96,1280]{1,0:T(8,128)(2,1)S(1)} %collective-permute-done.12.refs_3_), channel_id=1, source_target_pairs={{0,6},{1,25},{2,0},{3,27},{4,2},{5,29},{6,4},{7,31},{8,14},{9,1},{... | collective-permute-start | bytes 737288 | tf_op jit(solution)/shard_map/ppermute | solution.py:32
  72.7 2.2 %collective-permute-start.24 = (bf16[288,1280]{1,0:T(8,128)(2,1)S(1)}, bf16[288,1280]{1,0:T(8,128)(2,1)S(1)}, u32[]{:S(2)}, u32[]{:S(2)}) collective-permute-start(bf16[288,1280]{1,0:T(8,128)(2,1)S(1)} %join.14.refs_0_), channel_id=1, source_target_pairs={{0,24},{1,7},{2,26},{3,1},{4,28},{5,3},{6,30},{7,5},{8,0},{9,15},{... | collective-permute-start | bytes 2211848 | tf_op jit(solution)/shard_map/ppermute | solution.py:32
  75.3 2.8 %collective-permute-start.19 = (bf16[48,48,624]{2,1,0:T(8,128)(2,1)S(1)}, bf16[48,48,624]{2,1,0:T(8,128)(2,1)S(1)}, u32[]{:S(2)}, u32[]{:S(2)}) collective-permute-start(bf16[48,48,624]{2,1,0:T(8,128)(2,1)S(1)} %join.13.refs_2_), channel_id=1, source_target_pairs={{0,1},{1,0},{2,3},{3,2},{4,5},{5,4},{6,7},{7,6},{8,9},{9,8},{10,11... | collective-permute-start | bytes 8626184 | tf_op jit(solution)/shard_map/ppermute | solution.py:22
  78.2 4.6 %collective-permute-start.11 = (bf16[288,1280]{1,0:T(8,128)(2,1)S(1)}, bf16[288,1280]{1,0:T(8,128)(2,1)S(1)}, u32[]{:S(2)}, u32[]{:S(2)}) collective-permute-start(bf16[288,1280]{1,0:T(8,128)(2,1)S(1)} %join.11.refs_0_), channel_id=1, source_target_pairs={{0,6},{1,25},{2,0},{3,27},{4,2},{5,29},{6,4},{7,31},{8,14},{9,1},{... | collective-permute-start | bytes 2211848 | tf_op jit(solution)/shard_map/ppermute | solution.py:32
  82.8 3.3 %collective-permute-done.23.refs_0_ = bf16[288,1280]{1,0:T(8,128)(2,1)S(1)} collective-permute-done((bf16[288,1280]{1,0:T(8,128)(2,1)S(1)}, bf16[288,1280]{1,0:T(8,128)(2,1)S(1)}, u32[]{:S(2)}, u32[]{:S(2)}) %collective-permute-start.23) | collective-permute-done | bytes 737312 | tf_op jit(solution)/shard_map/ppermute | solution.py:32
  88.9 5.2 %collective-permute-done.10.refs_1_ = bf16[288,1280]{1,0:T(8,128)(2,1)S(1)} collective-permute-done((bf16[288,1280]{1,0:T(8,128)(2,1)S(1)}, bf16[288,1280]{1,0:T(8,128)(2,1)S(1)}, u32[]{:S(2)}, u32[]{:S(2)}) %collective-permute-start.10) | collective-permute-done | bytes 737312 | tf_op jit(solution)/shard_map/ppermute | solution.py:32
  94.3 8.1 %collective-permute-done.30.refs_3_ = bf16[288,1280]{1,0:T(8,128)(2,1)S(1)} collective-permute-done((bf16[288,1280]{1,0:T(8,128)(2,1)S(1)}, bf16[288,1280]{1,0:T(8,128)(2,1)S(1)}, u32[]{:S(2)}, u32[]{:S(2)}) %collective-permute-start.30) | collective-permute-done | bytes 737312 | tf_op jit(solution)/shard_map/ppermute | solution.py:32
  102.4 28.9 %collective-permute-done.27.refs_0_ = bf16[192,1280]{1,0:T(8,128)(2,1)S(1)} collective-permute-done((bf16[192,1280]{1,0:T(8,128)(2,1)S(1)}, bf16[192,1280]{1,0:T(8,128)(2,1)S(1)}, u32[]{:S(2)}, u32[]{:S(2)}) %collective-permute-start.27) | collective-permute-done | bytes 491552 | tf_op jit(solution)/shard_map/ppermute | solution.py:32
  131.3 7.7 %collective-permute-done.28.refs_1_ = bf16[192,1280]{1,0:T(8,128)(2,1)S(1)} collective-permute-done((bf16[192,1280]{1,0:T(8,128)(2,1)S(1)}, bf16[192,1280]{1,0:T(8,128)(2,1)S(1)}, u32[]{:S(2)}, u32[]{:S(2)}) %collective-permute-start.28) | collective-permute-done | bytes 491552 | tf_op jit(solution)/shard_map/ppermute | solution.py:32
  139.0 2.7 %collective-permute-start.35 = (bf16[288,1280]{1,0:T(8,128)(2,1)S(1)}, bf16[288,1280]{1,0:T(8,128)(2,1)S(1)}, u32[]{:S(2)}, u32[]{:S(2)}) collective-permute-start(bf16[288,1280]{1,0:T(8,128)(2,1)S(1)} %collective-permute-done.29.refs_2_), channel_id=1, source_target_pairs={{0,6},{1,25},{2,0},{3,27},{4,2},{5,29},{6,4},{7,31},{8,14},{9,1},{... | collective-permute-start | bytes 2211848 | tf_op jit(solution)/shard_map/ppermute | solution.py:32
  143.7 7.2 %collective-permute-done.36.refs_2_ = bf16[288,1280]{1,0:T(8,128)(2,1)S(1)} collective-permute-done((bf16[288,1280]{1,0:T(8,128)(2,1)S(1)}, bf16[288,1280]{1,0:T(8,128)(2,1)S(1)}, u32[]{:S(2)}, u32[]{:S(2)}) %collective-permute-start.36) | collective-permute-done | bytes 737312 | tf_op jit(solution)/shard_map/ppermute | solution.py:32
  150.8 2.7 %collective-permute-start.37 = (bf16[288,1280]{1,0:T(8,128)(2,1)S(1)}, bf16[288,1280]{1,0:T(8,128)(2,1)S(1)}, u32[]{:S(2)}, u32[]{:S(2)}) collective-permute-start(bf16[288,1280]{1,0:T(8,128)(2,1)S(1)} %collective-permute-done.35.refs_1_), channel_id=1, source_target_pairs={{0,6},{1,25},{2,0},{3,27},{4,2},{5,29},{6,4},{7,31},{8,14},{9,1},{... | collective-permute-start | bytes 2211848 | tf_op jit(solution)/shard_map/ppermute | solution.py:32
  153.5 5.2 %collective-permute-done.34.refs_0_ = bf16[288,1280]{1,0:T(8,128)(2,1)S(1)} collective-permute-done((bf16[288,1280]{1,0:T(8,128)(2,1)S(1)}, bf16[288,1280]{1,0:T(8,128)(2,1)S(1)}, u32[]{:S(2)}, u32[]{:S(2)}) %collective-permute-start.34) | collective-permute-done | bytes 737312 | tf_op jit(solution)/shard_map/ppermute | solution.py:32
  160.8 2.4 %convolution_add_fusion.3 = f32[624,1280]{1,0:T(8,128)S(1)} fusion(f32[624,1280]{1,0:T(8,128)S(1)} %fusion, bf16[1152,624]{1,0:T(8,128)(2,1)S(1)} %get-tuple-element.41, bf16[1152,1280]{1,0:T(8,128)(2,1)S(1)} %join.12), kind=kOutput, calls=%fused_computation.3 | convolution fusion | flops 1841049600 | bytes 10776576 | tf_op jit(solution)/shard_map/dot_general | solution.py:290
  165.4 3.2 %convolution_add_fusion.2 = f32[624,1280]{1,0:T(8,128)S(1)} fusion(f32[624,1280]{1,0:T(8,128)S(1)} %add.26, bf16[1728,624]{1,0:T(8,128)(2,1)S(1)} %get-tuple-element.54, bf16[1728,1280]{1,0:T(8,128)(2,1)S(1)} %join.18), kind=kOutput, calls=%fused_computation.2 | convolution fusion | flops 2761175040 | bytes 12969984 | tf_op jit(solution)/shard_map/dot_general | solution.py:290
  171.1 2.2 %convolution_add_fusion.1 = f32[624,1280]{1,0:T(8,128)S(1)} fusion(f32[624,1280]{1,0:T(8,128)S(1)} %add.29, bf16[864,624]{1,0:T(8,128)(2,1)S(1)} %get-tuple-element.57, bf16[864,1280]{1,0:T(8,128)(2,1)S(1)} %join.19), kind=kOutput, calls=%fused_computation.1 | convolution fusion | flops 1380986880 | bytes 9679872 | tf_op jit(solution)/shard_map/dot_general | solution.py:290
  174.6 7.7 %collective-permute-start.38 = (f32[312,1280]{1,0:T(8,128)S(1)}, f32[312,1280]{1,0:T(8,128)S(1)}, u32[]{:S(2)}, u32[]{:S(2)}) collective-permute-start(f32[312,1280]{1,0:T(8,128)S(1)} %get-tuple-element.60), channel_id=1, source_target_pairs={{0,1},{1,0},{2,3},{3,2},{4,5},{5,4},{6,7},{7,6},{8,9},{9,8},{10,11... | collective-permute-start | bytes 4792328 | tf_op jit(solution)/shard_map/ppermute | solution.py:22
  182.3 3.1 %collective-permute-done.38.got_ref = f32[312,1280]{1,0:T(8,128)S(1)} collective-permute-done((f32[312,1280]{1,0:T(8,128)S(1)}, f32[312,1280]{1,0:T(8,128)S(1)}, u32[]{:S(2)}, u32[]{:S(2)}) %collective-permute-start.38) | collective-permute-done | bytes 1597472 | tf_op jit(solution)/shard_map/ppermute | solution.py:22
  185.4 1.9 %assemble.1 = f32[312,2496]{1,0:T(8,128)} custom-call(f32[312,1280]{1,0:T(8,128)S(1)} %get-tuple-element.59.kept_ref, f32[312,1280]{1,0:T(8,128)S(1)} %collective-permute-done.38.got_ref), custom_call_target="tpu_custom_call" | custom-call | tf_op jit(solution)/shard_map/assemble/pallas_call | solution.py:259
  (86 shorter events, 37.6 us)
Async XLA Ops:
  3.0 8.5 %collective-permute-start = (bf16[4,48,624]{2,1,0:T(8,128)(2,1)S(1)}, bf16[4,48,624]{2,1,0:T(8,128)(2,1)S(1)}, u32[]{:S(2)}, u32[]{:S(2)}) collective-permute-start(bf16[4,48,624]{2,1,0:T(8,128)(2,1)S(1)} %get-tuple-element.34), channel_id=1, source_target_pairs={{0,8},{1,3},{2,10},{3,5},{4,12},{5,7},{6,14},{7,1},{8,16},{9,11},{... | collective-permute-start | bytes 718856 | tf_op jit(solution)/shard_map/ppermute | solution.py:32
  5.6 8.0 %collective-permute-start.1 = (bf16[4,48,624]{2,1,0:T(8,128)(2,1)S(1)}, bf16[4,48,624]{2,1,0:T(8,128)(2,1)S(1)}, u32[]{:S(2)}, u32[]{:S(2)}) collective-permute-start(bf16[4,48,624]{2,1,0:T(8,128)(2,1)S(1)} %get-tuple-element.35), channel_id=1, source_target_pairs={{0,24},{1,7},{2,26},{3,1},{4,28},{5,3},{6,30},{7,5},{8,0},{9,15},{... | collective-permute-start | bytes 718856 | tf_op jit(solution)/shard_map/ppermute | solution.py:32
  7.8 7.5 %collective-permute-start.2 = (bf16[4,48,624]{2,1,0:T(8,128)(2,1)S(1)}, bf16[4,48,624]{2,1,0:T(8,128)(2,1)S(1)}, u32[]{:S(2)}, u32[]{:S(2)}) collective-permute-start(bf16[4,48,624]{2,1,0:T(8,128)(2,1)S(1)} %get-tuple-element.36), channel_id=1, source_target_pairs={{0,16},{1,5},{2,18},{3,7},{4,20},{5,1},{6,22},{7,3},{8,24},{9,13},... | collective-permute-start | bytes 718856 | tf_op jit(solution)/shard_map/ppermute | solution.py:32
  16.4 7.4 %collective-permute-start.4 = (bf16[4,48,624]{2,1,0:T(8,128)(2,1)S(1)}, bf16[4,48,624]{2,1,0:T(8,128)(2,1)S(1)}, u32[]{:S(2)}, u32[]{:S(2)}) collective-permute-start(bf16[4,48,624]{2,1,0:T(8,128)(2,1)S(1)} %get-tuple-element.39), channel_id=1, source_target_pairs={{0,6},{1,25},{2,0},{3,27},{4,2},{5,29},{6,4},{7,31},{8,14},{9,1},{... | collective-permute-start | bytes 718856 | tf_op jit(solution)/shard_map/ppermute | solution.py:32
  25.5 22.0 %collective-permute-start.16 = (bf16[16,48,624]{2,1,0:T(8,128)(2,1)S(1)}, bf16[16,48,624]{2,1,0:T(8,128)(2,1)S(1)}, u32[]{:S(2)}, u32[]{:S(2)}) collective-permute-start(bf16[16,48,624]{2,1,0:T(8,128)(2,1)S(1)} %join.10.refs_0_), channel_id=1, source_target_pairs={{0,32},{32,64},{64,96},{96,0},{1,33},{33,65},{65,97},{97,1},{2,34}... | collective-permute-start | bytes 2875400 | tf_op jit(solution)/shard_map/ppermute | solution.py:18
  26.9 21.3 %collective-permute-start.15 = (bf16[16,48,624]{2,1,0:T(8,128)(2,1)S(1)}, bf16[16,48,624]{2,1,0:T(8,128)(2,1)S(1)}, u32[]{:S(2)}, u32[]{:S(2)}) collective-permute-start(bf16[16,48,624]{2,1,0:T(8,128)(2,1)S(1)} %join.10.refs_0_), channel_id=1, source_target_pairs={{0,96},{32,0},{64,32},{96,64},{1,97},{33,1},{65,33},{97,65},{2,98}... | collective-permute-start | bytes 2875400 | tf_op jit(solution)/shard_map/ppermute | solution.py:18
  34.2 18.2 %collective-permute-start.20 = (bf16[96,1280]{1,0:T(8,128)(2,1)S(1)}, bf16[96,1280]{1,0:T(8,128)(2,1)S(1)}, u32[]{:S(2)}, u32[]{:S(2)}) collective-permute-start(bf16[96,1280]{1,0:T(8,128)(2,1)S(1)} %get-tuple-element.49), channel_id=1, source_target_pairs={{0,96},{32,0},{64,32},{96,64},{1,97},{33,1},{65,33},{97,65},{2,98}... | collective-permute-start | bytes 737288 | tf_op jit(solution)/shard_map/ppermute | solution.py:18
  35.8 20.1 %collective-permute-start.21 = (bf16[96,1280]{1,0:T(8,128)(2,1)S(1)}, bf16[96,1280]{1,0:T(8,128)(2,1)S(1)}, u32[]{:S(2)}, u32[]{:S(2)}) collective-permute-start(bf16[96,1280]{1,0:T(8,128)(2,1)S(1)} %get-tuple-element.50), channel_id=1, source_target_pairs={{0,64},{32,96},{64,0},{96,32},{1,65},{33,97},{65,1},{97,33},{2,66}... | collective-permute-start | bytes 737288 | tf_op jit(solution)/shard_map/ppermute | solution.py:18
  39.7 24.5 %collective-permute-start.22 = (bf16[96,1280]{1,0:T(8,128)(2,1)S(1)}, bf16[96,1280]{1,0:T(8,128)(2,1)S(1)}, u32[]{:S(2)}, u32[]{:S(2)}) collective-permute-start(bf16[96,1280]{1,0:T(8,128)(2,1)S(1)} %get-tuple-element.51), channel_id=1, source_target_pairs={{0,32},{32,64},{64,96},{96,0},{1,33},{33,65},{65,97},{97,1},{2,34}... | collective-permute-start | bytes 737288 | tf_op jit(solution)/shard_map/ppermute | solution.py:18
  47.5 18.2 %collective-permute-start.12 = (bf16[96,1280]{1,0:T(8,128)(2,1)S(1)}, bf16[96,1280]{1,0:T(8,128)(2,1)S(1)}, u32[]{:S(2)}, u32[]{:S(2)}) collective-permute-start(bf16[96,1280]{1,0:T(8,128)(2,1)S(1)} %collective-permute-done.8.refs_1_), channel_id=1, source_target_pairs={{0,8},{1,3},{2,10},{3,5},{4,12},{5,7},{6,14},{7,1},{8,16},{9,11},{... | collective-permute-start | bytes 737288 | tf_op jit(solution)/shard_map/ppermute | solution.py:32
  48.2 24.6 %collective-permute-start.17 = (bf16[8,48,624]{2,1,0:T(8,128)(2,1)S(1)}, bf16[8,48,624]{2,1,0:T(8,128)(2,1)S(1)}, u32[]{:S(2)}, u32[]{:S(2)}) collective-permute-start(bf16[8,48,624]{2,1,0:T(8,128)(2,1)S(1)} %slice.24), channel_id=1, source_target_pairs={{0,32},{32,64},{64,96},{96,0},{1,33},{33,65},{65,97},{97,1},{2,34}... | collective-permute-start | bytes 1437704 | tf_op jit(solution)/shard_map/ppermute | solution.py:18
  52.5 22.5 %collective-permute-start.18 = (bf16[8,48,624]{2,1,0:T(8,128)(2,1)S(1)}, bf16[8,48,624]{2,1,0:T(8,128)(2,1)S(1)}, u32[]{:S(2)}, u32[]{:S(2)}) collective-permute-start(bf16[8,48,624]{2,1,0:T(8,128)(2,1)S(1)} %slice.25), channel_id=1, source_target_pairs={{0,96},{32,0},{64,32},{96,64},{1,97},{33,1},{65,33},{97,65},{2,98}... | collective-permute-start | bytes 1437704 | tf_op jit(solution)/shard_map/ppermute | solution.py:18
  55.8 22.4 %collective-permute-start.6 = (bf16[16,48,624]{2,1,0:T(8,128)(2,1)S(1)}, bf16[16,48,624]{2,1,0:T(8,128)(2,1)S(1)}, u32[]{:S(2)}, u32[]{:S(2)}) collective-permute-start(bf16[16,48,624]{2,1,0:T(8,128)(2,1)S(1)} %join.10.refs_0_), channel_id=1, source_target_pairs={{0,1},{1,0},{2,3},{3,2},{4,5},{5,4},{6,7},{7,6},{8,9},{9,8},{10,11... | collective-permute-start | bytes 2875400 | tf_op jit(solution)/shard_map/ppermute | solution.py:22
  72.3 13.9 %collective-permute-start.23 = (bf16[288,1280]{1,0:T(8,128)(2,1)S(1)}, bf16[288,1280]{1,0:T(8,128)(2,1)S(1)}, u32[]{:S(2)}, u32[]{:S(2)}) collective-permute-start(bf16[288,1280]{1,0:T(8,128)(2,1)S(1)} %join.14.refs_0_), channel_id=1, source_target_pairs={{0,8},{1,3},{2,10},{3,5},{4,12},{5,7},{6,14},{7,1},{8,16},{9,11},{... | collective-permute-start | bytes 2211848 | tf_op jit(solution)/shard_map/ppermute | solution.py:32
  72.7 14.8 %collective-permute-start.24 = (bf16[288,1280]{1,0:T(8,128)(2,1)S(1)}, bf16[288,1280]{1,0:T(8,128)(2,1)S(1)}, u32[]{:S(2)}, u32[]{:S(2)}) collective-permute-start(bf16[288,1280]{1,0:T(8,128)(2,1)S(1)} %join.14.refs_0_), channel_id=1, source_target_pairs={{0,24},{1,7},{2,26},{3,1},{4,28},{5,3},{6,30},{7,5},{8,0},{9,15},{... | collective-permute-start | bytes 2211848 | tf_op jit(solution)/shard_map/ppermute | solution.py:32
  75.0 19.1 %collective-permute-start.10 = (bf16[288,1280]{1,0:T(8,128)(2,1)S(1)}, bf16[288,1280]{1,0:T(8,128)(2,1)S(1)}, u32[]{:S(2)}, u32[]{:S(2)}) collective-permute-start(bf16[288,1280]{1,0:T(8,128)(2,1)S(1)} %join.11.refs_0_), channel_id=1, source_target_pairs={{0,2},{1,9},{2,4},{3,11},{4,6},{5,13},{6,0},{7,15},{8,10},{9,17},{... | collective-permute-start | bytes 2211848 | tf_op jit(solution)/shard_map/ppermute | solution.py:32
  75.3 83.5 %collective-permute-start.19 = (bf16[48,48,624]{2,1,0:T(8,128)(2,1)S(1)}, bf16[48,48,624]{2,1,0:T(8,128)(2,1)S(1)}, u32[]{:S(2)}, u32[]{:S(2)}) collective-permute-start(bf16[48,48,624]{2,1,0:T(8,128)(2,1)S(1)} %join.13.refs_2_), channel_id=1, source_target_pairs={{0,1},{1,0},{2,3},{3,2},{4,5},{5,4},{6,7},{7,6},{8,9},{9,8},{10,11... | collective-permute-start | bytes 8626184 | tf_op jit(solution)/shard_map/ppermute | solution.py:22
  78.2 16.0 %collective-permute-start.11 = (bf16[288,1280]{1,0:T(8,128)(2,1)S(1)}, bf16[288,1280]{1,0:T(8,128)(2,1)S(1)}, u32[]{:S(2)}, u32[]{:S(2)}) collective-permute-start(bf16[288,1280]{1,0:T(8,128)(2,1)S(1)} %join.11.refs_0_), channel_id=1, source_target_pairs={{0,6},{1,25},{2,0},{3,27},{4,2},{5,29},{6,4},{7,31},{8,14},{9,1},{... | collective-permute-start | bytes 2211848 | tf_op jit(solution)/shard_map/ppermute | solution.py:32
  86.1 16.2 %collective-permute-start.30 = (bf16[288,1280]{1,0:T(8,128)(2,1)S(1)}, bf16[288,1280]{1,0:T(8,128)(2,1)S(1)}, u32[]{:S(2)}, u32[]{:S(2)}) collective-permute-start(bf16[288,1280]{1,0:T(8,128)(2,1)S(1)} %join.14.refs_0_), channel_id=1, source_target_pairs={{0,2},{1,9},{2,4},{3,11},{4,6},{5,13},{6,0},{7,15},{8,10},{9,17},{... | collective-permute-start | bytes 2211848 | tf_op jit(solution)/shard_map/ppermute | solution.py:32
  87.6 14.8 %collective-permute-start.31 = (bf16[288,1280]{1,0:T(8,128)(2,1)S(1)}, bf16[288,1280]{1,0:T(8,128)(2,1)S(1)}, u32[]{:S(2)}, u32[]{:S(2)}) collective-permute-start(bf16[288,1280]{1,0:T(8,128)(2,1)S(1)} %join.14.refs_0_), channel_id=1, source_target_pairs={{0,6},{1,25},{2,0},{3,27},{4,2},{5,29},{6,4},{7,31},{8,14},{9,1},{... | collective-permute-start | bytes 2211848 | tf_op jit(solution)/shard_map/ppermute | solution.py:32
  94.2 47.5 %collective-permute-start.25 = (bf16[576,1280]{1,0:T(8,128)(2,1)S(1)}, bf16[576,1280]{1,0:T(8,128)(2,1)S(1)}, u32[]{:S(2)}, u32[]{:S(2)}) collective-permute-start(bf16[576,1280]{1,0:T(8,128)(2,1)S(1)} %join.15.refs_1_), channel_id=1, source_target_pairs={{0,2},{1,9},{2,4},{3,11},{4,6},{5,13},{6,0},{7,15},{8,10},{9,17},{... | collective-permute-start | bytes 4423688 | tf_op jit(solution)/shard_map/ppermute | solution.py:32
  94.2 37.1 %collective-permute-start.27 = (bf16[192,1280]{1,0:T(8,128)(2,1)S(1)}, bf16[192,1280]{1,0:T(8,128)(2,1)S(1)}, u32[]{:S(2)}, u32[]{:S(2)}) collective-permute-start(bf16[192,1280]{1,0:T(8,128)(2,1)S(1)} %slice.26), channel_id=1, source_target_pairs={{0,2},{1,9},{2,4},{3,11},{4,6},{5,13},{6,0},{7,15},{8,10},{9,17},{... | collective-permute-start | bytes 1474568 | tf_op jit(solution)/shard_map/ppermute | solution.py:32
  102.4 41.1 %collective-permute-start.26 = (bf16[576,1280]{1,0:T(8,128)(2,1)S(1)}, bf16[576,1280]{1,0:T(8,128)(2,1)S(1)}, u32[]{:S(2)}, u32[]{:S(2)}) collective-permute-start(bf16[576,1280]{1,0:T(8,128)(2,1)S(1)} %join.15.refs_1_), channel_id=1, source_target_pairs={{0,6},{1,25},{2,0},{3,27},{4,2},{5,29},{6,4},{7,31},{8,14},{9,1},{... | collective-permute-start | bytes 4423688 | tf_op jit(solution)/shard_map/ppermute | solution.py:32
  102.4 36.6 %collective-permute-start.29 = (bf16[288,1280]{1,0:T(8,128)(2,1)S(1)}, bf16[288,1280]{1,0:T(8,128)(2,1)S(1)}, u32[]{:S(2)}, u32[]{:S(2)}) collective-permute-start(bf16[288,1280]{1,0:T(8,128)(2,1)S(1)} %collective-permute-done.23.refs_0_), channel_id=1, source_target_pairs={{0,8},{1,3},{2,10},{3,5},{4,12},{5,7},{6,14},{7,1},{8,16},{9,11},{... | collective-permute-start | bytes 2211848 | tf_op jit(solution)/shard_map/ppermute | solution.py:32
  131.3 7.7 %collective-permute-start.28 = (bf16[192,1280]{1,0:T(8,128)(2,1)S(1)}, bf16[192,1280]{1,0:T(8,128)(2,1)S(1)}, u32[]{:S(2)}, u32[]{:S(2)}) collective-permute-start(bf16[192,1280]{1,0:T(8,128)(2,1)S(1)} %join.16), channel_id=1, source_target_pairs={{0,6},{1,25},{2,0},{3,27},{4,2},{5,29},{6,4},{7,31},{8,14},{9,1},{... | collective-permute-start | bytes 1474568 | tf_op jit(solution)/shard_map/ppermute | solution.py:32
  139.0 11.8 %collective-permute-start.36 = (bf16[288,1280]{1,0:T(8,128)(2,1)S(1)}, bf16[288,1280]{1,0:T(8,128)(2,1)S(1)}, u32[]{:S(2)}, u32[]{:S(2)}) collective-permute-start(bf16[288,1280]{1,0:T(8,128)(2,1)S(1)} %collective-permute-done.30.refs_3_), channel_id=1, source_target_pairs={{0,2},{1,9},{2,4},{3,11},{4,6},{5,13},{6,0},{7,15},{8,10},{9,17},{... | collective-permute-start | bytes 2211848 | tf_op jit(solution)/shard_map/ppermute | solution.py:32
  139.0 11.8 %collective-permute-start.35 = (bf16[288,1280]{1,0:T(8,128)(2,1)S(1)}, bf16[288,1280]{1,0:T(8,128)(2,1)S(1)}, u32[]{:S(2)}, u32[]{:S(2)}) collective-permute-start(bf16[288,1280]{1,0:T(8,128)(2,1)S(1)} %collective-permute-done.29.refs_2_), channel_id=1, source_target_pairs={{0,6},{1,25},{2,0},{3,27},{4,2},{5,29},{6,4},{7,31},{8,14},{9,1},{... | collective-permute-start | bytes 2211848 | tf_op jit(solution)/shard_map/ppermute | solution.py:32
  141.7 17.0 %collective-permute-start.34 = (bf16[288,1280]{1,0:T(8,128)(2,1)S(1)}, bf16[288,1280]{1,0:T(8,128)(2,1)S(1)}, u32[]{:S(2)}, u32[]{:S(2)}) collective-permute-start(bf16[288,1280]{1,0:T(8,128)(2,1)S(1)} %collective-permute-done.29.refs_2_), channel_id=1, source_target_pairs={{0,2},{1,9},{2,4},{3,11},{4,6},{5,13},{6,0},{7,15},{8,10},{9,17},{... | collective-permute-start | bytes 2211848 | tf_op jit(solution)/shard_map/ppermute | solution.py:32
  143.5 25.1 %collective-permute-start.32 = (bf16[144,1280]{1,0:T(8,128)(2,1)S(1)}, bf16[144,1280]{1,0:T(8,128)(2,1)S(1)}, u32[]{:S(2)}, u32[]{:S(2)}) collective-permute-start(bf16[144,1280]{1,0:T(8,128)(2,1)S(1)} %slice.28), channel_id=1, source_target_pairs={{0,2},{1,9},{2,4},{3,11},{4,6},{5,13},{6,0},{7,15},{8,10},{9,17},{... | collective-permute-start | bytes 1105928 | tf_op jit(solution)/shard_map/ppermute | solution.py:32
  150.8 18.9 %collective-permute-start.33 = (bf16[432,1280]{1,0:T(8,128)(2,1)S(1)}, bf16[432,1280]{1,0:T(8,128)(2,1)S(1)}, u32[]{:S(2)}, u32[]{:S(2)}) collective-permute-start(bf16[432,1280]{1,0:T(8,128)(2,1)S(1)} %slice.29), channel_id=1, source_target_pairs={{0,6},{1,25},{2,0},{3,27},{4,2},{5,29},{6,4},{7,31},{8,14},{9,1},{... | collective-permute-start | bytes 3317768 | tf_op jit(solution)/shard_map/ppermute | solution.py:32
  150.8 22.5 %collective-permute-start.37 = (bf16[288,1280]{1,0:T(8,128)(2,1)S(1)}, bf16[288,1280]{1,0:T(8,128)(2,1)S(1)}, u32[]{:S(2)}, u32[]{:S(2)}) collective-permute-start(bf16[288,1280]{1,0:T(8,128)(2,1)S(1)} %collective-permute-done.35.refs_1_), channel_id=1, source_target_pairs={{0,6},{1,25},{2,0},{3,27},{4,2},{5,29},{6,4},{7,31},{8,14},{9,1},{... | collective-permute-start | bytes 2211848 | tf_op jit(solution)/shard_map/ppermute | solution.py:32
  174.6 10.8 %collective-permute-start.38 = (f32[312,1280]{1,0:T(8,128)S(1)}, f32[312,1280]{1,0:T(8,128)S(1)}, u32[]{:S(2)}, u32[]{:S(2)}) collective-permute-start(f32[312,1280]{1,0:T(8,128)S(1)} %get-tuple-element.60), channel_id=1, source_target_pairs={{0,1},{1,0},{2,3},{3,2},{4,5},{5,4},{6,7},{7,6},{8,9},{9,8},{10,11... | collective-permute-start | bytes 4792328 | tf_op jit(solution)/shard_map/ppermute | solution.py:22
  (9 other events, 44.8 us)

commit v7 on v1

--- a/solution.py
+++ b/solution.py
@@ -235,26 +235,24 @@
     )(tile)
 
 
-def assemble_kernel(kept_ref, got_ref, out_ref):
-    rest = out_ref.shape[1] - WIDE
-    for core in range(CORES):
-
-        @pl.when(lax.axis_index("core") == core)
-        def _():
-            first, last = (kept_ref, got_ref) if core == 0 else (got_ref, kept_ref)
-            out_ref[:, :WIDE] = first[...]
-            out_ref[:, WIDE:] = last[:, :rest]
-
-
-def assemble(kept, got, columns):
-    return pl.pallas_call(
-        assemble_kernel,
-        out_shape=jax.ShapeDtypeStruct((got.shape[0], columns), got.dtype),
-        in_specs=[VMEM, VMEM],
-        out_specs=VMEM,
+def write_kernel(half_ref, *refs):
+    refs[-1][...] = half_ref[...]
+
+
+def write(flip, half, columns, out=None):
+    args = (half,) if out is None else (half, out)
+    rows = half.shape[0]
+    return pl.pallas_call(
+        write_kernel,
+        grid=(1,),
+        out_shape=jax.ShapeDtypeStruct((rows, columns), half.dtype),
+        in_specs=[pl.BlockSpec((rows, WIDE), lambda i: (0, 0)), pl.BlockSpec(memory_space=pltpu.HBM)][: len(args)],
+        out_specs=pl.BlockSpec((rows, WIDE), lambda i: (0, lax.rem(lax.axis_index("core") + flip, CORES))),
+        input_output_aliases={} if out is None else {1: 0},
         compiler_params=pltpu.CompilerParams(vmem_limit_bytes=8 << 20),
-        name="assemble",
-    )(kept, got)
+        cost_estimate=pl.CostEstimate(flops=0, bytes_accessed=2 * half.size * 4, transcendentals=0),
+        name="write",
+    )(*args)
 
 
 def body(b_tensor, aux_counts):
@@ -294,7 +292,9 @@
         tile = lax.optimization_barrier(tile + product(weights[i], blocks[i]))
 
     kept, sent = halve(tile)
-    return assemble(kept, swap_cores(sent), basis // SIDE)
+    got = swap_cores(sent)
+    out = write(0, kept, basis // SIDE)
+    return write(1, got, basis // SIDE, out)
 
 
 def solution(mesh):

time: 174 us -> 173 us (level)
  transfers between devices with their start and end apart: 37 -> 37, of which waited for: 20 -> 20; matrix products, arithmetic and copies ran while one was open for 9% -> 9% of each run, Pallas kernels for 1% -> 2%
where the time goes in v7:
time: 173 us
  waiting for transfers between devices  99.3 us (57%)
  starting transfers between devices  49.8 us (29%)
  matrix products  14.3 us (8%)
  Pallas kernels  5.89 us (3%)
  local copies, waits for them, and re-layouts  2.1 us (1%)
    ppermute x26, waiting for transfers between devices, along_plane(): return lax.ppermute(block, ('x', 'z', 'core'), route)  78.5 us
    ppermute x26, starting transfers between devices, along_plane(): return lax.ppermute(block, ('x', 'z', 'core'), route)  23.8 us
    ppermute x7, waiting for transfers between devices, along_y(): lax.ppermute(block, 'y', [(i, (i + step) % SIDE) for i in range(SIDE)])  17.5 us
    ppermute x4, starting transfers between devices, swap_cores(): return lax.ppermute(block, 'core', [(0, 1), (1, 0)])  14.6 us
    dot_general x9, matrix products, product(): lax.dot_general(weight, block, (((0,), (0,)), ((), ())), preferred_elemen...  14.3 us
    ppermute x7, starting transfers between devices, along_y(): lax.ppermute(block, 'y', [(i, (i + step) % SIDE) for i in range(SIDE)])  11.4 us
  transfers between devices with their start and end apart: 37, of which 20 were waited for; matrix products, arithmetic and copies ran while one was open for 9% of the time, Pallas kernels for 2%

profile of v7, /device:TPU:1, one launch (start us, length us, event | category | flops | bytes accessed | tf_op | source)
XLA Modules:
  0.0 173.3 jit_solution(7169751142068602516)
XLA Ops:
  3.0 2.5 %collective-permute-start = (bf16[4,48,624]{2,1,0:T(8,128)(2,1)S(1)}, bf16[4,48,624]{2,1,0:T(8,128)(2,1)S(1)}, u32[]{:S(2)}, u32[]{:S(2)}) collective-permute-start(bf16[4,48,624]{2,1,0:T(8,128)(2,1)S(1)} %get-tuple-element.34), channel_id=1, source_target_pairs={{0,8},{1,3},{2,10},{3,5},{4,12},{5,7},{6,14},{7,1},{8,16},{9,11},{... | collective-permute-start | bytes 718856 | tf_op jit(solution)/shard_map/ppermute | solution.py:32
  5.6 2.2 %collective-permute-start.1 = (bf16[4,48,624]{2,1,0:T(8,128)(2,1)S(1)}, bf16[4,48,624]{2,1,0:T(8,128)(2,1)S(1)}, u32[]{:S(2)}, u32[]{:S(2)}) collective-permute-start(bf16[4,48,624]{2,1,0:T(8,128)(2,1)S(1)} %get-tuple-element.35), channel_id=1, source_target_pairs={{0,24},{1,7},{2,26},{3,1},{4,28},{5,3},{6,30},{7,5},{8,0},{9,15},{... | collective-permute-start | bytes 718856 | tf_op jit(solution)/shard_map/ppermute | solution.py:32
  9.0 2.5 %collective-permute-done.refs_1_ = bf16[4,48,624]{2,1,0:T(8,128)(2,1)S(1)} collective-permute-done((bf16[4,48,624]{2,1,0:T(8,128)(2,1)S(1)}, bf16[4,48,624]{2,1,0:T(8,128)(2,1)S(1)}, u32[]{:S(2)}, u32[]{:S(2)}) %collective-permute-start) | collective-permute-done | bytes 239648 | tf_op jit(solution)/shard_map/ppermute | solution.py:32
  11.5 2.0 %collective-permute-done.1.refs_2_ = bf16[4,48,624]{2,1,0:T(8,128)(2,1)S(1)} collective-permute-done((bf16[4,48,624]{2,1,0:T(8,128)(2,1)S(1)}, bf16[4,48,624]{2,1,0:T(8,128)(2,1)S(1)}, u32[]{:S(2)}, u32[]{:S(2)}) %collective-permute-start.1) | collective-permute-done | bytes 239648 | tf_op jit(solution)/shard_map/ppermute | solution.py:32
  13.5 1.7 collective-permute-done.2.refs_3_
  16.4 1.6 collective-permute-start.4
  19.4 2.5 %collective-permute-done.3.refs_1_ = bf16[4,48,624]{2,1,0:T(8,128)(2,1)S(1)} collective-permute-done((bf16[4,48,624]{2,1,0:T(8,128)(2,1)S(1)}, bf16[4,48,624]{2,1,0:T(8,128)(2,1)S(1)}, u32[]{:S(2)}, u32[]{:S(2)}) %collective-permute-start.3) | collective-permute-done | bytes 239648 | tf_op jit(solution)/shard_map/ppermute | solution.py:32
  21.9 1.9 %collective-permute-done.4.refs_2_ = bf16[4,48,624]{2,1,0:T(8,128)(2,1)S(1)} collective-permute-done((bf16[4,48,624]{2,1,0:T(8,128)(2,1)S(1)}, bf16[4,48,624]{2,1,0:T(8,128)(2,1)S(1)}, u32[]{:S(2)}, u32[]{:S(2)}) %collective-permute-start.4) | collective-permute-done | bytes 239648 | tf_op jit(solution)/shard_map/ppermute | solution.py:32
  23.8 1.6 collective-permute-done.5.refs_3_
  26.9 1.5 collective-permute-start.13
  28.4 3.1 %collective-permute-start.7 = (bf16[4,48,1280]{2,1,0:T(8,128)(2,1)S(1)}, bf16[4,48,1280]{2,1,0:T(8,128)(2,1)S(1)}, u32[]{:S(2)}, u32[]{:S(2)}) collective-permute-start(bf16[4,48,1280]{2,1,0:T(8,128)(2,1)S(1)} %get-tuple-element.46), channel_id=1, source_target_pairs={{0,1},{1,0},{2,3},{3,2},{4,5},{5,4},{6,7},{7,6},{8,9},{9,8},{10,11... | collective-permute-start | bytes 1474568 | tf_op jit(solution)/shard_map/ppermute | solution.py:22
  33.0 1.6 collective-permute-start.18
  35.7 16.8 %collective-permute-done.18.refs_0_ = bf16[96,1280]{1,0:T(8,128)(2,1)S(1)} collective-permute-done((bf16[96,1280]{1,0:T(8,128)(2,1)S(1)}, bf16[96,1280]{1,0:T(8,128)(2,1)S(1)}, u32[]{:S(2)}, u32[]{:S(2)}) %collective-permute-start.18) | collective-permute-done | bytes 245792 | tf_op jit(solution)/shard_map/ppermute | solution.py:18
  53.6 2.2 %collective-permute-start.9 = (bf16[96,1280]{1,0:T(8,128)(2,1)S(1)}, bf16[96,1280]{1,0:T(8,128)(2,1)S(1)}, u32[]{:S(2)}, u32[]{:S(2)}) collective-permute-start(bf16[96,1280]{1,0:T(8,128)(2,1)S(1)} %get-tuple-element.47.refs_0_), channel_id=1, source_target_pairs={{0,24},{1,7},{2,26},{3,1},{4,28},{5,3},{6,30},{7,5},{8,0},{9,15},{... | collective-permute-start | bytes 737288 | tf_op jit(solution)/shard_map/ppermute | solution.py:32
  56.6 5.3 %collective-permute-start.15 = (bf16[8,48,624]{2,1,0:T(8,128)(2,1)S(1)}, bf16[8,48,624]{2,1,0:T(8,128)(2,1)S(1)}, u32[]{:S(2)}, u32[]{:S(2)}) collective-permute-start(bf16[8,48,624]{2,1,0:T(8,128)(2,1)S(1)} %slice.24), channel_id=1, source_target_pairs={{0,32},{32,64},{64,96},{96,0},{1,33},{33,65},{65,97},{97,1},{2,34}... | collective-permute-start | bytes 1437704 | tf_op jit(solution)/shard_map/ppermute | solution.py:18
  63.7 1.5 collective-permute-start.22
  65.2 6.3 %collective-permute-done.10.refs_3_ = bf16[96,1280]{1,0:T(8,128)(2,1)S(1)} collective-permute-done((bf16[96,1280]{1,0:T(8,128)(2,1)S(1)}, bf16[96,1280]{1,0:T(8,128)(2,1)S(1)}, u32[]{:S(2)}, u32[]{:S(2)}) %collective-permute-start.10) | collective-permute-done | bytes 245792 | tf_op jit(solution)/shard_map/ppermute | solution.py:32
  71.5 7.8 %collective-permute-start.6 = (bf16[16,48,624]{2,1,0:T(8,128)(2,1)S(1)}, bf16[16,48,624]{2,1,0:T(8,128)(2,1)S(1)}, u32[]{:S(2)}, u32[]{:S(2)}) collective-permute-start(bf16[16,48,624]{2,1,0:T(8,128)(2,1)S(1)} %join.9.refs_0_), channel_id=1, source_target_pairs={{0,1},{1,0},{2,3},{3,2},{4,5},{5,4},{6,7},{7,6},{8,9},{9,8},{10,11... | collective-permute-start | bytes 2875400 | tf_op jit(solution)/shard_map/ppermute | solution.py:22
  80.8 2.7 %collective-permute-start.12 = (bf16[384,1280]{1,0:T(8,128)(2,1)S(1)}, bf16[384,1280]{1,0:T(8,128)(2,1)S(1)}, u32[]{:S(2)}, u32[]{:S(2)}) collective-permute-start(bf16[384,1280]{1,0:T(8,128)(2,1)S(1)} %join.10.refs_0_), channel_id=1, source_target_pairs={{0,6},{1,25},{2,0},{3,27},{4,2},{5,29},{6,4},{7,31},{8,14},{9,1},{... | collective-permute-start | bytes 2949128 | tf_op jit(solution)/shard_map/ppermute | solution.py:32
  83.6 18.2 %collective-permute-done.28.refs_3_ = bf16[288,1280]{1,0:T(8,128)(2,1)S(1)} collective-permute-done((bf16[288,1280]{1,0:T(8,128)(2,1)S(1)}, bf16[288,1280]{1,0:T(8,128)(2,1)S(1)}, u32[]{:S(2)}, u32[]{:S(2)}) %collective-permute-start.28) | collective-permute-done | bytes 737312 | tf_op jit(solution)/shard_map/ppermute | solution.py:32
  102.8 9.6 %collective-permute-done.29.refs_4_ = bf16[288,1280]{1,0:T(8,128)(2,1)S(1)} collective-permute-done((bf16[288,1280]{1,0:T(8,128)(2,1)S(1)}, bf16[288,1280]{1,0:T(8,128)(2,1)S(1)}, u32[]{:S(2)}, u32[]{:S(2)}) %collective-permute-start.29) | collective-permute-done | bytes 737312 | tf_op jit(solution)/shard_map/ppermute | solution.py:32
  112.4 9.1 %collective-permute-done.27.refs_2_ = bf16[288,1280]{1,0:T(8,128)(2,1)S(1)} collective-permute-done((bf16[288,1280]{1,0:T(8,128)(2,1)S(1)}, bf16[288,1280]{1,0:T(8,128)(2,1)S(1)}, u32[]{:S(2)}, u32[]{:S(2)}) %collective-permute-start.27) | collective-permute-done | bytes 737312 | tf_op jit(solution)/shard_map/ppermute | solution.py:32
  121.5 9.2 %collective-permute-done.25.refs_0_ = bf16[192,1280]{1,0:T(8,128)(2,1)S(1)} collective-permute-done((bf16[192,1280]{1,0:T(8,128)(2,1)S(1)}, bf16[192,1280]{1,0:T(8,128)(2,1)S(1)}, u32[]{:S(2)}, u32[]{:S(2)}) %collective-permute-start.25) | collective-permute-done | bytes 491552 | tf_op jit(solution)/shard_map/ppermute | solution.py:32
  130.8 2.7 %collective-permute-done.26.refs_1_ = bf16[192,1280]{1,0:T(8,128)(2,1)S(1)} collective-permute-done((bf16[192,1280]{1,0:T(8,128)(2,1)S(1)}, bf16[192,1280]{1,0:T(8,128)(2,1)S(1)}, u32[]{:S(2)}, u32[]{:S(2)}) %collective-permute-start.26) | collective-permute-done | bytes 491552 | tf_op jit(solution)/shard_map/ppermute | solution.py:32
  136.9 5.7 %collective-permute-done.34.refs_2_ = bf16[288,1280]{1,0:T(8,128)(2,1)S(1)} collective-permute-done((bf16[288,1280]{1,0:T(8,128)(2,1)S(1)}, bf16[288,1280]{1,0:T(8,128)(2,1)S(1)}, u32[]{:S(2)}, u32[]{:S(2)}) %collective-permute-start.34) | collective-permute-done | bytes 737312 | tf_op jit(solution)/shard_map/ppermute | solution.py:32
  144.1 2.4 %collective-permute-start.35 = (bf16[288,1280]{1,0:T(8,128)(2,1)S(1)}, bf16[288,1280]{1,0:T(8,128)(2,1)S(1)}, u32[]{:S(2)}, u32[]{:S(2)}) collective-permute-start(bf16[288,1280]{1,0:T(8,128)(2,1)S(1)} %collective-permute-done.33.refs_1_), channel_id=1, source_target_pairs={{0,6},{1,25},{2,0},{3,27},{4,2},{5,29},{6,4},{7,31},{8,14},{9,1},{... | collective-permute-start | bytes 2211848 | tf_op jit(solution)/shard_map/ppermute | solution.py:32
  146.5 4.0 %collective-permute-done.32.refs_0_ = bf16[288,1280]{1,0:T(8,128)(2,1)S(1)} collective-permute-done((bf16[288,1280]{1,0:T(8,128)(2,1)S(1)}, bf16[288,1280]{1,0:T(8,128)(2,1)S(1)}, u32[]{:S(2)}, u32[]{:S(2)}) %collective-permute-start.32) | collective-permute-done | bytes 737312 | tf_op jit(solution)/shard_map/ppermute | solution.py:32
  152.6 2.4 %convolution_add_fusion.3 = f32[624,1280]{1,0:T(8,128)S(1)} fusion(f32[624,1280]{1,0:T(8,128)S(1)} %fusion, bf16[1152,624]{1,0:T(8,128)(2,1)S(1)} %get-tuple-element.41, bf16[1152,1280]{1,0:T(8,128)(2,1)S(1)} %join.11), kind=kOutput, calls=%fused_computation.3 | convolution fusion | flops 1841049600 | bytes 10776576 | tf_op jit(solution)/shard_map/dot_general | solution.py:280
  157.2 3.2 %convolution_add_fusion.2 = f32[624,1280]{1,0:T(8,128)S(1)} fusion(f32[624,1280]{1,0:T(8,128)S(1)} %add.26, bf16[1728,624]{1,0:T(8,128)(2,1)S(1)} %get-tuple-element.54, bf16[1728,1280]{1,0:T(8,128)(2,1)S(1)} %join.16), kind=kOutput, calls=%fused_computation.2 | convolution fusion | flops 2761175040 | bytes 12969984 | tf_op jit(solution)/shard_map/dot_general | solution.py:280
  162.9 2.2 %convolution_add_fusion.1 = f32[624,1280]{1,0:T(8,128)S(1)} fusion(f32[624,1280]{1,0:T(8,128)S(1)} %add.29, bf16[864,624]{1,0:T(8,128)(2,1)S(1)} %get-tuple-element.57, bf16[864,1280]{1,0:T(8,128)(2,1)S(1)} %join.17), kind=kOutput, calls=%fused_computation.1 | convolution fusion | flops 1380986880 | bytes 9679872 | tf_op jit(solution)/shard_map/dot_general | solution.py:280
  166.3 2.6 %collective-permute-start.36 = (f32[312,1280]{1,0:T(8,128)S(1)}, f32[312,1280]{1,0:T(8,128)S(1)}, u32[]{:S(2)}, u32[]{:S(2)}) collective-permute-start(f32[312,1280]{1,0:T(8,128)S(1)} %get-tuple-element.59), channel_id=1, source_target_pairs={{0,1},{1,0},{2,3},{3,2},{4,5},{5,4},{6,7},{7,6},{8,9},{9,8},{10,11... | collective-permute-start | bytes 4792328 | tf_op jit(solution)/shard_map/ppermute | solution.py:22
  170.2 1.8 %collective-permute-done.36.half_ref = f32[312,1280]{1,0:T(8,128)S(1)} collective-permute-done((f32[312,1280]{1,0:T(8,128)S(1)}, f32[312,1280]{1,0:T(8,128)S(1)}, u32[]{:S(2)}, u32[]{:S(2)}) %collective-permute-start.36) | collective-permute-done | bytes 1597472 | tf_op jit(solution)/shard_map/ppermute | solution.py:22
  (82 shorter events, 32.6 us)
Async XLA Ops:
  3.0 8.5 %collective-permute-start = (bf16[4,48,624]{2,1,0:T(8,128)(2,1)S(1)}, bf16[4,48,624]{2,1,0:T(8,128)(2,1)S(1)}, u32[]{:S(2)}, u32[]{:S(2)}) collective-permute-start(bf16[4,48,624]{2,1,0:T(8,128)(2,1)S(1)} %get-tuple-element.34), channel_id=1, source_target_pairs={{0,8},{1,3},{2,10},{3,5},{4,12},{5,7},{6,14},{7,1},{8,16},{9,11},{... | collective-permute-start | bytes 718856 | tf_op jit(solution)/shard_map/ppermute | solution.py:32
  5.6 8.0 %collective-permute-start.1 = (bf16[4,48,624]{2,1,0:T(8,128)(2,1)S(1)}, bf16[4,48,624]{2,1,0:T(8,128)(2,1)S(1)}, u32[]{:S(2)}, u32[]{:S(2)}) collective-permute-start(bf16[4,48,624]{2,1,0:T(8,128)(2,1)S(1)} %get-tuple-element.35), channel_id=1, source_target_pairs={{0,24},{1,7},{2,26},{3,1},{4,28},{5,3},{6,30},{7,5},{8,0},{9,15},{... | collective-permute-start | bytes 718856 | tf_op jit(solution)/shard_map/ppermute | solution.py:32
  7.8 7.5 %collective-permute-start.2 = (bf16[4,48,624]{2,1,0:T(8,128)(2,1)S(1)}, bf16[4,48,624]{2,1,0:T(8,128)(2,1)S(1)}, u32[]{:S(2)}, u32[]{:S(2)}) collective-permute-start(bf16[4,48,624]{2,1,0:T(8,128)(2,1)S(1)} %get-tuple-element.36), channel_id=1, source_target_pairs={{0,16},{1,5},{2,18},{3,7},{4,20},{5,1},{6,22},{7,3},{8,24},{9,13},... | collective-permute-start | bytes 718856 | tf_op jit(solution)/shard_map/ppermute | solution.py:32
  25.5 31.0 %collective-permute-start.14 = (bf16[16,48,624]{2,1,0:T(8,128)(2,1)S(1)}, bf16[16,48,624]{2,1,0:T(8,128)(2,1)S(1)}, u32[]{:S(2)}, u32[]{:S(2)}) collective-permute-start(bf16[16,48,624]{2,1,0:T(8,128)(2,1)S(1)} %join.9.refs_0_), channel_id=1, source_target_pairs={{0,32},{32,64},{64,96},{96,0},{1,33},{33,65},{65,97},{97,1},{2,34}... | collective-permute-start | bytes 2875400 | tf_op jit(solution)/shard_map/ppermute | solution.py:18
  26.9 35.0 %collective-permute-start.13 = (bf16[16,48,624]{2,1,0:T(8,128)(2,1)S(1)}, bf16[16,48,624]{2,1,0:T(8,128)(2,1)S(1)}, u32[]{:S(2)}, u32[]{:S(2)}) collective-permute-start(bf16[16,48,624]{2,1,0:T(8,128)(2,1)S(1)} %join.9.refs_0_), channel_id=1, source_target_pairs={{0,96},{32,0},{64,32},{96,64},{1,97},{33,1},{65,33},{97,65},{2,98}... | collective-permute-start | bytes 2875400 | tf_op jit(solution)/shard_map/ppermute | solution.py:18
  33.0 19.4 %collective-permute-start.18 = (bf16[96,1280]{1,0:T(8,128)(2,1)S(1)}, bf16[96,1280]{1,0:T(8,128)(2,1)S(1)}, u32[]{:S(2)}, u32[]{:S(2)}) collective-permute-start(bf16[96,1280]{1,0:T(8,128)(2,1)S(1)} %get-tuple-element.49), channel_id=1, source_target_pairs={{0,96},{32,0},{64,32},{96,64},{1,97},{33,1},{65,33},{97,65},{2,98}... | collective-permute-start | bytes 737288 | tf_op jit(solution)/shard_map/ppermute | solution.py:18
  34.6 19.0 %collective-permute-start.19 = (bf16[96,1280]{1,0:T(8,128)(2,1)S(1)}, bf16[96,1280]{1,0:T(8,128)(2,1)S(1)}, u32[]{:S(2)}, u32[]{:S(2)}) collective-permute-start(bf16[96,1280]{1,0:T(8,128)(2,1)S(1)} %get-tuple-element.50), channel_id=1, source_target_pairs={{0,64},{32,96},{64,0},{96,32},{1,65},{33,97},{65,1},{97,33},{2,66}... | collective-permute-start | bytes 737288 | tf_op jit(solution)/shard_map/ppermute | solution.py:18
  35.0 21.0 %collective-permute-start.20 = (bf16[96,1280]{1,0:T(8,128)(2,1)S(1)}, bf16[96,1280]{1,0:T(8,128)(2,1)S(1)}, u32[]{:S(2)}, u32[]{:S(2)}) collective-permute-start(bf16[96,1280]{1,0:T(8,128)(2,1)S(1)} %get-tuple-element.51), channel_id=1, source_target_pairs={{0,32},{32,64},{64,96},{96,0},{1,33},{33,65},{65,97},{97,1},{2,34}... | collective-permute-start | bytes 737288 | tf_op jit(solution)/shard_map/ppermute | solution.py:18
  52.5 10.6 %collective-permute-start.8 = (bf16[96,1280]{1,0:T(8,128)(2,1)S(1)}, bf16[96,1280]{1,0:T(8,128)(2,1)S(1)}, u32[]{:S(2)}, u32[]{:S(2)}) collective-permute-start(bf16[96,1280]{1,0:T(8,128)(2,1)S(1)} %get-tuple-element.47.refs_0_), channel_id=1, source_target_pairs={{0,8},{1,3},{2,10},{3,5},{4,12},{5,7},{6,14},{7,1},{8,16},{9,11},{... | collective-permute-start | bytes 737288 | tf_op jit(solution)/shard_map/ppermute | solution.py:32
  53.6 10.1 %collective-permute-start.9 = (bf16[96,1280]{1,0:T(8,128)(2,1)S(1)}, bf16[96,1280]{1,0:T(8,128)(2,1)S(1)}, u32[]{:S(2)}, u32[]{:S(2)}) collective-permute-start(bf16[96,1280]{1,0:T(8,128)(2,1)S(1)} %get-tuple-element.47.refs_0_), channel_id=1, source_target_pairs={{0,24},{1,7},{2,26},{3,1},{4,28},{5,3},{6,30},{7,5},{8,0},{9,15},{... | collective-permute-start | bytes 737288 | tf_op jit(solution)/shard_map/ppermute | solution.py:32
  56.0 24.8 %collective-permute-start.21 = (bf16[288,1280]{1,0:T(8,128)(2,1)S(1)}, bf16[288,1280]{1,0:T(8,128)(2,1)S(1)}, u32[]{:S(2)}, u32[]{:S(2)}) collective-permute-start(bf16[288,1280]{1,0:T(8,128)(2,1)S(1)} %join.13.refs_0_), channel_id=1, source_target_pairs={{0,8},{1,3},{2,10},{3,5},{4,12},{5,7},{6,14},{7,1},{8,16},{9,11},{... | collective-permute-start | bytes 2211848 | tf_op jit(solution)/shard_map/ppermute | solution.py:32
  56.6 22.8 %collective-permute-start.15 = (bf16[8,48,624]{2,1,0:T(8,128)(2,1)S(1)}, bf16[8,48,624]{2,1,0:T(8,128)(2,1)S(1)}, u32[]{:S(2)}, u32[]{:S(2)}) collective-permute-start(bf16[8,48,624]{2,1,0:T(8,128)(2,1)S(1)} %slice.24), channel_id=1, source_target_pairs={{0,32},{32,64},{64,96},{96,0},{1,33},{33,65},{65,97},{97,1},{2,34}... | collective-permute-start | bytes 1437704 | tf_op jit(solution)/shard_map/ppermute | solution.py:18
  61.9 9.6 %collective-permute-start.10 = (bf16[96,1280]{1,0:T(8,128)(2,1)S(1)}, bf16[96,1280]{1,0:T(8,128)(2,1)S(1)}, u32[]{:S(2)}, u32[]{:S(2)}) collective-permute-start(bf16[96,1280]{1,0:T(8,128)(2,1)S(1)} %get-tuple-element.47.refs_0_), channel_id=1, source_target_pairs={{0,16},{1,5},{2,18},{3,7},{4,20},{5,1},{6,22},{7,3},{8,24},{9,13},... | collective-permute-start | bytes 737288 | tf_op jit(solution)/shard_map/ppermute | solution.py:32
  63.1 16.3 %collective-permute-start.16 = (bf16[8,48,624]{2,1,0:T(8,128)(2,1)S(1)}, bf16[8,48,624]{2,1,0:T(8,128)(2,1)S(1)}, u32[]{:S(2)}, u32[]{:S(2)}) collective-permute-start(bf16[8,48,624]{2,1,0:T(8,128)(2,1)S(1)} %slice.25), channel_id=1, source_target_pairs={{0,96},{32,0},{64,32},{96,64},{1,97},{33,1},{65,33},{97,65},{2,98}... | collective-permute-start | bytes 1437704 | tf_op jit(solution)/shard_map/ppermute | solution.py:18
  63.7 17.1 %collective-permute-start.22 = (bf16[288,1280]{1,0:T(8,128)(2,1)S(1)}, bf16[288,1280]{1,0:T(8,128)(2,1)S(1)}, u32[]{:S(2)}, u32[]{:S(2)}) collective-permute-start(bf16[288,1280]{1,0:T(8,128)(2,1)S(1)} %join.13.refs_0_), channel_id=1, source_target_pairs={{0,24},{1,7},{2,26},{3,1},{4,28},{5,3},{6,30},{7,5},{8,0},{9,15},{... | collective-permute-start | bytes 2211848 | tf_op jit(solution)/shard_map/ppermute | solution.py:32
  71.5 12.1 %collective-permute-start.6 = (bf16[16,48,624]{2,1,0:T(8,128)(2,1)S(1)}, bf16[16,48,624]{2,1,0:T(8,128)(2,1)S(1)}, u32[]{:S(2)}, u32[]{:S(2)}) collective-permute-start(bf16[16,48,624]{2,1,0:T(8,128)(2,1)S(1)} %join.9.refs_0_), channel_id=1, source_target_pairs={{0,1},{1,0},{2,3},{3,2},{4,5},{5,4},{6,7},{7,6},{8,9},{9,8},{10,11... | collective-permute-start | bytes 2875400 | tf_op jit(solution)/shard_map/ppermute | solution.py:22
  79.4 22.4 %collective-permute-start.11 = (bf16[384,1280]{1,0:T(8,128)(2,1)S(1)}, bf16[384,1280]{1,0:T(8,128)(2,1)S(1)}, u32[]{:S(2)}, u32[]{:S(2)}) collective-permute-start(bf16[384,1280]{1,0:T(8,128)(2,1)S(1)} %join.10.refs_0_), channel_id=1, source_target_pairs={{0,2},{1,9},{2,4},{3,11},{4,6},{5,13},{6,0},{7,15},{8,10},{9,17},{... | collective-permute-start | bytes 2949128 | tf_op jit(solution)/shard_map/ppermute | solution.py:32
  79.7 70.9 %collective-permute-start.17 = (bf16[48,48,624]{2,1,0:T(8,128)(2,1)S(1)}, bf16[48,48,624]{2,1,0:T(8,128)(2,1)S(1)}, u32[]{:S(2)}, u32[]{:S(2)}) collective-permute-start(bf16[48,48,624]{2,1,0:T(8,128)(2,1)S(1)} %join.12.refs_0_), channel_id=1, source_target_pairs={{0,1},{1,0},{2,3},{3,2},{4,5},{5,4},{6,7},{7,6},{8,9},{9,8},{10,11... | collective-permute-start | bytes 8626184 | tf_op jit(solution)/shard_map/ppermute | solution.py:22
  80.8 21.0 %collective-permute-start.28 = (bf16[288,1280]{1,0:T(8,128)(2,1)S(1)}, bf16[288,1280]{1,0:T(8,128)(2,1)S(1)}, u32[]{:S(2)}, u32[]{:S(2)}) collective-permute-start(bf16[288,1280]{1,0:T(8,128)(2,1)S(1)} %join.13.refs_0_), channel_id=1, source_target_pairs={{0,2},{1,9},{2,4},{3,11},{4,6},{5,13},{6,0},{7,15},{8,10},{9,17},{... | collective-permute-start | bytes 2211848 | tf_op jit(solution)/shard_map/ppermute | solution.py:32
  80.8 21.5 %collective-permute-start.12 = (bf16[384,1280]{1,0:T(8,128)(2,1)S(1)}, bf16[384,1280]{1,0:T(8,128)(2,1)S(1)}, u32[]{:S(2)}, u32[]{:S(2)}) collective-permute-start(bf16[384,1280]{1,0:T(8,128)(2,1)S(1)} %join.10.refs_0_), channel_id=1, source_target_pairs={{0,6},{1,25},{2,0},{3,27},{4,2},{5,29},{6,4},{7,31},{8,14},{9,1},{... | collective-permute-start | bytes 2949128 | tf_op jit(solution)/shard_map/ppermute | solution.py:32
  83.6 51.1 %collective-permute-start.23 = (bf16[576,1280]{1,0:T(8,128)(2,1)S(1)}, bf16[576,1280]{1,0:T(8,128)(2,1)S(1)}, u32[]{:S(2)}, u32[]{:S(2)}) collective-permute-start(bf16[576,1280]{1,0:T(8,128)(2,1)S(1)} %join.14.refs_1_), channel_id=1, source_target_pairs={{0,2},{1,9},{2,4},{3,11},{4,6},{5,13},{6,0},{7,15},{8,10},{9,17},{... | collective-permute-start | bytes 4423688 | tf_op jit(solution)/shard_map/ppermute | solution.py:32
  101.8 10.6 %collective-permute-start.29 = (bf16[288,1280]{1,0:T(8,128)(2,1)S(1)}, bf16[288,1280]{1,0:T(8,128)(2,1)S(1)}, u32[]{:S(2)}, u32[]{:S(2)}) collective-permute-start(bf16[288,1280]{1,0:T(8,128)(2,1)S(1)} %join.13.refs_0_), channel_id=1, source_target_pairs={{0,6},{1,25},{2,0},{3,27},{4,2},{5,29},{6,4},{7,31},{8,14},{9,1},{... | collective-permute-start | bytes 2211848 | tf_op jit(solution)/shard_map/ppermute | solution.py:32
  101.8 19.7 %collective-permute-start.27 = (bf16[288,1280]{1,0:T(8,128)(2,1)S(1)}, bf16[288,1280]{1,0:T(8,128)(2,1)S(1)}, u32[]{:S(2)}, u32[]{:S(2)}) collective-permute-start(bf16[288,1280]{1,0:T(8,128)(2,1)S(1)} %collective-permute-done.21.refs_0_), channel_id=1, source_target_pairs={{0,8},{1,3},{2,10},{3,5},{4,12},{5,7},{6,14},{7,1},{8,16},{9,11},{... | collective-permute-start | bytes 2211848 | tf_op jit(solution)/shard_map/ppermute | solution.py:32
  102.2 34.5 %collective-permute-start.24 = (bf16[576,1280]{1,0:T(8,128)(2,1)S(1)}, bf16[576,1280]{1,0:T(8,128)(2,1)S(1)}, u32[]{:S(2)}, u32[]{:S(2)}) collective-permute-start(bf16[576,1280]{1,0:T(8,128)(2,1)S(1)} %join.14.refs_1_), channel_id=1, source_target_pairs={{0,6},{1,25},{2,0},{3,27},{4,2},{5,29},{6,4},{7,31},{8,14},{9,1},{... | collective-permute-start | bytes 4423688 | tf_op jit(solution)/shard_map/ppermute | solution.py:32
  112.4 18.4 %collective-permute-start.25 = (bf16[192,1280]{1,0:T(8,128)(2,1)S(1)}, bf16[192,1280]{1,0:T(8,128)(2,1)S(1)}, u32[]{:S(2)}, u32[]{:S(2)}) collective-permute-start(bf16[192,1280]{1,0:T(8,128)(2,1)S(1)} %slice.26), channel_id=1, source_target_pairs={{0,2},{1,9},{2,4},{3,11},{4,6},{5,13},{6,0},{7,15},{8,10},{9,17},{... | collective-permute-start | bytes 1474568 | tf_op jit(solution)/shard_map/ppermute | solution.py:32
  121.5 11.9 %collective-permute-start.26 = (bf16[192,1280]{1,0:T(8,128)(2,1)S(1)}, bf16[192,1280]{1,0:T(8,128)(2,1)S(1)}, u32[]{:S(2)}, u32[]{:S(2)}) collective-permute-start(bf16[192,1280]{1,0:T(8,128)(2,1)S(1)} %slice.27), channel_id=1, source_target_pairs={{0,6},{1,25},{2,0},{3,27},{4,2},{5,29},{6,4},{7,31},{8,14},{9,1},{... | collective-permute-start | bytes 1474568 | tf_op jit(solution)/shard_map/ppermute | solution.py:32
  130.8 11.8 %collective-permute-start.34 = (bf16[288,1280]{1,0:T(8,128)(2,1)S(1)}, bf16[288,1280]{1,0:T(8,128)(2,1)S(1)}, u32[]{:S(2)}, u32[]{:S(2)}) collective-permute-start(bf16[288,1280]{1,0:T(8,128)(2,1)S(1)} %collective-permute-done.28.refs_3_), channel_id=1, source_target_pairs={{0,2},{1,9},{2,4},{3,11},{4,6},{5,13},{6,0},{7,15},{8,10},{9,17},{... | collective-permute-start | bytes 2211848 | tf_op jit(solution)/shard_map/ppermute | solution.py:32
  133.5 10.6 %collective-permute-start.33 = (bf16[288,1280]{1,0:T(8,128)(2,1)S(1)}, bf16[288,1280]{1,0:T(8,128)(2,1)S(1)}, u32[]{:S(2)}, u32[]{:S(2)}) collective-permute-start(bf16[288,1280]{1,0:T(8,128)(2,1)S(1)} %collective-permute-done.27.refs_2_), channel_id=1, source_target_pairs={{0,6},{1,25},{2,0},{3,27},{4,2},{5,29},{6,4},{7,31},{8,14},{9,1},{... | collective-permute-start | bytes 2211848 | tf_op jit(solution)/shard_map/ppermute | solution.py:32
  134.7 15.8 %collective-permute-start.32 = (bf16[288,1280]{1,0:T(8,128)(2,1)S(1)}, bf16[288,1280]{1,0:T(8,128)(2,1)S(1)}, u32[]{:S(2)}, u32[]{:S(2)}) collective-permute-start(bf16[288,1280]{1,0:T(8,128)(2,1)S(1)} %collective-permute-done.27.refs_2_), channel_id=1, source_target_pairs={{0,2},{1,9},{2,4},{3,11},{4,6},{5,13},{6,0},{7,15},{8,10},{9,17},{... | collective-permute-start | bytes 2211848 | tf_op jit(solution)/shard_map/ppermute | solution.py:32
  136.8 23.7 %collective-permute-start.30 = (bf16[144,1280]{1,0:T(8,128)(2,1)S(1)}, bf16[144,1280]{1,0:T(8,128)(2,1)S(1)}, u32[]{:S(2)}, u32[]{:S(2)}) collective-permute-start(bf16[144,1280]{1,0:T(8,128)(2,1)S(1)} %slice.28), channel_id=1, source_target_pairs={{0,2},{1,9},{2,4},{3,11},{4,6},{5,13},{6,0},{7,15},{8,10},{9,17},{... | collective-permute-start | bytes 1105928 | tf_op jit(solution)/shard_map/ppermute | solution.py:32
  142.6 18.9 %collective-permute-start.31 = (bf16[432,1280]{1,0:T(8,128)(2,1)S(1)}, bf16[432,1280]{1,0:T(8,128)(2,1)S(1)}, u32[]{:S(2)}, u32[]{:S(2)}) collective-permute-start(bf16[432,1280]{1,0:T(8,128)(2,1)S(1)} %slice.29), channel_id=1, source_target_pairs={{0,6},{1,25},{2,0},{3,27},{4,2},{5,29},{6,4},{7,31},{8,14},{9,1},{... | collective-permute-start | bytes 3317768 | tf_op jit(solution)/shard_map/ppermute | solution.py:32
  144.1 21.0 %collective-permute-start.35 = (bf16[288,1280]{1,0:T(8,128)(2,1)S(1)}, bf16[288,1280]{1,0:T(8,128)(2,1)S(1)}, u32[]{:S(2)}, u32[]{:S(2)}) collective-permute-start(bf16[288,1280]{1,0:T(8,128)(2,1)S(1)} %collective-permute-done.33.refs_1_), channel_id=1, source_target_pairs={{0,6},{1,25},{2,0},{3,27},{4,2},{5,29},{6,4},{7,31},{8,14},{9,1},{... | collective-permute-start | bytes 2211848 | tf_op jit(solution)/shard_map/ppermute | solution.py:32
  (7 other events, 33.5 us)

commit v8 on v7

--- a/solution.py
+++ b/solution.py
@@ -183,9 +183,9 @@
     first = at(0, 0, -1, 1, 2) + at(-1, 0) + at(1, 0)
     parts = [(first, 0, join([own, near, far, *own_sides]))]
     parts += [(at(v, -1, 1), 0, block) for v, block in zip((-1, 1), near_sides)]
-    parts += [(at(-1, 2) + at(1, 2) + at(2, 0), 0, join([*far_sides, own_opposite]))]
+    parts += [(at(-1, 2) + at(1, 2), 0, join(far_sides))]
     parts += [(at(2, -1, 1), 0, near_opposite[0]), (at(2, -1, 1), len(OTHERS) // 2, near_opposite[1])]
-    parts += [(at(2, 2), 0, far_opposite)]
+    parts += [(at(2, 2), 0, far_opposite), (at(2, 0), 0, own_opposite)]
     return parts
 
 
@@ -288,7 +288,7 @@
         layout.append(blocks[skipped : skipped + block.shape[0] // rows.shape[1]])
     weights = (*arrange(layout, rest, other_rest), weights[1])
     blocks = [block for *_, block in parts] + [early[1][1]]
-    for i in (1, 2, len(parts), 0, 4, 5, 3, *range(6, len(parts))):
+    for i in (1, 2, len(parts), 3, 0, *range(4, len(parts))):
         tile = lax.optimization_barrier(tile + product(weights[i], blocks[i]))
 
     kept, sent = halve(tile)

time: 173 us -> 184 us (1.064)
  starting transfers between devices: 49.8 us -> 60.4 us
    ppermute x4, starting transfers between devices: 14.6 us -> 22.2 us  [swap_cores(): return lax.ppermute(block, 'core', [(0, 1), (1, 0)])]
    ppermute x26, starting transfers between devices: 23.8 us -> 29.9 us  [along_plane(): return lax.ppermute(block, ('x', 'z', 'core'), route)]
    ppermute x7, starting transfers between devices: 11.4 us -> 8.31 us  [along_y(): lax.ppermute(block, 'y', [(i, (i + step) % SIDE) for i in range(SIDE)])]
    dot_general x9 -> x10, matrix products: 14.3 us -> 14.8 us  [product(): lax.dot_general(weight, block, (((0,), (0,)), ((), ())), preferred_elemen...]
  transfers between devices with their start and end apart: 37 -> 37, of which waited for: 20 -> 19; matrix products, arithmetic and copies ran while one was open for 9% -> 9% of each run, Pallas kernels for 2% -> 2%
where the time goes in v8:
time: 184 us
  waiting for transfers between devices  98.5 us (54%)
  starting transfers between devices  60.4 us (33%)
  matrix products  14.8 us (8%)
  Pallas kernels  5.82 us (3%)
  other arithmetic  2.37 us (1%)
  local copies, waits for them, and re-layouts  2.1 us (1%)
    ppermute x26, waiting for transfers between devices, along_plane(): return lax.ppermute(block, ('x', 'z', 'core'), route)  77.9 us
    ppermute x26, starting transfers between devices, along_plane(): return lax.ppermute(block, ('x', 'z', 'core'), route)  29.9 us
    ppermute x4, starting transfers between devices, swap_cores(): return lax.ppermute(block, 'core', [(0, 1), (1, 0)])  22.2 us
    ppermute x7, waiting for transfers between devices, along_y(): lax.ppermute(block, 'y', [(i, (i + step) % SIDE) for i in range(SIDE)])  17.3 us
    dot_general x10, matrix products, product(): lax.dot_general(weight, block, (((0,), (0,)), ((), ())), preferred_elemen...  14.8 us
    ppermute x7, starting transfers between devices, along_y(): lax.ppermute(block, 'y', [(i, (i + step) % SIDE) for i in range(SIDE)])  8.31 us
  transfers between devices with their start and end apart: 37, of which 19 were waited for; matrix products, arithmetic and copies ran while one was open for 9% of the time, Pallas kernels for 2%

profile of v8, /device:TPU:1, one launch (start us, length us, event | category | flops | bytes accessed | tf_op | source)
XLA Modules:
  0.0 184.3 jit_solution(7425386487510716568)
XLA Ops:
  3.0 2.5 %collective-permute-start = (bf16[4,48,624]{2,1,0:T(8,128)(2,1)S(1)}, bf16[4,48,624]{2,1,0:T(8,128)(2,1)S(1)}, u32[]{:S(2)}, u32[]{:S(2)}) collective-permute-start(bf16[4,48,624]{2,1,0:T(8,128)(2,1)S(1)} %get-tuple-element.35), channel_id=1, source_target_pairs={{0,8},{1,3},{2,10},{3,5},{4,12},{5,7},{6,14},{7,1},{8,16},{9,11},{... | collective-permute-start | bytes 718856 | tf_op jit(solution)/shard_map/ppermute | solution.py:32
  5.6 2.2 %collective-permute-start.1 = (bf16[4,48,624]{2,1,0:T(8,128)(2,1)S(1)}, bf16[4,48,624]{2,1,0:T(8,128)(2,1)S(1)}, u32[]{:S(2)}, u32[]{:S(2)}) collective-permute-start(bf16[4,48,624]{2,1,0:T(8,128)(2,1)S(1)} %get-tuple-element.36), channel_id=1, source_target_pairs={{0,24},{1,7},{2,26},{3,1},{4,28},{5,3},{6,30},{7,5},{8,0},{9,15},{... | collective-permute-start | bytes 718856 | tf_op jit(solution)/shard_map/ppermute | solution.py:32
  9.0 2.5 %collective-permute-done.refs_1_ = bf16[4,48,624]{2,1,0:T(8,128)(2,1)S(1)} collective-permute-done((bf16[4,48,624]{2,1,0:T(8,128)(2,1)S(1)}, bf16[4,48,624]{2,1,0:T(8,128)(2,1)S(1)}, u32[]{:S(2)}, u32[]{:S(2)}) %collective-permute-start) | collective-permute-done | bytes 239648 | tf_op jit(solution)/shard_map/ppermute | solution.py:32
  11.5 2.0 %collective-permute-done.1.refs_2_ = bf16[4,48,624]{2,1,0:T(8,128)(2,1)S(1)} collective-permute-done((bf16[4,48,624]{2,1,0:T(8,128)(2,1)S(1)}, bf16[4,48,624]{2,1,0:T(8,128)(2,1)S(1)}, u32[]{:S(2)}, u32[]{:S(2)}) %collective-permute-start.1) | collective-permute-done | bytes 239648 | tf_op jit(solution)/shard_map/ppermute | solution.py:32
  13.5 1.7 collective-permute-done.2.refs_3_
  16.4 1.6 collective-permute-start.4
  19.4 2.5 %collective-permute-done.3.refs_1_ = bf16[4,48,624]{2,1,0:T(8,128)(2,1)S(1)} collective-permute-done((bf16[4,48,624]{2,1,0:T(8,128)(2,1)S(1)}, bf16[4,48,624]{2,1,0:T(8,128)(2,1)S(1)}, u32[]{:S(2)}, u32[]{:S(2)}) %collective-permute-start.3) | collective-permute-done | bytes 239648 | tf_op jit(solution)/shard_map/ppermute | solution.py:32
  21.9 1.9 %collective-permute-done.4.refs_2_ = bf16[4,48,624]{2,1,0:T(8,128)(2,1)S(1)} collective-permute-done((bf16[4,48,624]{2,1,0:T(8,128)(2,1)S(1)}, bf16[4,48,624]{2,1,0:T(8,128)(2,1)S(1)}, u32[]{:S(2)}, u32[]{:S(2)}) %collective-permute-start.4) | collective-permute-done | bytes 239648 | tf_op jit(solution)/shard_map/ppermute | solution.py:32
  28.4 3.1 %collective-permute-start.7 = (bf16[4,48,1280]{2,1,0:T(8,128)(2,1)S(1)}, bf16[4,48,1280]{2,1,0:T(8,128)(2,1)S(1)}, u32[]{:S(2)}, u32[]{:S(2)}) collective-permute-start(bf16[4,48,1280]{2,1,0:T(8,128)(2,1)S(1)} %get-tuple-element.47), channel_id=1, source_target_pairs={{0,1},{1,0},{2,3},{3,2},{4,5},{5,4},{6,7},{7,6},{8,9},{9,8},{10,11... | collective-permute-start | bytes 1474568 | tf_op jit(solution)/shard_map/ppermute | solution.py:22
  35.7 11.9 %collective-permute-done.14.refs_3_ = bf16[16,48,624]{2,1,0:T(8,128)(2,1)S(1)} collective-permute-done((bf16[16,48,624]{2,1,0:T(8,128)(2,1)S(1)}, bf16[16,48,624]{2,1,0:T(8,128)(2,1)S(1)}, u32[]{:S(2)}, u32[]{:S(2)}) %collective-permute-start.14) | collective-permute-done | bytes 958496 | tf_op jit(solution)/shard_map/ppermute | solution.py:18
  47.7 2.7 %collective-permute-start.16 = (bf16[8,48,624]{2,1,0:T(8,128)(2,1)S(1)}, bf16[8,48,624]{2,1,0:T(8,128)(2,1)S(1)}, u32[]{:S(2)}, u32[]{:S(2)}) collective-permute-start(bf16[8,48,624]{2,1,0:T(8,128)(2,1)S(1)} %slice.25), channel_id=1, source_target_pairs={{0,96},{32,0},{64,32},{96,64},{1,97},{33,1},{65,33},{97,65},{2,98}... | collective-permute-start | bytes 1437704 | tf_op jit(solution)/shard_map/ppermute | solution.py:18
  50.4 2.0 %collective-permute-done.18.refs_0_ = bf16[96,1280]{1,0:T(8,128)(2,1)S(1)} collective-permute-done((bf16[96,1280]{1,0:T(8,128)(2,1)S(1)}, bf16[96,1280]{1,0:T(8,128)(2,1)S(1)}, u32[]{:S(2)}, u32[]{:S(2)}) %collective-permute-start.18) | collective-permute-done | bytes 245792 | tf_op jit(solution)/shard_map/ppermute | solution.py:18
  52.5 11.4 %collective-permute-start.6 = (bf16[16,48,624]{2,1,0:T(8,128)(2,1)S(1)}, bf16[16,48,624]{2,1,0:T(8,128)(2,1)S(1)}, u32[]{:S(2)}, u32[]{:S(2)}) collective-permute-start(bf16[16,48,624]{2,1,0:T(8,128)(2,1)S(1)} %join.9.refs_0_), channel_id=1, source_target_pairs={{0,1},{1,0},{2,3},{3,2},{4,5},{5,4},{6,7},{7,6},{8,9},{9,8},{10,11... | collective-permute-start | bytes 2875400 | tf_op jit(solution)/shard_map/ppermute | solution.py:22
  65.2 3.4 %collective-permute-done.15.refs_1_ = bf16[8,48,624]{2,1,0:T(8,128)(2,1)S(1)} collective-permute-done((bf16[8,48,624]{2,1,0:T(8,128)(2,1)S(1)}, bf16[8,48,624]{2,1,0:T(8,128)(2,1)S(1)}, u32[]{:S(2)}, u32[]{:S(2)}) %collective-permute-start.15) | collective-permute-done | bytes 479264 | tf_op jit(solution)/shard_map/ppermute | solution.py:18
  68.6 2.2 %collective-permute-start.9 = (bf16[96,1280]{1,0:T(8,128)(2,1)S(1)}, bf16[96,1280]{1,0:T(8,128)(2,1)S(1)}, u32[]{:S(2)}, u32[]{:S(2)}) collective-permute-start(bf16[96,1280]{1,0:T(8,128)(2,1)S(1)} %get-tuple-element.48.refs_0_), channel_id=1, source_target_pairs={{0,24},{1,7},{2,26},{3,1},{4,28},{5,3},{6,30},{7,5},{8,0},{9,15},{... | collective-permute-start | bytes 737288 | tf_op jit(solution)/shard_map/ppermute | solution.py:32
  71.2 7.2 %collective-permute-done.8.refs_1_ = bf16[96,1280]{1,0:T(8,128)(2,1)S(1)} collective-permute-done((bf16[96,1280]{1,0:T(8,128)(2,1)S(1)}, bf16[96,1280]{1,0:T(8,128)(2,1)S(1)}, u32[]{:S(2)}, u32[]{:S(2)}) %collective-permute-start.8) | collective-permute-done | bytes 245792 | tf_op jit(solution)/shard_map/ppermute | solution.py:32
  82.2 2.7 %collective-permute-start.12 = (bf16[384,1280]{1,0:T(8,128)(2,1)S(1)}, bf16[384,1280]{1,0:T(8,128)(2,1)S(1)}, u32[]{:S(2)}, u32[]{:S(2)}) collective-permute-start(bf16[384,1280]{1,0:T(8,128)(2,1)S(1)} %join.10.refs_0_), channel_id=1, source_target_pairs={{0,6},{1,25},{2,0},{3,27},{4,2},{5,29},{6,4},{7,31},{8,14},{9,1},{... | collective-permute-start | bytes 2949128 | tf_op jit(solution)/shard_map/ppermute | solution.py:32
  84.8 7.5 %collective-permute-done.22.refs_1_ = bf16[288,1280]{1,0:T(8,128)(2,1)S(1)} collective-permute-done((bf16[288,1280]{1,0:T(8,128)(2,1)S(1)}, bf16[288,1280]{1,0:T(8,128)(2,1)S(1)}, u32[]{:S(2)}, u32[]{:S(2)}) %collective-permute-start.22) | collective-permute-done | bytes 737312 | tf_op jit(solution)/shard_map/ppermute | solution.py:32
  92.3 1.8 collective-permute-start.31
  94.8 9.2 %collective-permute-done.11.refs_1_ = bf16[384,1280]{1,0:T(8,128)(2,1)S(1)} collective-permute-done((bf16[384,1280]{1,0:T(8,128)(2,1)S(1)}, bf16[384,1280]{1,0:T(8,128)(2,1)S(1)}, u32[]{:S(2)}, u32[]{:S(2)}) %collective-permute-start.11) | collective-permute-done | bytes 983072 | tf_op jit(solution)/shard_map/ppermute | solution.py:32
  104.0 2.8 %collective-permute-start.24 = (bf16[576,1280]{1,0:T(8,128)(2,1)S(1)}, bf16[576,1280]{1,0:T(8,128)(2,1)S(1)}, u32[]{:S(2)}, u32[]{:S(2)}) collective-permute-start(bf16[576,1280]{1,0:T(8,128)(2,1)S(1)} %join.14.refs_1_), channel_id=1, source_target_pairs={{0,6},{1,25},{2,0},{3,27},{4,2},{5,29},{6,4},{7,31},{8,14},{9,1},{... | collective-permute-start | bytes 4423688 | tf_op jit(solution)/shard_map/ppermute | solution.py:32
  106.8 4.4 %collective-permute-done.31.refs_4_ = bf16[288,1280]{1,0:T(8,128)(2,1)S(1)} collective-permute-done((bf16[288,1280]{1,0:T(8,128)(2,1)S(1)}, bf16[288,1280]{1,0:T(8,128)(2,1)S(1)}, u32[]{:S(2)}, u32[]{:S(2)}) %collective-permute-start.31) | collective-permute-done | bytes 737312 | tf_op jit(solution)/shard_map/ppermute | solution.py:32
  111.3 2.6 %collective-permute-done.27.refs_2_ = bf16[288,1280]{1,0:T(8,128)(2,1)S(1)} collective-permute-done((bf16[288,1280]{1,0:T(8,128)(2,1)S(1)}, bf16[288,1280]{1,0:T(8,128)(2,1)S(1)}, u32[]{:S(2)}, u32[]{:S(2)}) %collective-permute-start.27) | collective-permute-done | bytes 737312 | tf_op jit(solution)/shard_map/ppermute | solution.py:32
  114.7 22.2 %collective-permute-done.25.refs_0_ = bf16[192,1280]{1,0:T(8,128)(2,1)S(1)} collective-permute-done((bf16[192,1280]{1,0:T(8,128)(2,1)S(1)}, bf16[192,1280]{1,0:T(8,128)(2,1)S(1)}, u32[]{:S(2)}, u32[]{:S(2)}) %collective-permute-start.25) | collective-permute-done | bytes 491552 | tf_op jit(solution)/shard_map/ppermute | solution.py:32
  136.9 2.7 %collective-permute-start.29 = (bf16[288,1280]{1,0:T(8,128)(2,1)S(1)}, bf16[288,1280]{1,0:T(8,128)(2,1)S(1)}, u32[]{:S(2)}, u32[]{:S(2)}) collective-permute-start(bf16[288,1280]{1,0:T(8,128)(2,1)S(1)} %collective-permute-done.27.refs_2_), channel_id=1, source_target_pairs={{0,6},{1,25},{2,0},{3,27},{4,2},{5,29},{6,4},{7,31},{8,14},{9,1},{... | collective-permute-start | bytes 2211848 | tf_op jit(solution)/shard_map/ppermute | solution.py:32
  141.6 7.1 %collective-permute-done.28.refs_0_ = bf16[288,1280]{1,0:T(8,128)(2,1)S(1)} collective-permute-done((bf16[288,1280]{1,0:T(8,128)(2,1)S(1)}, bf16[288,1280]{1,0:T(8,128)(2,1)S(1)}, u32[]{:S(2)}, u32[]{:S(2)}) %collective-permute-start.28) | collective-permute-done | bytes 737312 | tf_op jit(solution)/shard_map/ppermute | solution.py:32
  148.7 2.7 %collective-permute-start.34 = (bf16[288,1280]{1,0:T(8,128)(2,1)S(1)}, bf16[288,1280]{1,0:T(8,128)(2,1)S(1)}, u32[]{:S(2)}, u32[]{:S(2)}) collective-permute-start(bf16[288,1280]{1,0:T(8,128)(2,1)S(1)} %collective-permute-done.29.refs_1_), channel_id=1, source_target_pairs={{0,6},{1,25},{2,0},{3,27},{4,2},{5,29},{6,4},{7,31},{8,14},{9,1},{... | collective-permute-start | bytes 2211848 | tf_op jit(solution)/shard_map/ppermute | solution.py:32
  153.4 2.3 %convolution_add_fusion.2 = f32[624,1280]{1,0:T(8,128)S(1)} fusion(f32[624,1280]{1,0:T(8,128)S(1)} %fusion, bf16[1152,624]{1,0:T(8,128)(2,1)S(1)} %get-tuple-element.42, bf16[1152,1280]{1,0:T(8,128)(2,1)S(1)} %join.11), kind=kOutput, calls=%fused_computation.2 | convolution fusion | flops 1841049600 | bytes 10776576 | tf_op jit(solution)/shard_map/dot_general | solution.py:280
  155.7 3.2 %fusion.3 = f32[624,1280]{1,0:T(8,128)S(1)} fusion(bf16[1728,624]{1,0:T(8,128)(2,1)S(1)} %get-tuple-element.56, bf16[1728,1280]{1,0:T(8,128)(2,1)S(1)} %join.17), kind=kOutput, calls=%fused_computation.6 | convolution fusion | flops 2760376320 | bytes 9775104 | tf_op jit(solution)/shard_map/dot_general | solution.py:280
  165.7 5.4 %collective-permute-done.34 = bf16[288,1280]{1,0:T(8,128)(2,1)S(1)} collective-permute-done((bf16[288,1280]{1,0:T(8,128)(2,1)S(1)}, bf16[288,1280]{1,0:T(8,128)(2,1)S(1)}, u32[]{:S(2)}, u32[]{:S(2)}) %collective-permute-start.34) | collective-permute-done | bytes 737312 | tf_op jit(solution)/shard_map/ppermute | solution.py:32
  173.8 6.1 %collective-permute-start.36 = (f32[312,1280]{1,0:T(8,128)S(1)}, f32[312,1280]{1,0:T(8,128)S(1)}, u32[]{:S(2)}, u32[]{:S(2)}) collective-permute-start(f32[312,1280]{1,0:T(8,128)S(1)} %get-tuple-element.61), channel_id=1, source_target_pairs={{0,1},{1,0},{2,3},{3,2},{4,5},{5,4},{6,7},{7,6},{8,9},{9,8},{10,11... | collective-permute-start | bytes 4792328 | tf_op jit(solution)/shard_map/ppermute | solution.py:22
  181.2 1.8 collective-permute-done.36.half_ref
  (85 shorter events, 38.7 us)
Async XLA Ops:
  3.0 8.5 %collective-permute-start = (bf16[4,48,624]{2,1,0:T(8,128)(2,1)S(1)}, bf16[4,48,624]{2,1,0:T(8,128)(2,1)S(1)}, u32[]{:S(2)}, u32[]{:S(2)}) collective-permute-start(bf16[4,48,624]{2,1,0:T(8,128)(2,1)S(1)} %get-tuple-element.35), channel_id=1, source_target_pairs={{0,8},{1,3},{2,10},{3,5},{4,12},{5,7},{6,14},{7,1},{8,16},{9,11},{... | collective-permute-start | bytes 718856 | tf_op jit(solution)/shard_map/ppermute | solution.py:32
  5.6 8.0 %collective-permute-start.1 = (bf16[4,48,624]{2,1,0:T(8,128)(2,1)S(1)}, bf16[4,48,624]{2,1,0:T(8,128)(2,1)S(1)}, u32[]{:S(2)}, u32[]{:S(2)}) collective-permute-start(bf16[4,48,624]{2,1,0:T(8,128)(2,1)S(1)} %get-tuple-element.36), channel_id=1, source_target_pairs={{0,24},{1,7},{2,26},{3,1},{4,28},{5,3},{6,30},{7,5},{8,0},{9,15},{... | collective-permute-start | bytes 718856 | tf_op jit(solution)/shard_map/ppermute | solution.py:32
  25.5 22.0 %collective-permute-start.14 = (bf16[16,48,624]{2,1,0:T(8,128)(2,1)S(1)}, bf16[16,48,624]{2,1,0:T(8,128)(2,1)S(1)}, u32[]{:S(2)}, u32[]{:S(2)}) collective-permute-start(bf16[16,48,624]{2,1,0:T(8,128)(2,1)S(1)} %join.9.refs_0_), channel_id=1, source_target_pairs={{0,32},{32,64},{64,96},{96,0},{1,33},{33,65},{65,97},{97,1},{2,34}... | collective-permute-start | bytes 2875400 | tf_op jit(solution)/shard_map/ppermute | solution.py:18
  26.9 20.8 %collective-permute-start.13 = (bf16[16,48,624]{2,1,0:T(8,128)(2,1)S(1)}, bf16[16,48,624]{2,1,0:T(8,128)(2,1)S(1)}, u32[]{:S(2)}, u32[]{:S(2)}) collective-permute-start(bf16[16,48,624]{2,1,0:T(8,128)(2,1)S(1)} %join.9.refs_0_), channel_id=1, source_target_pairs={{0,96},{32,0},{64,32},{96,64},{1,97},{33,1},{65,33},{97,65},{2,98}... | collective-permute-start | bytes 2875400 | tf_op jit(solution)/shard_map/ppermute | solution.py:18
  33.0 19.4 %collective-permute-start.18 = (bf16[96,1280]{1,0:T(8,128)(2,1)S(1)}, bf16[96,1280]{1,0:T(8,128)(2,1)S(1)}, u32[]{:S(2)}, u32[]{:S(2)}) collective-permute-start(bf16[96,1280]{1,0:T(8,128)(2,1)S(1)} %get-tuple-element.50), channel_id=1, source_target_pairs={{0,96},{32,0},{64,32},{96,64},{1,97},{33,1},{65,33},{97,65},{2,98}... | collective-permute-start | bytes 737288 | tf_op jit(solution)/shard_map/ppermute | solution.py:18
  34.6 29.2 %collective-permute-start.19 = (bf16[96,1280]{1,0:T(8,128)(2,1)S(1)}, bf16[96,1280]{1,0:T(8,128)(2,1)S(1)}, u32[]{:S(2)}, u32[]{:S(2)}) collective-permute-start(bf16[96,1280]{1,0:T(8,128)(2,1)S(1)} %get-tuple-element.51), channel_id=1, source_target_pairs={{0,64},{32,96},{64,0},{96,32},{1,65},{33,97},{65,1},{97,33},{2,66}... | collective-permute-start | bytes 737288 | tf_op jit(solution)/shard_map/ppermute | solution.py:18
  35.0 28.9 %collective-permute-start.20 = (bf16[96,1280]{1,0:T(8,128)(2,1)S(1)}, bf16[96,1280]{1,0:T(8,128)(2,1)S(1)}, u32[]{:S(2)}, u32[]{:S(2)}) collective-permute-start(bf16[96,1280]{1,0:T(8,128)(2,1)S(1)} %get-tuple-element.52), channel_id=1, source_target_pairs={{0,32},{32,64},{64,96},{96,0},{1,33},{33,65},{65,97},{97,1},{2,34}... | collective-permute-start | bytes 737288 | tf_op jit(solution)/shard_map/ppermute | solution.py:18
  47.6 21.0 %collective-permute-start.15 = (bf16[8,48,624]{2,1,0:T(8,128)(2,1)S(1)}, bf16[8,48,624]{2,1,0:T(8,128)(2,1)S(1)}, u32[]{:S(2)}, u32[]{:S(2)}) collective-permute-start(bf16[8,48,624]{2,1,0:T(8,128)(2,1)S(1)} %slice.24), channel_id=1, source_target_pairs={{0,32},{32,64},{64,96},{96,0},{1,33},{33,65},{65,97},{97,1},{2,34}... | collective-permute-start | bytes 1437704 | tf_op jit(solution)/shard_map/ppermute | solution.py:18
  47.7 23.0 %collective-permute-start.16 = (bf16[8,48,624]{2,1,0:T(8,128)(2,1)S(1)}, bf16[8,48,624]{2,1,0:T(8,128)(2,1)S(1)}, u32[]{:S(2)}, u32[]{:S(2)}) collective-permute-start(bf16[8,48,624]{2,1,0:T(8,128)(2,1)S(1)} %slice.25), channel_id=1, source_target_pairs={{0,96},{32,0},{64,32},{96,64},{1,97},{33,1},{65,33},{97,65},{2,98}... | collective-permute-start | bytes 1437704 | tf_op jit(solution)/shard_map/ppermute | solution.py:18
  52.5 29.6 %collective-permute-start.6 = (bf16[16,48,624]{2,1,0:T(8,128)(2,1)S(1)}, bf16[16,48,624]{2,1,0:T(8,128)(2,1)S(1)}, u32[]{:S(2)}, u32[]{:S(2)}) collective-permute-start(bf16[16,48,624]{2,1,0:T(8,128)(2,1)S(1)} %join.9.refs_0_), channel_id=1, source_target_pairs={{0,1},{1,0},{2,3},{3,2},{4,5},{5,4},{6,7},{7,6},{8,9},{9,8},{10,11... | collective-permute-start | bytes 2875400 | tf_op jit(solution)/shard_map/ppermute | solution.py:22
  63.9 18.3 %collective-permute-start.21 = (bf16[288,1280]{1,0:T(8,128)(2,1)S(1)}, bf16[288,1280]{1,0:T(8,128)(2,1)S(1)}, u32[]{:S(2)}, u32[]{:S(2)}) collective-permute-start(bf16[288,1280]{1,0:T(8,128)(2,1)S(1)} %join.13.refs_0_), channel_id=1, source_target_pairs={{0,8},{1,3},{2,10},{3,5},{4,12},{5,7},{6,14},{7,1},{8,16},{9,11},{... | collective-permute-start | bytes 2211848 | tf_op jit(solution)/shard_map/ppermute | solution.py:32
  65.1 13.3 %collective-permute-start.8 = (bf16[96,1280]{1,0:T(8,128)(2,1)S(1)}, bf16[96,1280]{1,0:T(8,128)(2,1)S(1)}, u32[]{:S(2)}, u32[]{:S(2)}) collective-permute-start(bf16[96,1280]{1,0:T(8,128)(2,1)S(1)} %get-tuple-element.48.refs_0_), channel_id=1, source_target_pairs={{0,8},{1,3},{2,10},{3,5},{4,12},{5,7},{6,14},{7,1},{8,16},{9,11},{... | collective-permute-start | bytes 737288 | tf_op jit(solution)/shard_map/ppermute | solution.py:32
  68.6 11.4 %collective-permute-start.9 = (bf16[96,1280]{1,0:T(8,128)(2,1)S(1)}, bf16[96,1280]{1,0:T(8,128)(2,1)S(1)}, u32[]{:S(2)}, u32[]{:S(2)}) collective-permute-start(bf16[96,1280]{1,0:T(8,128)(2,1)S(1)} %get-tuple-element.48.refs_0_), channel_id=1, source_target_pairs={{0,24},{1,7},{2,26},{3,1},{4,28},{5,3},{6,30},{7,5},{8,0},{9,15},{... | collective-permute-start | bytes 737288 | tf_op jit(solution)/shard_map/ppermute | solution.py:32
  70.8 10.9 %collective-permute-start.10 = (bf16[96,1280]{1,0:T(8,128)(2,1)S(1)}, bf16[96,1280]{1,0:T(8,128)(2,1)S(1)}, u32[]{:S(2)}, u32[]{:S(2)}) collective-permute-start(bf16[96,1280]{1,0:T(8,128)(2,1)S(1)} %get-tuple-element.48.refs_0_), channel_id=1, source_target_pairs={{0,16},{1,5},{2,18},{3,7},{4,20},{5,1},{6,22},{7,3},{8,24},{9,13},... | collective-permute-start | bytes 737288 | tf_op jit(solution)/shard_map/ppermute | solution.py:32
  78.4 73.0 %collective-permute-start.17 = (bf16[48,48,624]{2,1,0:T(8,128)(2,1)S(1)}, bf16[48,48,624]{2,1,0:T(8,128)(2,1)S(1)}, u32[]{:S(2)}, u32[]{:S(2)}) collective-permute-start(bf16[48,48,624]{2,1,0:T(8,128)(2,1)S(1)} %join.12.refs_0_), channel_id=1, source_target_pairs={{0,1},{1,0},{2,3},{3,2},{4,5},{5,4},{6,7},{7,6},{8,9},{9,8},{10,11... | collective-permute-start | bytes 8626184 | tf_op jit(solution)/shard_map/ppermute | solution.py:22
  80.0 12.3 %collective-permute-start.22 = (bf16[288,1280]{1,0:T(8,128)(2,1)S(1)}, bf16[288,1280]{1,0:T(8,128)(2,1)S(1)}, u32[]{:S(2)}, u32[]{:S(2)}) collective-permute-start(bf16[288,1280]{1,0:T(8,128)(2,1)S(1)} %join.13.refs_0_), channel_id=1, source_target_pairs={{0,24},{1,7},{2,26},{3,1},{4,28},{5,3},{6,30},{7,5},{8,0},{9,15},{... | collective-permute-start | bytes 2211848 | tf_op jit(solution)/shard_map/ppermute | solution.py:32
  81.6 12.5 %collective-permute-start.30 = (bf16[288,1280]{1,0:T(8,128)(2,1)S(1)}, bf16[288,1280]{1,0:T(8,128)(2,1)S(1)}, u32[]{:S(2)}, u32[]{:S(2)}) collective-permute-start(bf16[288,1280]{1,0:T(8,128)(2,1)S(1)} %join.13.refs_0_), channel_id=1, source_target_pairs={{0,2},{1,9},{2,4},{3,11},{4,6},{5,13},{6,0},{7,15},{8,10},{9,17},{... | collective-permute-start | bytes 2211848 | tf_op jit(solution)/shard_map/ppermute | solution.py:32
  82.1 21.9 %collective-permute-start.11 = (bf16[384,1280]{1,0:T(8,128)(2,1)S(1)}, bf16[384,1280]{1,0:T(8,128)(2,1)S(1)}, u32[]{:S(2)}, u32[]{:S(2)}) collective-permute-start(bf16[384,1280]{1,0:T(8,128)(2,1)S(1)} %join.10.refs_0_), channel_id=1, source_target_pairs={{0,2},{1,9},{2,4},{3,11},{4,6},{5,13},{6,0},{7,15},{8,10},{9,17},{... | collective-permute-start | bytes 2949128 | tf_op jit(solution)/shard_map/ppermute | solution.py:32
  82.2 21.8 %collective-permute-start.12 = (bf16[384,1280]{1,0:T(8,128)(2,1)S(1)}, bf16[384,1280]{1,0:T(8,128)(2,1)S(1)}, u32[]{:S(2)}, u32[]{:S(2)}) collective-permute-start(bf16[384,1280]{1,0:T(8,128)(2,1)S(1)} %join.10.refs_0_), channel_id=1, source_target_pairs={{0,6},{1,25},{2,0},{3,27},{4,2},{5,29},{6,4},{7,31},{8,14},{9,1},{... | collective-permute-start | bytes 2949128 | tf_op jit(solution)/shard_map/ppermute | solution.py:32
  92.3 18.9 %collective-permute-start.31 = (bf16[288,1280]{1,0:T(8,128)(2,1)S(1)}, bf16[288,1280]{1,0:T(8,128)(2,1)S(1)}, u32[]{:S(2)}, u32[]{:S(2)}) collective-permute-start(bf16[288,1280]{1,0:T(8,128)(2,1)S(1)} %join.13.refs_0_), channel_id=1, source_target_pairs={{0,6},{1,25},{2,0},{3,27},{4,2},{5,29},{6,4},{7,31},{8,14},{9,1},{... | collective-permute-start | bytes 2211848 | tf_op jit(solution)/shard_map/ppermute | solution.py:32
  94.1 19.7 %collective-permute-start.27 = (bf16[288,1280]{1,0:T(8,128)(2,1)S(1)}, bf16[288,1280]{1,0:T(8,128)(2,1)S(1)}, u32[]{:S(2)}, u32[]{:S(2)}) collective-permute-start(bf16[288,1280]{1,0:T(8,128)(2,1)S(1)} %collective-permute-done.21.refs_0_), channel_id=1, source_target_pairs={{0,8},{1,3},{2,10},{3,5},{4,12},{5,7},{6,14},{7,1},{8,16},{9,11},{... | collective-permute-start | bytes 2211848 | tf_op jit(solution)/shard_map/ppermute | solution.py:32
  104.0 37.3 %collective-permute-start.23 = (bf16[576,1280]{1,0:T(8,128)(2,1)S(1)}, bf16[576,1280]{1,0:T(8,128)(2,1)S(1)}, u32[]{:S(2)}, u32[]{:S(2)}) collective-permute-start(bf16[576,1280]{1,0:T(8,128)(2,1)S(1)} %join.14.refs_1_), channel_id=1, source_target_pairs={{0,2},{1,9},{2,4},{3,11},{4,6},{5,13},{6,0},{7,15},{8,10},{9,17},{... | collective-permute-start | bytes 4423688 | tf_op jit(solution)/shard_map/ppermute | solution.py:32
  104.0 37.4 %collective-permute-start.24 = (bf16[576,1280]{1,0:T(8,128)(2,1)S(1)}, bf16[576,1280]{1,0:T(8,128)(2,1)S(1)}, u32[]{:S(2)}, u32[]{:S(2)}) collective-permute-start(bf16[576,1280]{1,0:T(8,128)(2,1)S(1)} %join.14.refs_1_), channel_id=1, source_target_pairs={{0,6},{1,25},{2,0},{3,27},{4,2},{5,29},{6,4},{7,31},{8,14},{9,1},{... | collective-permute-start | bytes 4423688 | tf_op jit(solution)/shard_map/ppermute | solution.py:32
  111.3 25.6 %collective-permute-start.25 = (bf16[192,1280]{1,0:T(8,128)(2,1)S(1)}, bf16[192,1280]{1,0:T(8,128)(2,1)S(1)}, u32[]{:S(2)}, u32[]{:S(2)}) collective-permute-start(bf16[192,1280]{1,0:T(8,128)(2,1)S(1)} %slice.26), channel_id=1, source_target_pairs={{0,2},{1,9},{2,4},{3,11},{4,6},{5,13},{6,0},{7,15},{8,10},{9,17},{... | collective-permute-start | bytes 1474568 | tf_op jit(solution)/shard_map/ppermute | solution.py:32
  113.9 23.0 %collective-permute-start.26 = (bf16[192,1280]{1,0:T(8,128)(2,1)S(1)}, bf16[192,1280]{1,0:T(8,128)(2,1)S(1)}, u32[]{:S(2)}, u32[]{:S(2)}) collective-permute-start(bf16[192,1280]{1,0:T(8,128)(2,1)S(1)} %slice.27), channel_id=1, source_target_pairs={{0,6},{1,25},{2,0},{3,27},{4,2},{5,29},{6,4},{7,31},{8,14},{9,1},{... | collective-permute-start | bytes 1474568 | tf_op jit(solution)/shard_map/ppermute | solution.py:32
  136.9 11.8 %collective-permute-start.28 = (bf16[288,1280]{1,0:T(8,128)(2,1)S(1)}, bf16[288,1280]{1,0:T(8,128)(2,1)S(1)}, u32[]{:S(2)}, u32[]{:S(2)}) collective-permute-start(bf16[288,1280]{1,0:T(8,128)(2,1)S(1)} %collective-permute-done.27.refs_2_), channel_id=1, source_target_pairs={{0,2},{1,9},{2,4},{3,11},{4,6},{5,13},{6,0},{7,15},{8,10},{9,17},{... | collective-permute-start | bytes 2211848 | tf_op jit(solution)/shard_map/ppermute | solution.py:32
  136.9 11.8 %collective-permute-start.29 = (bf16[288,1280]{1,0:T(8,128)(2,1)S(1)}, bf16[288,1280]{1,0:T(8,128)(2,1)S(1)}, u32[]{:S(2)}, u32[]{:S(2)}) collective-permute-start(bf16[288,1280]{1,0:T(8,128)(2,1)S(1)} %collective-permute-done.27.refs_2_), channel_id=1, source_target_pairs={{0,6},{1,25},{2,0},{3,27},{4,2},{5,29},{6,4},{7,31},{8,14},{9,1},{... | collective-permute-start | bytes 2211848 | tf_op jit(solution)/shard_map/ppermute | solution.py:32
  141.3 30.9 %collective-permute-start.35 = (bf16[288,1280]{1,0:T(8,128)(2,1)S(1)}, bf16[288,1280]{1,0:T(8,128)(2,1)S(1)}, u32[]{:S(2)}, u32[]{:S(2)}) collective-permute-start(bf16[288,1280]{1,0:T(8,128)(2,1)S(1)} %collective-permute-done.30.refs_3_), channel_id=1, source_target_pairs={{0,2},{1,9},{2,4},{3,11},{4,6},{5,13},{6,0},{7,15},{8,10},{9,17},{... | collective-permute-start | bytes 2211848 | tf_op jit(solution)/shard_map/ppermute | solution.py:32
  141.4 21.5 %collective-permute-start.32 = (bf16[144,1280]{1,0:T(8,128)(2,1)S(1)}, bf16[144,1280]{1,0:T(8,128)(2,1)S(1)}, u32[]{:S(2)}, u32[]{:S(2)}) collective-permute-start(bf16[144,1280]{1,0:T(8,128)(2,1)S(1)} %slice.28), channel_id=1, source_target_pairs={{0,2},{1,9},{2,4},{3,11},{4,6},{5,13},{6,0},{7,15},{8,10},{9,17},{... | collective-permute-start | bytes 1105928 | tf_op jit(solution)/shard_map/ppermute | solution.py:32
  148.7 15.3 %collective-permute-start.33 = (bf16[432,1280]{1,0:T(8,128)(2,1)S(1)}, bf16[432,1280]{1,0:T(8,128)(2,1)S(1)}, u32[]{:S(2)}, u32[]{:S(2)}) collective-permute-start(bf16[432,1280]{1,0:T(8,128)(2,1)S(1)} %slice.29), channel_id=1, source_target_pairs={{0,6},{1,25},{2,0},{3,27},{4,2},{5,29},{6,4},{7,31},{8,14},{9,1},{... | collective-permute-start | bytes 3317768 | tf_op jit(solution)/shard_map/ppermute | solution.py:32
  148.7 22.5 %collective-permute-start.34 = (bf16[288,1280]{1,0:T(8,128)(2,1)S(1)}, bf16[288,1280]{1,0:T(8,128)(2,1)S(1)}, u32[]{:S(2)}, u32[]{:S(2)}) collective-permute-start(bf16[288,1280]{1,0:T(8,128)(2,1)S(1)} %collective-permute-done.29.refs_1_), channel_id=1, source_target_pairs={{0,6},{1,25},{2,0},{3,27},{4,2},{5,29},{6,4},{7,31},{8,14},{9,1},{... | collective-permute-start | bytes 2211848 | tf_op jit(solution)/shard_map/ppermute | solution.py:32
  173.8 9.2 %collective-permute-start.36 = (f32[312,1280]{1,0:T(8,128)S(1)}, f32[312,1280]{1,0:T(8,128)S(1)}, u32[]{:S(2)}, u32[]{:S(2)}) collective-permute-start(f32[312,1280]{1,0:T(8,128)S(1)} %get-tuple-element.61), channel_id=1, source_target_pairs={{0,1},{1,0},{2,3},{3,2},{4,5},{5,4},{6,7},{7,6},{8,9},{9,8},{10,11... | collective-permute-start | bytes 4792328 | tf_op jit(solution)/shard_map/ppermute | solution.py:22
  (7 other events, 35.3 us)
